TPU v7x, 32 devices: a whole 2x2x4 slice. The times are simulated.
32 devices in a mesh: dp: 16 (over z, x, core), tensor: 2 (over y).
Axes of the slice: x: 2, y: 2, z: 4, core: 2. Of those that a mesh axis runs over, the one named last changes fastest.
Arguments:
- latents: bfloat16 [16384, 1536], P('dp'), may hold values from -6 to 6
- cotangent: bfloat16 [16384, 1536], P('dp'), may hold values from -8 to 8
- caption: bfloat16 [16, 256, 4096], P('dp'), may hold values from -6 to 6
- caption_lens: int32 [16], P('dp'), may hold values from 8 to 256, as said below
- patch_row: int32 [16, 1024], P('dp'), may hold values from 0 to 63, as said below
- patch_col: int32 [16, 1024], P('dp'), may hold values from 0 to 63, as said below
- timestep: int32 [16], P('dp'), may hold values from 0 to 999
- query_proj: bfloat16 [1536, 1536], P('dp', 'tensor'), may hold values from -0.15625 to 0.15625
- key_proj: bfloat16 [1536, 1536], P('dp', 'tensor'), may hold values from -0.15625 to 0.15625
- value_proj: bfloat16 [1536, 1536], P('dp', 'tensor'), may hold values from -0.15625 to 0.15625
- output_proj: bfloat16 [1536, 1536], P('tensor', 'dp'), may hold values from -0.625 to 0.625
- textkey_proj: bfloat16 [4096, 1536], P('dp', 'tensor'), may hold values from -0.09375 to 0.09375
- textval_proj: bfloat16 [4096, 1536], P('dp', 'tensor'), may hold values from -0.09375 to 0.09375
- gate_proj: bfloat16 [1536, 4096], P('dp', 'tensor'), may hold values from -0.15625 to 0.15625
- up_proj: bfloat16 [1536, 4096], P('dp', 'tensor'), may hold values from -0.15625 to 0.15625
- down_proj: bfloat16 [4096, 1536], P('tensor', 'dp'), may hold values from -0.09375 to 0.09375
- modulation: bfloat16 [1024, 6144], P('dp', 'tensor'), may hold values from -0.375 to 0.375
- attn_gain: bfloat16 [1536], P('dp'), may hold values from 0.5 to 1.5
- ffn_gain: bfloat16 [1536], P('dp'), may hold values from 0.5 to 1.5
- query_gain: bfloat16 [64], P('dp'), may hold values from 0.59765625 to 1.59375
- key_gain: bfloat16 [64], P('dp'), may hold values from 0.59765625 to 1.59375
- textkey_gain: bfloat16 [64], P('dp'), may hold values from 0.59765625 to 1.59375
- cross_gate: bfloat16 [24], P('tensor'), may hold values from -2.5 to 2.5
Outputs:
- output: bfloat16 [16384, 1536], P('dp')
- grad_latents: bfloat16 [16384, 1536], P('dp')
- grad_caption: bfloat16 [16, 256, 4096], P('dp', None, 'tensor')
- grad_embed: float32 [16, 1024], P('dp', 'tensor')
- grad_query: float32 [1536, 1536], P('dp', 'tensor')
- grad_key: float32 [1536, 1536], P('dp', 'tensor')
- grad_value: float32 [1536, 1536], P('dp', 'tensor')
- grad_output: float32 [1536, 1536], P('tensor', 'dp')
- grad_textkey: float32 [4096, 1536], P('dp', 'tensor')
- grad_textval: float32 [4096, 1536], P('dp', 'tensor')
- grad_gate: float32 [1536, 4096], P('dp', 'tensor')
- grad_up: float32 [1536, 4096], P('dp', 'tensor')
- grad_down: float32 [4096, 1536], P('tensor', 'dp')
- grad_modul: float32 [1024, 6144], P('dp', 'tensor')
- grad_attngain: float32 [1536], P('dp')
- grad_ffngain: float32 [1536], P('dp')
- grad_qgain: float32 [64], P('dp')
- grad_kgain: float32 [64], P('dp')
- grad_tkgain: float32 [64], P('dp')
- grad_xgate: float32 [24], P('tensor')
Inputs may be any that keep to these rules, and one draw needn't show every extreme that they name: `caption_lens`: at least one image uses all 256 caption slots. `patch_row`: each image's 1024 patches form a grid of H rows and 1024 / H columns in row-major order, H one of 16, 32, 64; patch_col gives the column in the same grid. `patch_col`: the column in the grid that patch_row describes.
All inputs are finite; a program needn't handle non-finite values.
Results may differ from a plain program's by a relative error of at most 0.04.
Values may be sent and summed in bfloat16 or wider, within the bound.
No kernel may reach another device: no remote copies, remote signals or barrier semaphores. Data moves between devices by JAX's collectives and lax.ppermute only.
A program may use at most 448 MiB of HBM per device.

v0:
```python
import math

import jax
import jax.numpy as jnp
from jax import lax
from jax.sharding import PartitionSpec as P

EPSILON = 1e-06


def inv_rms(values):
    return lax.rsqrt(jnp.mean(values * values, axis=-1, keepdims=True) + EPSILON)


def rounded(values):
    return lax.optimization_barrier(values.astype(jnp.bfloat16)).astype(jnp.float32)


def rotary(values, row_pos, col_pos, direction):
    quarter = values.shape[-1] // 4
    frequency = jnp.exp(-math.log(10000.0) * jnp.arange(quarter, dtype=jnp.float32) / quarter)
    angles = jnp.concatenate(
        [
            row_pos.astype(jnp.float32)[:, None] * frequency,
            col_pos.astype(jnp.float32)[:, None] * frequency,
        ],
        axis=1,
    )[:, None, :]
    cosine = jnp.cos(angles)
    sine_part = direction * jnp.sin(angles)
    first_half = values[..., : 2 * quarter]
    second = values[..., 2 * quarter :]
    return jnp.concatenate(
        [first_half * cosine - second * sine_part, first_half * sine_part + second * cosine],
        axis=-1,
    )


def time_embed(step_vals, embed_width):
    half_width = embed_width // 2
    frequency = jnp.exp(-math.log(10000.0) * jnp.arange(half_width, dtype=jnp.float32) / half_width)
    phases = step_vals.astype(jnp.float32)[:, None] * frequency
    return jnp.concatenate([jnp.cos(phases), jnp.sin(phases)], axis=1)


def soft_keep(scores):
    row_max = jnp.max(scores, axis=-1, keepdims=True)
    exp_scores = jnp.exp(scores - row_max)
    row_total = jnp.sum(exp_scores, axis=-1, keepdims=True)
    return (exp_scores / row_total, row_max + jnp.log(row_total))


def norm_back(grad_hat, normed, factor):
    return factor * (grad_hat - normed * jnp.mean(grad_hat * normed, axis=-1, keepdims=True))


def attend(block_in):
    query_blk, key_blk, value_blk, tkey_blk, tval_blk, mask_blk = block_in
    scaling = query_blk.shape[-1] ** (-0.5)
    scores = (
        jnp.einsum("qhd,khd->hqk", query_blk, key_blk, preferred_element_type=jnp.float32) * scaling
    )
    probs_self, lse_self = soft_keep(scores)
    own_out = jnp.einsum(
        "hqk,khd->qhd",
        probs_self.astype(jnp.bfloat16),
        value_blk,
        preferred_element_type=jnp.float32,
    )
    cross_scores = (
        jnp.einsum("qhd,khd->hqk", query_blk, tkey_blk, preferred_element_type=jnp.float32)
        * scaling
    )
    cross_scores = jnp.where(mask_blk[None, None, :], cross_scores, -1e30)
    probs_text, lse_text = soft_keep(cross_scores)
    cross_out = jnp.einsum(
        "hqk,khd->qhd",
        probs_text.astype(jnp.bfloat16),
        tval_blk,
        preferred_element_type=jnp.float32,
    )
    return (own_out, cross_out, lse_self, lse_text)


def attend_back(block_in):
    (
        query_blk,
        key_blk,
        value_blk,
        tkey_blk,
        tval_blk,
        mask_blk,
        lse_self,
        lse_text,
        grad_own,
        grad_cross,
    ) = block_in
    scaling = query_blk.shape[-1] ** (-0.5)
    probs_self = jnp.exp(
        jnp.einsum("qhd,khd->hqk", query_blk, key_blk, preferred_element_type=jnp.float32) * scaling
        - lse_self
    )
    dprobs = jnp.einsum("qhd,khd->hqk", grad_own, value_blk, preferred_element_type=jnp.float32)
    dscore = (probs_self * (dprobs - jnp.sum(probs_self * dprobs, axis=-1, keepdims=True))).astype(
        jnp.bfloat16
    )
    dquery = (
        jnp.einsum("hqk,khd->qhd", dscore, key_blk, preferred_element_type=jnp.float32) * scaling
    )
    grad_key = (
        jnp.einsum("hqk,qhd->khd", dscore, query_blk, preferred_element_type=jnp.float32) * scaling
    )
    grad_value = jnp.einsum(
        "hqk,qhd->khd",
        probs_self.astype(jnp.bfloat16),
        grad_own,
        preferred_element_type=jnp.float32,
    )
    cross_scores = (
        jnp.einsum("qhd,khd->hqk", query_blk, tkey_blk, preferred_element_type=jnp.float32)
        * scaling
    )
    probs_text = jnp.exp(jnp.where(mask_blk[None, None, :], cross_scores, -1e30) - lse_text)
    dprobs_text = jnp.einsum(
        "qhd,khd->hqk", grad_cross, tval_blk, preferred_element_type=jnp.float32
    )
    dscore_text = (
        probs_text * (dprobs_text - jnp.sum(probs_text * dprobs_text, axis=-1, keepdims=True))
    ).astype(jnp.bfloat16)
    dquery = (
        dquery
        + jnp.einsum("hqk,khd->qhd", dscore_text, tkey_blk, preferred_element_type=jnp.float32)
        * scaling
    )
    grad_tkey = (
        jnp.einsum("hqk,qhd->khd", dscore_text, query_blk, preferred_element_type=jnp.float32)
        * scaling
    )
    grad_tval = jnp.einsum(
        "hqk,qhd->khd",
        probs_text.astype(jnp.bfloat16),
        grad_cross,
        preferred_element_type=jnp.float32,
    )
    return (dquery, grad_key, grad_value, grad_tkey, grad_tval)


def local(
    latents,
    cotangent,
    caption,
    caption_lens,
    patch_row,
    patch_col,
    timestep,
    query_proj,
    key_proj,
    value_proj,
    output_proj,
    textkey_proj,
    textval_proj,
    gate_proj,
    up_proj,
    down_proj,
    modulation,
    attn_gain,
    ffn_gain,
    query_gain,
    key_gain,
    textkey_gain,
    cross_gate,
):
    gathered = (
        lax.all_gather(query_proj, "dp", axis=0, tiled=True),
        lax.all_gather(key_proj, "dp", axis=0, tiled=True),
        lax.all_gather(value_proj, "dp", axis=0, tiled=True),
        lax.all_gather(output_proj, "dp", axis=1, tiled=True),
        lax.all_gather(textkey_proj, "dp", axis=0, tiled=True),
        lax.all_gather(textval_proj, "dp", axis=0, tiled=True),
        lax.all_gather(gate_proj, "dp", axis=0, tiled=True),
        lax.all_gather(up_proj, "dp", axis=0, tiled=True),
        lax.all_gather(down_proj, "dp", axis=1, tiled=True),
        lax.all_gather(modulation, "dp", axis=0, tiled=True),
        lax.all_gather(attn_gain, "dp", axis=0, tiled=True),
        lax.all_gather(ffn_gain, "dp", axis=0, tiled=True),
        lax.all_gather(query_gain, "dp", axis=0, tiled=True),
        lax.all_gather(key_gain, "dp", axis=0, tiled=True),
        lax.all_gather(textkey_gain, "dp", axis=0, tiled=True),
    )
    (
        full_query,
        full_key,
        full_value,
        full_output,
        full_tkey,
        full_tval,
        full_gate,
        full_up,
        full_down,
        full_mod,
    ) = gathered[:10]
    gain_one = gathered[10].astype(jnp.float32)
    gain_two = gathered[11].astype(jnp.float32)
    gain_query = gathered[12].astype(jnp.float32)
    gain_key = gathered[13].astype(jnp.float32)
    gain_text = gathered[14].astype(jnp.float32)
    tanh_cross = jnp.tanh(cross_gate.astype(jnp.float32))[:, None]
    images, length = patch_row.shape
    model_dim = latents.shape[1]
    head_dim = gain_query.shape[0]
    heads_here = full_query.shape[1] // head_dim
    cap_len = caption.shape[1]
    rows_all = images * length
    embedding = time_embed(timestep, full_mod.shape[0])
    sig_embed = jax.nn.sigmoid(embedding)
    cond_bf = (embedding * sig_embed).astype(jnp.bfloat16)
    mod_here = jnp.dot(cond_bf, full_mod, preferred_element_type=jnp.float32)
    mod_all = lax.all_gather(mod_here, "tensor", axis=1, tiled=True)
    scale_one = mod_all[:, None, 0:model_dim]
    gate_one = jnp.tanh(mod_all[:, None, model_dim : 2 * model_dim])
    scale_two = mod_all[:, None, 2 * model_dim : 3 * model_dim]
    gate_two = jnp.tanh(mod_all[:, None, 3 * model_dim : 4 * model_dim])
    resid_in = latents.astype(jnp.float32).reshape(images, length, model_dim)
    factor_one = inv_rms(resid_in)
    normed_one = resid_in * factor_one
    attn_in = (
        (normed_one * gain_one * (1.0 + scale_one))
        .astype(jnp.bfloat16)
        .reshape(rows_all, model_dim)
    )
    heads_shape = (images, length, heads_here, head_dim)
    query_raw = jnp.dot(attn_in, full_query, preferred_element_type=jnp.float32).reshape(
        heads_shape
    )
    key_raw = jnp.dot(attn_in, full_key, preferred_element_type=jnp.float32).reshape(heads_shape)
    values_bf = (
        jnp.dot(attn_in, full_value, preferred_element_type=jnp.float32)
        .astype(jnp.bfloat16)
        .reshape(heads_shape)
    )
    query_fac = inv_rms(query_raw)
    query_hat = query_raw * query_fac
    key_fac = inv_rms(key_raw)
    key_hat = key_raw * key_fac
    rotate = jax.vmap(rotary, in_axes=(0, 0, 0, None))
    query_bf = rotate(query_hat * gain_query, patch_row, patch_col, 1.0).astype(jnp.bfloat16)
    key_bf = rotate(key_hat * gain_key, patch_row, patch_col, 1.0).astype(jnp.bfloat16)
    text_shape = (images, cap_len, heads_here, head_dim)
    text_raw = jnp.einsum(
        "bce,ef->bcf", caption, full_tkey, preferred_element_type=jnp.float32
    ).reshape(text_shape)
    text_fac = inv_rms(text_raw)
    text_hat = text_raw * text_fac
    tkeys_bf = (text_hat * gain_text).astype(jnp.bfloat16)
    tvals_bf = (
        jnp.einsum("bce,ef->bcf", caption, full_tval, preferred_element_type=jnp.float32)
        .astype(jnp.bfloat16)
        .reshape(text_shape)
    )
    keep_mask = jnp.arange(cap_len)[None, :] < caption_lens[:, None]
    own_out, cross_out, lse_self, lse_text = lax.map(
        attend, (query_bf, key_bf, values_bf, tkeys_bf, tvals_bf, keep_mask)
    )
    mixed_heads = (
        (own_out + tanh_cross * cross_out)
        .astype(jnp.bfloat16)
        .reshape(rows_all, heads_here * head_dim)
    )
    attn_out = (
        lax.psum(
            jnp.dot(mixed_heads, full_output, preferred_element_type=jnp.float32).astype(
                jnp.bfloat16
            ),
            "tensor",
        )
        .astype(jnp.float32)
        .reshape(images, length, model_dim)
    )
    residual = resid_in + gate_one * attn_out
    factor_two = inv_rms(residual)
    normed_two = residual * factor_two
    ffn_in = (
        (normed_two * gain_two * (1.0 + scale_two))
        .astype(jnp.bfloat16)
        .reshape(rows_all, model_dim)
    )
    gate_pre = jnp.dot(ffn_in, full_gate, preferred_element_type=jnp.float32)
    up_pre = jnp.dot(ffn_in, full_up, preferred_element_type=jnp.float32)
    sig_gate = jax.nn.sigmoid(gate_pre)
    act_gate = gate_pre * sig_gate
    hidden = (act_gate * up_pre).astype(jnp.bfloat16)
    ffn_out = (
        lax.psum(
            jnp.dot(hidden, full_down, preferred_element_type=jnp.float32).astype(jnp.bfloat16),
            "tensor",
        )
        .astype(jnp.float32)
        .reshape(images, length, model_dim)
    )
    output = (residual + gate_two * ffn_out).astype(jnp.bfloat16).reshape(rows_all, model_dim)
    back_weights = (
        lax.all_gather(query_proj, "dp", axis=0, tiled=True),
        lax.all_gather(key_proj, "dp", axis=0, tiled=True),
        lax.all_gather(value_proj, "dp", axis=0, tiled=True),
        lax.all_gather(output_proj, "dp", axis=1, tiled=True),
        lax.all_gather(textkey_proj, "dp", axis=0, tiled=True),
        lax.all_gather(textval_proj, "dp", axis=0, tiled=True),
        lax.all_gather(gate_proj, "dp", axis=0, tiled=True),
        lax.all_gather(up_proj, "dp", axis=0, tiled=True),
        lax.all_gather(down_proj, "dp", axis=1, tiled=True),
        lax.all_gather(modulation, "dp", axis=0, tiled=True),
    )
    (
        back_query,
        back_key,
        back_value,
        back_output,
        back_tkey,
        back_tval,
        back_gate,
        back_up,
        back_down,
        back_mod,
    ) = back_weights
    grad_out = cotangent.astype(jnp.float32).reshape(images, length, model_dim)
    dgate_two = jnp.sum(grad_out * ffn_out, axis=1) * (1.0 - gate_two[:, 0] ** 2)
    grad_ffn = (gate_two * grad_out).astype(jnp.bfloat16).reshape(rows_all, model_dim)
    grad_down = jnp.einsum("rf,rd->fd", hidden, grad_ffn, preferred_element_type=jnp.float32)
    dhidden = jnp.einsum("rd,fd->rf", grad_ffn, back_down, preferred_element_type=jnp.float32)
    dgate_pre = (dhidden * up_pre * sig_gate * (1.0 + gate_pre * (1.0 - sig_gate))).astype(
        jnp.bfloat16
    )
    dup_pre = (dhidden * act_gate).astype(jnp.bfloat16)
    grad_gate = jnp.einsum("rd,rf->df", ffn_in, dgate_pre, preferred_element_type=jnp.float32)
    grad_up = jnp.einsum("rd,rf->df", ffn_in, dup_pre, preferred_element_type=jnp.float32)
    ffn_part = jnp.einsum(
        "rf,df->rd", dgate_pre, back_gate, preferred_element_type=jnp.float32
    ) + jnp.einsum("rf,df->rd", dup_pre, back_up, preferred_element_type=jnp.float32)
    dffn_in = (
        lax.psum(ffn_part.astype(jnp.bfloat16), "tensor")
        .astype(jnp.float32)
        .reshape(images, length, model_dim)
    )
    grad_gaintwo = jnp.sum(dffn_in * normed_two * (1.0 + scale_two), axis=(0, 1))
    dscale_two = jnp.sum(dffn_in * normed_two * gain_two, axis=1)
    dresid = grad_out + norm_back(dffn_in * gain_two * (1.0 + scale_two), normed_two, factor_two)
    dgate_one = jnp.sum(dresid * attn_out, axis=1) * (1.0 - gate_one[:, 0] ** 2)
    grad_attn = (gate_one * dresid).astype(jnp.bfloat16).reshape(rows_all, model_dim)
    grad_output = jnp.einsum(
        "rc,rd->cd", mixed_heads, grad_attn, preferred_element_type=jnp.float32
    )
    dmixed = (
        jnp.einsum("rd,cd->rc", grad_attn, back_output, preferred_element_type=jnp.float32)
        .astype(jnp.bfloat16)
        .reshape(heads_shape)
    )
    dmixed_f = dmixed.astype(jnp.float32)
    xgate_here = jnp.sum(dmixed_f * cross_out, axis=(0, 1, 3)) * (1.0 - tanh_cross[:, 0] ** 2)
    heads_total = heads_here * lax.axis_size("tensor")
    head_start = lax.axis_index("tensor") * heads_here
    xgate_full = lax.dynamic_update_slice_in_dim(
        jnp.zeros((heads_total,), jnp.float32), xgate_here, head_start, 0
    )
    xgate_sum = lax.psum(xgate_full, ("dp", "tensor"))
    grad_xgate = lax.dynamic_slice_in_dim(xgate_sum, head_start, heads_here, 0)
    dother = (tanh_cross * dmixed_f).astype(jnp.bfloat16)
    dquery, grad_keys, dvalues, dtkeys, dtvals = lax.map(
        attend_back,
        (
            query_bf,
            key_bf,
            values_bf,
            tkeys_bf,
            tvals_bf,
            keep_mask,
            lse_self,
            lse_text,
            dmixed,
            dother,
        ),
    )
    query_turn = rotate(rounded(dquery), patch_row, patch_col, -1.0)
    key_turn = rotate(rounded(grad_keys), patch_row, patch_col, -1.0)
    grad_qgain = jnp.sum(query_turn * query_hat, axis=(0, 1, 2))
    grad_kgain = jnp.sum(key_turn * key_hat, axis=(0, 1, 2))
    dq_raw = (
        norm_back(query_turn * gain_query, query_hat, query_fac)
        .astype(jnp.bfloat16)
        .reshape(rows_all, heads_here * head_dim)
    )
    dk_raw = (
        norm_back(key_turn * gain_key, key_hat, key_fac)
        .astype(jnp.bfloat16)
        .reshape(rows_all, heads_here * head_dim)
    )
    dv_bf = dvalues.astype(jnp.bfloat16).reshape(rows_all, heads_here * head_dim)
    tkey_round = rounded(dtkeys)
    grad_tkgain = jnp.sum(tkey_round * text_hat, axis=(0, 1, 2))
    dtext_raw = (
        norm_back(tkey_round * gain_text, text_hat, text_fac)
        .astype(jnp.bfloat16)
        .reshape(images, cap_len, heads_here * head_dim)
    )
    dtv_bf = dtvals.astype(jnp.bfloat16).reshape(images, cap_len, heads_here * head_dim)
    grad_query = jnp.einsum("rd,rc->dc", attn_in, dq_raw, preferred_element_type=jnp.float32)
    grad_key = jnp.einsum("rd,rc->dc", attn_in, dk_raw, preferred_element_type=jnp.float32)
    grad_value = jnp.einsum("rd,rc->dc", attn_in, dv_bf, preferred_element_type=jnp.float32)
    attn_part = (
        jnp.einsum("rc,dc->rd", dq_raw, back_query, preferred_element_type=jnp.float32)
        + jnp.einsum("rc,dc->rd", dk_raw, back_key, preferred_element_type=jnp.float32)
        + jnp.einsum("rc,dc->rd", dv_bf, back_value, preferred_element_type=jnp.float32)
    )
    grad_textkey = jnp.einsum("bce,bcf->ef", caption, dtext_raw, preferred_element_type=jnp.float32)
    grad_textval = jnp.einsum("bce,bcf->ef", caption, dtv_bf, preferred_element_type=jnp.float32)
    caption_part = jnp.einsum(
        "bcf,ef->bce", dtext_raw, back_tkey, preferred_element_type=jnp.float32
    ) + jnp.einsum("bcf,ef->bce", dtv_bf, back_tval, preferred_element_type=jnp.float32)
    dattn_in, grad_qgain, grad_kgain, grad_tkgain = (
        lax.psum(attn_part.astype(jnp.bfloat16), "tensor").astype(jnp.float32),
        lax.psum(grad_qgain.astype(jnp.bfloat16), "tensor").astype(jnp.float32),
        lax.psum(grad_kgain.astype(jnp.bfloat16), "tensor").astype(jnp.float32),
        lax.psum(grad_tkgain.astype(jnp.bfloat16), "tensor").astype(jnp.float32),
    )
    dattn_in = dattn_in.reshape(images, length, model_dim)
    grad_gainone = jnp.sum(dattn_in * normed_one * (1.0 + scale_one), axis=(0, 1))
    dscale_one = jnp.sum(dattn_in * normed_one * gain_one, axis=1)
    grad_latents = (
        (dresid + norm_back(dattn_in * gain_one * (1.0 + scale_one), normed_one, factor_one))
        .astype(jnp.bfloat16)
        .reshape(rows_all, model_dim)
    )
    dmod_all = jnp.concatenate([dscale_one, dgate_one, dscale_two, dgate_two], axis=1).astype(
        jnp.bfloat16
    )
    cols_here = back_mod.shape[1]
    dmod_here = lax.dynamic_slice_in_dim(
        dmod_all, lax.axis_index("tensor") * cols_here, cols_here, 1
    )
    grad_modul = jnp.einsum("bt,bc->tc", cond_bf, dmod_here, preferred_element_type=jnp.float32)
    embed_part = jnp.einsum(
        "bc,tc->bt", dmod_here, back_mod, preferred_element_type=jnp.float32
    ) * (sig_embed * (1.0 + embedding * (1.0 - sig_embed)))
    dcaption, dembed = (
        lax.psum_scatter(
            caption_part.astype(jnp.bfloat16), "tensor", scatter_dimension=2, tiled=True
        ).astype(jnp.float32),
        lax.psum_scatter(
            embed_part.astype(jnp.bfloat16), "tensor", scatter_dimension=1, tiled=True
        ).astype(jnp.float32),
    )
    all_grads = tuple(
        (
            lax.psum_scatter(
                grad_query.astype(jnp.bfloat16), "dp", scatter_dimension=0, tiled=True
            ).astype(jnp.float32),
            lax.psum_scatter(
                grad_key.astype(jnp.bfloat16), "dp", scatter_dimension=0, tiled=True
            ).astype(jnp.float32),
            lax.psum_scatter(
                grad_value.astype(jnp.bfloat16), "dp", scatter_dimension=0, tiled=True
            ).astype(jnp.float32),
            lax.psum_scatter(
                grad_output.astype(jnp.bfloat16), "dp", scatter_dimension=1, tiled=True
            ).astype(jnp.float32),
            lax.psum_scatter(
                grad_textkey.astype(jnp.bfloat16), "dp", scatter_dimension=0, tiled=True
            ).astype(jnp.float32),
            lax.psum_scatter(
                grad_textval.astype(jnp.bfloat16), "dp", scatter_dimension=0, tiled=True
            ).astype(jnp.float32),
            lax.psum_scatter(
                grad_gate.astype(jnp.bfloat16), "dp", scatter_dimension=0, tiled=True
            ).astype(jnp.float32),
            lax.psum_scatter(
                grad_up.astype(jnp.bfloat16), "dp", scatter_dimension=0, tiled=True
            ).astype(jnp.float32),
            lax.psum_scatter(
                grad_down.astype(jnp.bfloat16), "dp", scatter_dimension=1, tiled=True
            ).astype(jnp.float32),
            lax.psum_scatter(
                grad_modul.astype(jnp.bfloat16), "dp", scatter_dimension=0, tiled=True
            ).astype(jnp.float32),
            lax.psum_scatter(
                grad_gainone.astype(jnp.bfloat16), "dp", scatter_dimension=0, tiled=True
            ).astype(jnp.float32),
            lax.psum_scatter(
                grad_gaintwo.astype(jnp.bfloat16), "dp", scatter_dimension=0, tiled=True
            ).astype(jnp.float32),
            lax.psum_scatter(
                grad_qgain.astype(jnp.bfloat16), "dp", scatter_dimension=0, tiled=True
            ).astype(jnp.float32),
            lax.psum_scatter(
                grad_kgain.astype(jnp.bfloat16), "dp", scatter_dimension=0, tiled=True
            ).astype(jnp.float32),
            lax.psum_scatter(
                grad_tkgain.astype(jnp.bfloat16), "dp", scatter_dimension=0, tiled=True
            ).astype(jnp.float32),
        )
    )
    return (output, grad_latents, dcaption.astype(jnp.bfloat16), dembed) + all_grads + (grad_xgate,)


def solution(mesh):
    in_specs = (
        P("dp", None),
        P("dp", None),
        P("dp", None, None),
        P("dp"),
        P("dp", None),
        P("dp", None),
        P("dp"),
        P("dp", "tensor"),
        P("dp", "tensor"),
        P("dp", "tensor"),
        P("tensor", "dp"),
        P("dp", "tensor"),
        P("dp", "tensor"),
        P("dp", "tensor"),
        P("dp", "tensor"),
        P("tensor", "dp"),
        P("dp", "tensor"),
        P("dp"),
        P("dp"),
        P("dp"),
        P("dp"),
        P("dp"),
        P("tensor"),
    )
    out_specs = (
        P("dp", None),
        P("dp", None),
        P("dp", None, "tensor"),
        P("dp", "tensor"),
        P("dp", "tensor"),
        P("dp", "tensor"),
        P("dp", "tensor"),
        P("tensor", "dp"),
        P("dp", "tensor"),
        P("dp", "tensor"),
        P("dp", "tensor"),
        P("dp", "tensor"),
        P("tensor", "dp"),
        P("dp", "tensor"),
        P("dp"),
        P("dp"),
        P("dp"),
        P("dp"),
        P("dp"),
        P("tensor"),
    )
    return jax.shard_map(local, mesh=mesh, in_specs=in_specs, out_specs=out_specs, check_vma=False)
```

profile of v0, /device:TPU:0, one launch (start us, length us, event | category | flops | bytes accessed | tf_op | source)
XLA Modules:
  0.0 1970.3 jit_solution(11357988120400581594)
XLA Ops:
  23.1 38.0 %all-reduce.11 = (bf16[1536]{0:T(1024)(128)(2,1)}, bf16[64]{0:T(256)(128)(2,1)S(1)}, bf16[1536]{0:T(1024)(128)(2,1)S(1)}, bf16[64]{0:T(256)(128)(2,1)S(1)}, bf16[64]{0:T(256)(128)(2,1)S(1)}) all-reduce(bf16[1536]{0:T(1024)(128)(2,1)S(1)} %dynamic-update-slice.4, ...), channel_id=1, replica_groups=mesh['dp'=16,'tensor'=2] {'dp'}, use_global_device_ids=true, to_apply=%add.4 | all-reduce | flops 3264 | bytes 13056
  85.5 53.3 %all-gather.20.cloned.1.call-done = bf16[4096,768]{1,0:T(8,128)(2,1)} async-done(((bf16[256,768]{1,0:T(8,128)(2,1)}), bf16[4096,768]{1,0:T(8,128)(2,1)}) %all-gather.20.cloned.1.call-update) | async-done | bytes 6291472 | tf_op jit(solution)/shard_map/all_gather | solution.py:179
  143.6 58.0 %all-gather.22.cloned.1.call-done = bf16[4096,768]{1,0:T(8,128)(2,1)} async-done(((bf16[256,768]{1,0:T(8,128)(2,1)}), bf16[4096,768]{1,0:T(8,128)(2,1)}) %all-gather.22.cloned.1.call-update) | async-done | bytes 6291472 | tf_op jit(solution)/shard_map/all_gather | solution.py:178
  207.9 36.8 %all-gather.18.cloned.1.call-done = bf16[1536,768]{1,0:T(8,128)(2,1)} async-done(((bf16[96,768]{1,0:T(8,128)(2,1)}), bf16[1536,768]{1,0:T(8,128)(2,1)}) %all-gather.18.cloned.1.call-update) | async-done | bytes 2359312 | tf_op jit(solution)/shard_map/all_gather | solution.py:175
  252.4 35.6 %all-gather.16.cloned.1.call-done = bf16[1536,768]{1,0:T(8,128)(2,1)} async-done(((bf16[96,768]{1,0:T(8,128)(2,1)}), bf16[1536,768]{1,0:T(8,128)(2,1)}) %all-gather.16.cloned.1.call-update) | async-done | bytes 2359312 | tf_op jit(solution)/shard_map/all_gather | solution.py:174
  387.9 83.1 %all-reduce.18.cloned.1.call-done = bf16[1024,1536]{1,0:T(8,128)(2,1)} async-done(((bf16[1024,1536]{1,0:T(8,128)(2,1)}), bf16[1024,1536]{1,0:T(8,128)(2,1)}) %all-reduce.18.cloned.1.call-update) | async-done | bytes 3145744 | tf_op jit(solution)/shard_map/psum | solution.py:270
  479.0 56.5 %all-gather.28.cloned.1.call-done = bf16[1536,2048]{1,0:T(8,128)(2,1)} async-done(((bf16[96,2048]{1,0:T(8,128)(2,1)}), bf16[1536,2048]{1,0:T(8,128)(2,1)}) %all-gather.28.cloned.1.call-update) | async-done | bytes 6291472 | tf_op jit(solution)/shard_map/all_gather | solution.py:181
  547.3 51.0 %all-gather.26.cloned.1.call-done = bf16[1536,2048]{1,0:T(8,128)(2,1)} async-done(((bf16[96,2048]{1,0:T(8,128)(2,1)}), bf16[1536,2048]{1,0:T(8,128)(2,1)}) %all-gather.26.cloned.1.call-update) | async-done | bytes 6291472 | tf_op jit(solution)/shard_map/all_gather | solution.py:180
  609.9 51.4 %all-gather.30.cloned.1.call-done = bf16[2048,1536]{0,1:T(8,128)(2,1)} async-done(((bf16[2048,96]{0,1:T(8,128)(2,1)}), bf16[2048,1536]{0,1:T(8,128)(2,1)}) %all-gather.30.cloned.1.call-update) | async-done | bytes 6291472 | tf_op jit(solution)/shard_map/all_gather | solution.py:182
  715.2 69.2 %all-reduce.20.cloned.1.call-done = bf16[1024,1536]{1,0:T(8,128)(2,1)} async-done(((bf16[1024,1536]{1,0:T(8,128)(2,1)}), bf16[1024,1536]{1,0:T(8,128)(2,1)}) %all-reduce.20.cloned.1.call-update) | async-done | bytes 3145744 | tf_op jit(solution)/shard_map/psum | solution.py:340
  822.5 33.0 %multiply_reduce_fusion = (f32[12,1024]{1,0:T(8,128)S(1)}, f32[12,1024,1024]{1,2,0:T(8,128)}) fusion(f32[12,1024,1024]{1,2,0:T(8,128)} %get-tuple-element.251, f32[12,1024]{1,0:T(8,128)S(1)} %log_add_fusion.1, bf16[1024,12,64]{0,2,1:T(8,128)(2,1)} %bitcast.190, bf16[1024,12,64]{0,2,1:T(8,128)(2,1)} %bitcast.210), kind=kOutput, calls=%fused_computation.1 | convolution fusion | flops 1660932096 | bytes 103907328 | tf_op jit(solution)/shard_map/while/body/eval_jaxpr/qhd,khd->hqk/dot_general | solution.py:103
  855.6 40.9 %multiply_convert_fusion = bf16[12,1024,1024]{1,2,0:T(8,128)(2,1)} fusion(f32[12,1024,1024]{1,2,0:T(8,128)} %get-tuple-element.253, f32[12,1024,1024]{1,2,0:T(8,128)} %get-tuple-element.251, f32[12,1024]{1,0:T(8,128)S(1)} %get-tuple-element.252, f32[12,1024]{1,0:T(8,128)S(1)} %log_add_fusion.1), kind=kLoop, calls=%fused_computation | loop fusion | flops 62914560 | bytes 125927424 | tf_op jit(solution)/shard_map/while/body/eval_jaxpr/convert_element_type | solution.py:104
  1036.8 82.0 %all-reduce.22.cloned.1.call-done = (bf16[1024,1536]{1,0:T(8,128)(2,1)}, bf16[1024,1536]{1,0:T(8,128)(2,1)}) async-done(((bf16[1024,1536]{1,0:T(8,128)(2,1)}, bf16[1024,1536]{1,0:T(8,128)(2,1)}), (bf16[1024,1536]{1,0:T(8,128)(2,1)}, bf16[1024,1536]{1,0:T(8,128)(2,1)})) %all-reduce.22.cloned.1.call-update) | async-done | bytes 6291472 | tf_op jit(solution)/shard_map/psum | solution.py:293
  1172.2 39.4 %psum.63 = f32[24]{0:T(128)S(1)} all-reduce(f32[24]{0:T(128)S(1)} %multiply_dynamic-update-slice_fusion), channel_id=1, replica_groups=mesh['dp'=16,'tensor'=2] {'dp','tensor'}, use_global_device_ids=true, to_apply=%region_52.53 | all-reduce | flops 24 | bytes 192 | tf_op jit(solution)/shard_map/psum | solution.py:364
  1214.0 37.5 %reduce-scatter.21.cloned.1.call-done = bf16[96,768]{1,0:T(8,128)(2,1)} async-done(((bf16[1536,768]{1,0:T(8,128)(2,1)}), bf16[96,768]{1,0:T(8,128)(2,1)}) %reduce-scatter.21.cloned.1.call-update) | async-done | bytes 147472 | tf_op jit(solution)/shard_map/reduce_scatter | solution.py:459
  1253.1 64.5 %reduce-scatter.19.cloned.1.call-done = bf16[96,768]{1,0:T(8,128)(2,1)} async-done(((bf16[1536,768]{1,0:T(8,128)(2,1)}), bf16[96,768]{1,0:T(8,128)(2,1)}) %reduce-scatter.19.cloned.1.call-update) | async-done | bytes 147472 | tf_op jit(solution)/shard_map/reduce_scatter | solution.py:456
  1350.2 33.2 %reduce-scatter.17.cloned.1.call-done = bf16[96,768]{1,0:T(8,128)(2,1)} async-done(((bf16[1536,768]{1,0:T(8,128)(2,1)}), bf16[96,768]{1,0:T(8,128)(2,1)}) %reduce-scatter.17.cloned.1.call-update) | async-done | bytes 147472 | tf_op jit(solution)/shard_map/reduce_scatter | solution.py:453
  1392.6 79.3 %reduce-scatter.31.cloned.1.call-done = bf16[96,2048]{1,0:T(8,128)(2,1)} async-done(((bf16[1536,2048]{1,0:T(8,128)(2,1)}), bf16[96,2048]{1,0:T(8,128)(2,1)}) %reduce-scatter.31.cloned.1.call-update) | async-done | bytes 393232 | tf_op jit(solution)/shard_map/reduce_scatter | solution.py:474
  1473.9 86.4 %reduce-scatter.29.cloned.1.call-done = bf16[96,2048]{1,0:T(8,128)(2,1)} async-done(((bf16[1536,2048]{1,0:T(8,128)(2,1)}), bf16[96,2048]{1,0:T(8,128)(2,1)}) %reduce-scatter.29.cloned.1.call-update) | async-done | bytes 393232 | tf_op jit(solution)/shard_map/reduce_scatter | solution.py:471
  1562.2 86.8 %reduce-scatter.33.cloned.1.call-done = bf16[2048,96]{0,1:T(8,128)(2,1)} async-done(((bf16[2048,1536]{0,1:T(8,128)(2,1)}), bf16[2048,96]{0,1:T(8,128)(2,1)}) %reduce-scatter.33.cloned.1.call-update) | async-done | bytes 393232 | tf_op jit(solution)/shard_map/reduce_scatter | solution.py:477
  1664.3 88.1 %reduce-scatter.27.cloned.1.call-done = bf16[256,768]{0,1:T(8,128)(2,1)} async-done(((bf16[4096,768]{0,1:T(8,128)(2,1)}), bf16[256,768]{0,1:T(8,128)(2,1)}) %reduce-scatter.27.cloned.1.call-update) | async-done | bytes 393232 | tf_op jit(solution)/shard_map/reduce_scatter | solution.py:468
  1754.5 86.3 %reduce-scatter.25.cloned.1.call-done = bf16[256,768]{0,1:T(8,128)(2,1)} async-done(((bf16[4096,768]{0,1:T(8,128)(2,1)}), bf16[256,768]{0,1:T(8,128)(2,1)}) %reduce-scatter.25.cloned.1.call-update) | async-done | bytes 393232 | tf_op jit(solution)/shard_map/reduce_scatter | solution.py:465
  1842.8 86.7 %reduce-scatter.35.cloned.1.call-done = bf16[64,3072]{1,0:T(8,128)(2,1)} async-done(((bf16[1024,3072]{1,0:T(8,128)(2,1)}), bf16[64,3072]{1,0:T(8,128)(2,1)}) %reduce-scatter.35.cloned.1.call-update) | async-done | bytes 393232 | tf_op jit(solution)/shard_map/reduce_scatter | solution.py:480
  1931.4 31.9 %reduce-scatter.15.cloned.1.call-done = bf16[1,256,2048]{2,1,0:T(8,128)(2,1)} async-done(((bf16[1,256,4096]{2,1,0:T(8,128)(2,1)}), bf16[1,256,2048]{2,1,0:T(8,128)(2,1)}) %reduce-scatter.15.cloned.1.call-update) | async-done | bytes 1048592 | tf_op jit(solution)/shard_map/reduce_scatter | solution.py:444
  (422 shorter events, 541.6 us)
Async XLA Ops:
  8.0 130.8 %all-gather.20.cloned.1.call-start = ((), (), s32[]{:S(2)}) async-start(), calls=%async_computation.16 | async-start | bytes 6684672 | tf_op jit(solution)/shard_map/all_gather | solution.py:179
  8.7 192.9 %all-gather.22.cloned.1.call-start = ((), (), s32[]{:S(2)}) async-start(), calls=%async_computation.17 | async-start | bytes 6684672 | tf_op jit(solution)/shard_map/all_gather | solution.py:178
  9.5 235.2 %all-gather.18.cloned.1.call-start = ((), (), s32[]{:S(2)}) async-start(), calls=%async_computation.15 | async-start | bytes 2506752 | tf_op jit(solution)/shard_map/all_gather | solution.py:175
  10.1 277.9 %all-gather.16.cloned.1.call-start = ((), (), s32[]{:S(2)}) async-start(), calls=%async_computation.14 | async-start | bytes 2506752 | tf_op jit(solution)/shard_map/all_gather | solution.py:174
  10.6 341.3 %all-gather.14.cloned.1.call-start = ((), (), s32[]{:S(2)}) async-start(), calls=%async_computation.13 | async-start | bytes 2506752 | tf_op jit(solution)/shard_map/all_gather | solution.py:176
  11.2 368.1 %all-gather.24.cloned.1.call-start = ((), (), s32[]{:S(2)}) async-start(), calls=%async_computation.18 | async-start | bytes 2506752 | tf_op jit(solution)/shard_map/all_gather | solution.py:177
  12.0 459.1 %all-reduce.18.cloned.1.call-start = ((), (), s32[]{:S(2)}) async-start(), calls=%async_computation.19 | async-start | bytes 6291456 | tf_op jit(solution)/shard_map/psum | solution.py:270
  385.8 149.6 %all-gather.28.cloned.1.call-start = ((), (), s32[]{:S(2)}) async-start(), calls=%async_computation.21 | async-start | bytes 6684672 | tf_op jit(solution)/shard_map/all_gather | solution.py:181
  386.6 211.8 %all-gather.26.cloned.1.call-start = ((), (), s32[]{:S(2)}) async-start(), calls=%async_computation.20 | async-start | bytes 6684672 | tf_op jit(solution)/shard_map/all_gather | solution.py:180
  387.1 274.2 %all-gather.30.cloned.1.call-start = ((), (), s32[]{:S(2)}) async-start(), calls=%async_computation.22 | async-start | bytes 6684672 | tf_op jit(solution)/shard_map/all_gather | solution.py:182
  387.9 396.6 %all-reduce.20.cloned.1.call-start = ((), (), s32[]{:S(2)}) async-start(), calls=%async_computation.23 | async-start | bytes 6291456 | tf_op jit(solution)/shard_map/psum | solution.py:340
  699.9 418.9 %all-reduce.22.cloned.1.call-start = ((), (), s32[]{:S(2)}) async-start(), calls=%async_computation.36 | async-start | bytes 12582912 | tf_op jit(solution)/shard_map/psum | solution.py:293
  965.1 247.2 %reduce-scatter.23.cloned.1.call-start = ((), (), s32[]{:S(2)}) async-start(), calls=%async_computation.28 | async-start | bytes 2506752 | tf_op jit(solution)/shard_map/reduce_scatter | solution.py:462
  973.1 278.4 %reduce-scatter.21.cloned.1.call-start = ((), (), s32[]{:S(2)}) async-start(), calls=%async_computation.27 | async-start | bytes 2506752 | tf_op jit(solution)/shard_map/reduce_scatter | solution.py:459
  980.0 337.6 %reduce-scatter.19.cloned.1.call-start = ((), (), s32[]{:S(2)}) async-start(), calls=%async_computation.26 | async-start | bytes 2506752 | tf_op jit(solution)/shard_map/reduce_scatter | solution.py:456
  986.9 396.4 %reduce-scatter.17.cloned.1.call-start = ((), (), s32[]{:S(2)}) async-start(), calls=%async_computation.25 | async-start | bytes 2506752 | tf_op jit(solution)/shard_map/reduce_scatter | solution.py:453
  994.0 477.9 %reduce-scatter.31.cloned.1.call-start = ((), (), s32[]{:S(2)}) async-start(), calls=%async_computation.32 | async-start | bytes 6684672 | tf_op jit(solution)/shard_map/reduce_scatter | solution.py:474
  1005.4 554.8 %reduce-scatter.29.cloned.1.call-start = ((), (), s32[]{:S(2)}) async-start(), calls=%async_computation.31 | async-start | bytes 6684672 | tf_op jit(solution)/shard_map/reduce_scatter | solution.py:471
  1016.8 632.2 %reduce-scatter.33.cloned.1.call-start = ((), (), s32[]{:S(2)}) async-start(), calls=%async_computation.33 | async-start | bytes 6684672 | tf_op jit(solution)/shard_map/reduce_scatter | solution.py:477
  1028.8 633.9 %reduce-scatter.37.cloned.1.call-start = ((), (), s32[]{:S(2)}) async-start(), calls=%async_computation.35 | async-start | bytes 393216
  1137.2 615.2 %reduce-scatter.27.cloned.1.call-start = ((), (), s32[]{:S(2)}) async-start(), calls=%async_computation.30 | async-start | bytes 6684672 | tf_op jit(solution)/shard_map/reduce_scatter | solution.py:468
  1142.0 698.8 %reduce-scatter.25.cloned.1.call-start = ((), (), s32[]{:S(2)}) async-start(), calls=%async_computation.29 | async-start | bytes 6684672 | tf_op jit(solution)/shard_map/reduce_scatter | solution.py:465
  1152.2 777.3 %reduce-scatter.35.cloned.1.call-start = ((), (), s32[]{:S(2)}) async-start(), calls=%async_computation.34 | async-start | bytes 6684672 | tf_op jit(solution)/shard_map/reduce_scatter | solution.py:480
  1157.1 806.3 %reduce-scatter.15.cloned.1.call-start = ((), (), s32[]{:S(2)}) async-start(), calls=%async_computation.24 | async-start | bytes 3145728 | tf_op jit(solution)/shard_map/reduce_scatter | solution.py:444
  (109 other events, 3159.6 us)
Sparse Core Ops, SparseCore 0:
  10.4 65.4 all-gather.11
  78.2 60.5 all-gather.19
  141.1 60.4 all-gather.21
  203.7 40.9 all-gather.17
  246.8 41.0 all-gather.15
  290.1 41.0 all-gather.13
  333.5 41.1 all-gather.23
  385.9 85.0 all-reduce.17
  473.6 61.8 all-gather.27
  537.8 60.4 all-gather.25
  600.9 60.4 all-gather.29
  700.0 84.3 all-reduce.19
  965.2 153.5 all-reduce.21
  1122.9 62.9 reduce-scatter.22
  1189.5 61.9 reduce-scatter.20
  1255.6 62.0 reduce-scatter.18
  1321.2 62.0 reduce-scatter.16
  1387.6 84.2 reduce-scatter.30
  1475.8 84.3 reduce-scatter.28
  1564.6 84.4 reduce-scatter.32
  1667.1 85.2 reduce-scatter.26
  1756.3 84.3 reduce-scatter.24
  1845.1 84.3 reduce-scatter.34
  1932.3 30.9 reduce-scatter.14
  (1 shorter events, 10.8 us)
where the time goes:
time: 1980 us; the launch traced here: 1970 us
  waiting for transfers between devices  1290 us (65%)
  matrix products  360 us (18%)
  other arithmetic  154 us (8%)
  blocking collectives  118 us (6%)
  local copies, waits for them, and re-layouts  28.8 us (1%)
  between operations  19.8 us (1%)
    reduce_scatter x1, waiting for transfers between devices, local(): lax.psum_scatter(grad_textval.astype(jnp.bfloat16), 'dp', scatter_dimensi...  88.1 us
    reduce_scatter x1, waiting for transfers between devices, local(): lax.psum_scatter(grad_down.astype(jnp.bfloat16), 'dp', scatter_dimension=...  86.8 us
    reduce_scatter x1, waiting for transfers between devices, local(): lax.psum_scatter(grad_modul.astype(jnp.bfloat16), 'dp', scatter_dimension...  86.7 us
    reduce_scatter x1, waiting for transfers between devices, local(): lax.psum_scatter(grad_gate.astype(jnp.bfloat16), 'dp', scatter_dimension=...  86.4 us
    reduce_scatter x1, waiting for transfers between devices, local(): lax.psum_scatter(grad_textkey.astype(jnp.bfloat16), 'dp', scatter_dimensi...  86.3 us
    psum x1, waiting for transfers between devices, local(): lax.psum(jnp.dot(mixed_heads, full_output, preferred_element_type=jnp.flo...  83.1 us
    psum x1, waiting for transfers between devices, local(): lax.psum(jnp.dot(hidden, full_down, preferred_element_type=jnp.float32).a...  82 us
    reduce_scatter x1, waiting for transfers between devices, local(): lax.psum_scatter(grad_up.astype(jnp.bfloat16), 'dp', scatter_dimension=0,...  79.3 us
  transfers between devices with their start and end apart: 25, of which 22 were waited for; matrix products, arithmetic and copies ran while one was open for 16% of the time, Pallas kernels for 0%

commit v1 on v0

v1 whole, which is shorter than its diff:
```python
import functools
import math

import jax
import jax.numpy as jnp
from jax import lax
from jax.experimental import pallas as pl
from jax.experimental.pallas import tpu as pltpu
from jax.sharding import PartitionSpec as P

EPSILON = 1e-06


def inv_rms(values):
    return lax.rsqrt(jnp.mean(values * values, axis=-1, keepdims=True) + EPSILON)


def time_embed(step_vals, embed_width):
    half_width = embed_width // 2
    frequency = jnp.exp(-math.log(10000.0) * jnp.arange(half_width, dtype=jnp.float32) / half_width)
    phases = step_vals.astype(jnp.float32)[:, None] * frequency
    return jnp.concatenate([jnp.cos(phases), jnp.sin(phases)], axis=1)


def norm_back(grad_hat, normed, factor):
    return factor * (grad_hat - normed * jnp.mean(grad_hat * normed, axis=-1, keepdims=True))


LANES = 128


def lane_ids(rows):
    return lax.broadcasted_iota(jnp.int32, (rows, LANES), 1)


def pair_matrix(same, half):
    row = lax.broadcasted_iota(jnp.int32, (LANES, LANES), 0) // half
    col = lax.broadcasted_iota(jnp.int32, (LANES, LANES), 1) // half
    return jnp.where((row == col) == same, 1.0, 0.0).astype(jnp.bfloat16)


def head_sums(values, matrix):
    high = values.astype(jnp.bfloat16)
    low = (values - high.astype(jnp.float32)).astype(jnp.bfloat16)
    return jnp.dot(high, matrix, preferred_element_type=jnp.float32) + jnp.dot(
        low, matrix, preferred_element_type=jnp.float32
    )


def swap_quarters(values, half):
    rows = values.shape[0]
    first = lane_ids(rows) % half < half // 2
    return jnp.where(
        first,
        pltpu.roll(values, LANES - half // 2, 1),
        pltpu.roll(values, half // 2, 1),
    )


def nt_dot(left, right):
    return lax.dot_general(
        left, right, (((1,), (1,)), ((), ())), preferred_element_type=jnp.float32
    )


def tn_dot(left, right):
    return lax.dot_general(
        left, right, (((0,), (0,)), ((), ())), preferred_element_type=jnp.float32
    )


def attend_kernel(
    half,
    block,
    len_ref,
    raw_ref,
    text_ref,
    cos_ref,
    sin_ref,
    gain_ref,
    tanh_ref,
    mixed_ref,
    qkv_ref,
    tkv_ref,
    own_ref,
    cross_ref,
    lse_ref,
):
    f32, bf16 = jnp.float32, jnp.bfloat16
    rows = raw_ref.shape[0]
    matrix = pair_matrix(True, half)

    def hat(raw):
        return raw * lax.rsqrt(head_sums(raw * raw, matrix) * (1.0 / half) + EPSILON)

    def turned(raw, gain):
        value = hat(raw) * gain
        return (value * cos_ref[...] + swap_quarters(value, half) * sin_ref[...]).astype(bf16)

    query = turned(raw_ref[:, :LANES], gain_ref[0:1])
    key = turned(raw_ref[:, LANES : 2 * LANES], gain_ref[1:2])
    value = raw_ref[:, 2 * LANES :].astype(bf16)
    tkey = (hat(text_ref[:, :LANES]) * gain_ref[2:3]).astype(bf16)
    tval = text_ref[:, LANES:].astype(bf16)
    qkv_ref[:, :LANES] = query
    qkv_ref[:, LANES : 2 * LANES] = key
    qkv_ref[:, 2 * LANES :] = value
    tkv_ref[:, :LANES] = tkey
    tkv_ref[:, LANES:] = tval
    one = jnp.ones((), bf16)
    zero = jnp.zeros((), bf16)

    def pick(a, b):
        return jnp.where(lane_ids(a.shape[0]) < half, a, b)

    def fill(a, fillers, first):
        other = jnp.full(a.shape, fillers, bf16)
        return pick(a, other) if first else pick(other, a)

    value_ones = [fill(value, one, True), fill(value, one, False)]
    tval_ones = [fill(tval, one, True), fill(tval, one, False)]
    keep = lax.broadcasted_iota(jnp.int32, (block, tkey.shape[0]), 1) < len_ref[0]

    def step(i, _):
        here = pl.ds(pl.multiple_of(i * block, block), block)
        q_blk = qkv_ref[here, :LANES] * jnp.asarray(half**-0.5, bf16)
        outs = []
        texts = []
        for head in range(2):
            q_one = fill(q_blk, zero, head == 0)
            e_self = jnp.exp(nt_dot(q_one, key)).astype(bf16)
            outs.append(jnp.dot(e_self, value_ones[head], preferred_element_type=f32))
            e_text = jnp.where(keep, jnp.exp(nt_dot(q_one, tkey)), 0.0).astype(bf16)
            texts.append(jnp.dot(e_text, tval_ones[head], preferred_element_type=f32))
        for n, (a, b) in enumerate((outs, texts)):
            total = pick(b, a)
            lse_ref[here, n * LANES : (n + 1) * LANES] = jnp.log(total)
            res = pick(a, b) / pltpu.roll(total, half, 1)
            if n == 0:
                own = res
                own_ref[here, :] = res
            else:
                cross_ref[here, :] = res
                mixed_ref[here, :] = (own + tanh_ref[0:1] * res).astype(bf16)
        return 0

    lax.fori_loop(0, rows // block, step, 0)


def attend_pairs(cap_len, raw, text, cosine, sine, gains, tanh_lanes, half):
    rows = raw.shape[0]
    pairs = raw.shape[1] // (3 * LANES)
    caps = text.shape[0]
    width = pairs * LANES
    f32, bf16 = jnp.float32, jnp.bfloat16
    col = lambda n, w: pl.BlockSpec((n, w), lambda p: (0, p))
    fix = lambda n: pl.BlockSpec((n, LANES), lambda p: (0, 0))
    return pl.pallas_call(
        functools.partial(attend_kernel, half, min(256, rows)),
        grid=(pairs,),
        in_specs=[
            pl.BlockSpec(memory_space=pltpu.SMEM),
            col(rows, 3 * LANES),
            col(caps, 2 * LANES),
            fix(rows),
            fix(rows),
            fix(8),
            col(8, LANES),
        ],
        out_specs=[
            col(rows, LANES),
            col(rows, 3 * LANES),
            col(caps, 2 * LANES),
            col(rows, LANES),
            col(rows, LANES),
            col(rows, 2 * LANES),
        ],
        out_shape=[
            jax.ShapeDtypeStruct((rows, width), bf16),
            jax.ShapeDtypeStruct((rows, 3 * width), bf16),
            jax.ShapeDtypeStruct((caps, 2 * width), bf16),
            jax.ShapeDtypeStruct((rows, width), f32),
            jax.ShapeDtypeStruct((rows, width), f32),
            jax.ShapeDtypeStruct((rows, 2 * width), f32),
        ],
        compiler_params=pltpu.CompilerParams(vmem_limit_bytes=50 * 2**20),
        name="attend_fwd",
    )(cap_len, raw, text, cosine, sine, gains, tanh_lanes)


def attend_back_kernel(
    half,
    block,
    len_ref,
    qkv_ref,
    tkv_ref,
    raw_ref,
    text_ref,
    own_ref,
    cross_ref,
    lse_ref,
    dmix_ref,
    cos_ref,
    sin_ref,
    gain_ref,
    tanh_ref,
    dqkv_ref,
    dtext_ref,
    stat_ref,
    qs_ref,
    os_ref,
    cq_ref,
    oc_ref,
    dq_ref,
    dk_ref,
    dv_ref,
    dtk_ref,
    dtv_ref,
):
    f32, bf16 = jnp.float32, jnp.bfloat16
    rows = raw_ref.shape[0]
    same = pair_matrix(True, half)
    cross_matrix = pair_matrix(False, half)

    def pick(a, b):
        return jnp.where(lane_ids(a.shape[0]) < half, a, b)

    def parts(value):
        spot = lane_ids(rows) % half
        high = value.astype(bf16).astype(f32)
        rest = value - high
        mid = rest.astype(bf16).astype(f32)
        low = rest - mid
        return jnp.where(
            spot == 0, high, jnp.where(spot == 1, mid, jnp.where(spot == 2, low, 0.0))
        ).astype(bf16)

    def ones_like_parts(value):
        return jnp.where(lane_ids(value.shape[0]) % half < 3, 1.0, 0.0).astype(bf16)

    grad = dmix_ref[...]
    grad_f = grad.astype(f32)
    other_f = (grad_f * tanh_ref[0:1]).astype(bf16).astype(f32)
    other = other_f.astype(bf16)
    delta_s = parts(-head_sums(grad_f * own_ref[...], cross_matrix))
    delta_c = parts(-head_sums(other_f * cross_ref[...], cross_matrix))
    lse_s = parts(-lse_ref[:, :LANES])
    lse_c = parts(-lse_ref[:, LANES:])
    query = qkv_ref[:, :LANES] * jnp.asarray(half**-0.5, bf16)
    key = qkv_ref[:, LANES : 2 * LANES]
    value = qkv_ref[:, 2 * LANES :]
    tkey = tkv_ref[:, :LANES]
    tval = tkv_ref[:, LANES:]
    for head in range(2):
        aug = (lambda a, b: pick(a, b)) if head == 0 else (lambda a, b: pick(b, a))
        qs_ref[head] = aug(query, lse_s)
        cq_ref[head] = aug(query, lse_c)
        os_ref[head] = aug(grad, delta_s)
        oc_ref[head] = aug(other, delta_c)
    zero = jnp.zeros((), bf16)

    def only(a, head):
        blank = jnp.full(a.shape, zero, bf16)
        return pick(a, blank) if head == 0 else pick(blank, a)

    def aug_ones(a, head):
        ones = ones_like_parts(a)
        return pick(a, ones) if head == 0 else pick(ones, a)

    key_aug = [aug_ones(key, h) for h in range(2)]
    val_aug = [aug_ones(value, h) for h in range(2)]
    tkey_aug = [aug_ones(tkey, h) for h in range(2)]
    tval_aug = [aug_ones(tval, h) for h in range(2)]
    key_only = [only(key, h) for h in range(2)]
    tkey_only = [only(tkey, h) for h in range(2)]
    dk_ref[...] = jnp.zeros_like(dk_ref)
    dv_ref[...] = jnp.zeros_like(dv_ref)
    dtk_ref[...] = jnp.zeros_like(dtk_ref)
    dtv_ref[...] = jnp.zeros_like(dtv_ref)
    caps = tkey.shape[0]
    keep = lax.broadcasted_iota(jnp.int32, (caps, block), 0) < len_ref[0]

    def step(i, _):
        here = pl.ds(pl.multiple_of(i * block, block), block)
        dq = jnp.zeros((block, LANES), f32)
        for head in range(2):
            q_aug, o_aug = qs_ref[head, here], os_ref[head, here]
            q_only, o_only = only(q_aug, head), only(o_aug, head)
            probs = jnp.exp(nt_dot(key_aug[head], q_aug))
            grads = (probs * nt_dot(val_aug[head], o_aug)).astype(bf16)
            dv_ref[...] += jnp.dot(probs.astype(bf16), o_only, preferred_element_type=f32)
            dk_ref[...] += jnp.dot(grads, q_only, preferred_element_type=f32)
            dq += tn_dot(grads, key_only[head])
            q_aug, o_aug = cq_ref[head, here], oc_ref[head, here]
            o_only = only(o_aug, head)
            probs = jnp.where(keep, jnp.exp(nt_dot(tkey_aug[head], q_aug)), 0.0)
            grads = (probs * nt_dot(tval_aug[head], o_aug)).astype(bf16)
            dtv_ref[...] += jnp.dot(probs.astype(bf16), o_only, preferred_element_type=f32)
            dtk_ref[...] += jnp.dot(grads, q_only, preferred_element_type=f32)
            dq += tn_dot(grads, tkey_only[head])
        dq_ref[here, :] = dq * half**-0.5
        return 0

    lax.fori_loop(0, rows // block, step, 0)

    def bring_back(grad_in, raw, gain, rotate):
        inv = lax.rsqrt(head_sums(raw * raw, same) * (1.0 / half) + EPSILON)
        normed = raw * inv
        turn = grad_in.astype(bf16).astype(f32)
        if rotate:
            turn = turn * cos_ref[...] - swap_quarters(turn, half) * sin_ref[...]
        scaled = turn * gain
        mean = head_sums(scaled * normed, same) * (1.0 / half)
        return (inv * (scaled - normed * mean)).astype(bf16), jnp.sum(
            turn * normed, axis=0, keepdims=True
        )

    res, stat_q = bring_back(dq_ref[...], raw_ref[:, :LANES], gain_ref[0:1], True)
    dqkv_ref[:, :LANES] = res
    res, stat_k = bring_back(dk_ref[...], raw_ref[:, LANES : 2 * LANES], gain_ref[1:2], True)
    dqkv_ref[:, LANES : 2 * LANES] = res
    dqkv_ref[:, 2 * LANES :] = dv_ref[...].astype(bf16)
    res, stat_t = bring_back(dtk_ref[...], text_ref[:, :LANES], gain_ref[2:3], False)
    dtext_ref[:, :LANES] = res
    dtext_ref[:, LANES:] = dtv_ref[...].astype(bf16)
    stat_x = jnp.sum(grad_f * cross_ref[...], axis=0, keepdims=True)
    stat_ref[...] = jnp.concatenate(
        [stat_q, stat_k, stat_t, stat_x, jnp.zeros((4, LANES), f32)], axis=0
    )


def attend_back_pairs(window, arrays, tables, half):
    cap_len, qkv, tkv, raw, text, own, cross, lse, dmix = arrays
    cosine, sine, gains, tanh_lanes = tables
    first, pairs = window
    rows, caps = raw.shape[0], text.shape[0]
    width = pairs * LANES
    f32, bf16 = jnp.float32, jnp.bfloat16

    def col(n, w):
        return pl.BlockSpec((n, w), lambda p: (0, p + first))

    def out(n, w):
        return pl.BlockSpec((n, w), lambda p: (0, p))

    def fix(n):
        return pl.BlockSpec((n, LANES), lambda p: (0, 0))

    return pl.pallas_call(
        functools.partial(attend_back_kernel, half, min(512, rows)),
        grid=(pairs,),
        in_specs=[
            pl.BlockSpec(memory_space=pltpu.SMEM),
            col(rows, 3 * LANES),
            col(caps, 2 * LANES),
            col(rows, 3 * LANES),
            col(caps, 2 * LANES),
            col(rows, LANES),
            col(rows, LANES),
            col(rows, 2 * LANES),
            col(rows, LANES),
            fix(rows),
            fix(rows),
            fix(8),
            col(8, LANES),
        ],
        out_specs=[out(rows, 3 * LANES), out(caps, 2 * LANES), out(8, LANES)],
        out_shape=[
            jax.ShapeDtypeStruct((rows, 3 * width), bf16),
            jax.ShapeDtypeStruct((caps, 2 * width), bf16),
            jax.ShapeDtypeStruct((8, width), f32),
        ],
        scratch_shapes=[pltpu.VMEM((2, rows, LANES), bf16)] * 4
        + [pltpu.VMEM((rows, LANES), f32)] * 3
        + [pltpu.VMEM((caps, LANES), f32)] * 2,
        compiler_params=pltpu.CompilerParams(vmem_limit_bytes=50 * 2**20),
        name="attend_bwd",
    )(cap_len, qkv, tkv, raw, text, own, cross, lse, dmix, cosine, sine, gains, tanh_lanes)


def gated(value, *tokens):
    return lax.optimization_barrier((value,) + tokens)[0]


def chip_ring(size):
    depth = size // 4
    return [2 * q if q < depth else 2 * (2 * depth - 1 - q) + 1 for q in range(size // 2)]


def ring_perm(size, step):
    order = chip_ring(size)
    count = len(order)
    return [
        (order[q] * 2 + c, order[(q + step) % count] * 2 + c) for q in range(count) for c in range(2)
    ]


def flip_perm(size, bit):
    return [(i, i ^ bit) for i in range(size)]


def ring_place(size):
    depth = size // 4
    index = lax.axis_index("dp")
    chip = index // 2
    level = chip // 2
    return jnp.where(chip % 2 == 0, level, 2 * depth - 1 - level), index % 2


def chip_at(place, size):
    depth = size // 4
    place = place % (2 * depth)
    return jnp.where(place < depth, 2 * place, 2 * (2 * depth - 1 - place) + 1)


def ring_gather(shard, size):
    count = size // 2
    rows, cols = shard.shape
    half = cols // 2
    place, core = ring_place(size)
    swap = flip_perm(size, 1)
    ahead, behind = ring_perm(size, 1), ring_perm(size, -1)
    pieces = [(0, 0, shard)]
    fwd = bwd = shard
    marks = []
    for step in range(1, count // 2):
        fwd = lax.ppermute(fwd, "dp", ahead)
        bwd = lax.ppermute(bwd, "dp", behind)
        pieces += [(-step, 0, fwd), (step, 0, bwd)]
        marks.append(fwd)
    last_f = lax.ppermute(fwd[:, :half], "dp", ahead)
    last_b = lax.ppermute(bwd[:, half:], "dp", behind)
    pieces += [(count // 2, 0, last_f), (count // 2, half, last_b)]
    marks.append(last_f)
    full = jnp.zeros((count, 2, rows, cols), shard.dtype)
    for offset, low, piece in pieces:
        other = lax.ppermute(piece, "dp", swap)
        chip = chip_at(place + offset, size)
        full = lax.dynamic_update_slice(full, piece[None, None], (chip, core, 0, low))
        full = lax.dynamic_update_slice(full, other[None, None], (chip, 1 - core, 0, low))
    return full.reshape(size * rows, cols), marks


def split_cols(left, size):
    rows, cols = left.shape
    blocks = left.reshape(rows, size // 2, 2, cols // size)
    core = lax.axis_index("dp") % 2
    mine = lax.dynamic_index_in_dim(blocks, core, 2, keepdims=False).reshape(rows, cols // 2)
    other = lax.dynamic_index_in_dim(blocks, 1 - core, 2, keepdims=False).reshape(rows, cols // 2)
    return mine, other


def core_away(parts, right, size):
    away = jnp.einsum("rm,rc->mc", parts[1], right, preferred_element_type=jnp.float32)
    away = away.astype(jnp.bfloat16)
    return away, lax.ppermute(away, "dp", flip_perm(size, 1))


def core_keep(parts, right, came, size):
    kept = jnp.einsum("rm,rc->mc", parts[0], right, preferred_element_type=jnp.float32)
    kept = (kept + came.astype(jnp.float32)).astype(jnp.bfloat16)
    return kept.reshape(size // 2, -1, right.shape[1])


def side_start(mine, size):
    count, rows, cols = mine.shape
    side = (lax.axis_index("dp") // 2) % 2
    grid = mine.reshape(count // 2, 2, rows, cols)
    away = lax.dynamic_index_in_dim(grid, 1 - side, 1, keepdims=False)
    kept = lax.dynamic_index_in_dim(grid, side, 1, keepdims=False)
    return kept, lax.ppermute(away, "dp", flip_perm(size, 2))


def side_end(kept, came):
    return (kept.astype(jnp.float32) + came.astype(jnp.float32)).astype(jnp.bfloat16)


def line_start(held, size):
    depth = held.shape[0]
    level = lax.axis_index("dp") // 4
    pieces = [lax.dynamic_index_in_dim(held, level, 0, keepdims=False)]
    for step in range(1, depth):
        piece = lax.dynamic_index_in_dim(held, (level + step) % depth, 0, keepdims=False)
        perm = [(i, (i + 4 * step) % size) for i in range(size)]
        pieces.append(lax.ppermute(piece, "dp", perm))
    return pieces


def line_end(pieces):
    total = pieces[0].astype(jnp.float32)
    for piece in pieces[1:]:
        total = total + piece.astype(jnp.float32)
    return total


def swap_start(part, size, chunks):
    step = part.shape[0] // chunks
    own = [part[i * step : (i + 1) * step] for i in range(chunks)]
    if size == 2:
        return own, [lax.ppermute(o, "tensor", flip_perm(size, 1)) for o in own]
    return own, [lax.psum(o, "tensor") for o in own]


def swap_end(own, came, size):
    f32 = jnp.float32
    both = [o.astype(f32) + c.astype(f32) if size == 2 else c.astype(f32) for o, c in zip(own, came)]
    return jnp.concatenate(both, axis=0) if len(both) > 1 else both[0]


def small_gather(value, name, size):
    bit = 1
    index = lax.axis_index(name)
    while bit < size:
        came = lax.ppermute(value, name, flip_perm(size, bit))
        upper = (index // bit) % 2 == 1
        value = jnp.where(
            upper, jnp.concatenate([came, value], 0), jnp.concatenate([value, came], 0)
        )
        bit *= 2
    return value


def small_scatter(value, name, size):
    bit = size // 2
    index = lax.axis_index(name)
    while bit:
        upper = (index // bit) % 2 == 1
        low, high = value[: value.shape[0] // 2], value[value.shape[0] // 2 :]
        came = lax.ppermute(jnp.where(upper, low, high), name, flip_perm(size, bit))
        value = jnp.where(upper, high, low) + came
        bit //= 2
    return value


def small_sum(value, name, size):
    bit = 1
    while bit < size:
        value = value + lax.ppermute(value, name, flip_perm(size, bit))
        bit *= 2
    return value


def tensor_scatter(part, size):
    if size == 2:
        index = lax.axis_index("tensor")
        width = part.shape[1] // 2
        away = lax.dynamic_slice_in_dim(part, (1 - index) * width, width, 1)
        kept = lax.dynamic_slice_in_dim(part, index * width, width, 1)
        came = lax.ppermute(away, "tensor", flip_perm(size, 1))
        return kept.astype(jnp.float32) + came.astype(jnp.float32)
    return lax.psum_scatter(part, "tensor", scatter_dimension=1, tiled=True).astype(jnp.float32)


def pair_cols(arrays, head_dim):
    rows, cols = arrays[0].shape
    pad = -cols % LANES
    arrays = [jnp.pad(a, ((0, 0), (0, pad))) if pad else a for a in arrays]
    pairs = (cols + pad) // LANES
    return jnp.stack([a.reshape(rows, pairs, LANES) for a in arrays], axis=2).reshape(rows, -1)


def unpair_cols(array, count, cols):
    rows = array.shape[0]
    split = array.reshape(rows, -1, count, LANES)
    return [split[:, :, i].reshape(rows, -1)[:, :cols] for i in range(count)]


def rotary_tables(row_pos, col_pos, quarter, repeat):
    frequency = jnp.exp(-math.log(10000.0) * jnp.arange(quarter, dtype=jnp.float32) / quarter)
    angles = jnp.concatenate(
        [
            row_pos.astype(jnp.float32)[:, None] * frequency,
            col_pos.astype(jnp.float32)[:, None] * frequency,
        ],
        axis=1,
    )
    sine = jnp.sin(angles)
    return jnp.tile(jnp.cos(angles), (1, 2 * repeat)), jnp.tile(
        jnp.concatenate([-sine, sine], axis=1), (1, repeat)
    )


def local(
    size,
    groups,
    latents,
    cotangent,
    caption,
    caption_lens,
    patch_row,
    patch_col,
    timestep,
    query_proj,
    key_proj,
    value_proj,
    output_proj,
    textkey_proj,
    textval_proj,
    gate_proj,
    up_proj,
    down_proj,
    modulation,
    attn_gain,
    ffn_gain,
    query_gain,
    key_gain,
    textkey_gain,
    cross_gate,
):
    f32, bf16 = jnp.float32, jnp.bfloat16
    rows_w, chan = query_proj.shape
    units = gate_proj.shape[1]
    head_part = query_gain.shape[0]
    head_dim = head_part * size
    heads_here = chan // head_dim
    model_dim = latents.shape[1]
    padded = chan + -chan % LANES
    pairs = padded // LANES
    dp_index = lax.axis_index("dp")
    tensor_index = lax.axis_index("tensor")

    text_shard = pair_cols([textkey_proj, textval_proj], head_dim)
    text_set = lax.all_gather(text_shard, "dp", axis=0, tiled=True)
    small = jnp.concatenate(
        [
            attn_gain.astype(f32),
            ffn_gain.astype(f32),
            query_gain.astype(f32),
            key_gain.astype(f32),
            textkey_gain.astype(f32),
            timestep.astype(f32),
        ]
    )[None]
    small_all = small_gather(small, "dp", size)
    first = jnp.concatenate(
        [pair_cols([query_proj, key_proj, value_proj], head_dim), pair_cols([output_proj.T], head_dim)],
        axis=1,
    )
    full_qkvo, _ = ring_gather(first, size)
    full_qkv, full_out_t = full_qkvo[:, : 3 * padded], full_qkvo[:, 3 * padded :]
    third = gated(jnp.concatenate([gate_proj, up_proj, down_proj.T], axis=1), small_all)
    ffn_set = lax.all_gather(third, "dp", axis=0, tiled=True)

    cuts = [rows_w, 2 * rows_w, 2 * rows_w + head_part]
    gain_one = small_all[:, : cuts[0]].reshape(-1)
    gain_two = small_all[:, cuts[0] : cuts[1]].reshape(-1)
    gain_query = small_all[:, cuts[1] : cuts[2]].reshape(-1)
    gain_key = small_all[:, cuts[2] : cuts[2] + head_part].reshape(-1)
    gain_text = small_all[:, cuts[2] + head_part : cuts[2] + 2 * head_part].reshape(-1)
    steps_all = small_all[:, cuts[2] + 2 * head_part :].reshape(-1)
    embed_rows = modulation.shape[0]
    embed_dim = embed_rows * size
    embed_all = time_embed(steps_all, embed_dim)
    cond_all = (embed_all * jax.nn.sigmoid(embed_all)).astype(bf16)
    cond_here = lax.dynamic_slice_in_dim(cond_all, dp_index * embed_rows, embed_rows, 1)
    mod_part = jnp.dot(cond_here, modulation, preferred_element_type=f32)
    mod_here = small_scatter(mod_part, "dp", size)
    mod_all = small_gather(mod_here, "tensor", groups).reshape(1, -1)
    scale_one = mod_all[:, 0:model_dim]
    gate_one = jnp.tanh(mod_all[:, model_dim : 2 * model_dim])
    scale_two = mod_all[:, 2 * model_dim : 3 * model_dim]
    gate_two = jnp.tanh(mod_all[:, 3 * model_dim : 4 * model_dim])
    tanh_cross = jnp.tanh(cross_gate.astype(f32))
    tanh_lanes = jnp.pad(jnp.repeat(tanh_cross, head_dim), (0, padded - chan))
    tanh_lanes = jnp.broadcast_to(tanh_lanes[None], (8, padded))
    per_tile = LANES // head_dim
    gain_lanes = jnp.pad(
        jnp.tile(jnp.stack([gain_query, gain_key, gain_text]), (1, per_tile)), ((0, 5), (0, 0))
    )
    cosine, sine = rotary_tables(patch_row[0], patch_col[0], head_dim // 4, per_tile)
    tables = (cosine, sine, gain_lanes, tanh_lanes)

    resid_in = latents.astype(f32)
    factor_one = inv_rms(resid_in)
    normed_one = resid_in * factor_one
    attn_in = (normed_one * gain_one * (1.0 + scale_one)).astype(bf16)
    qkv_raw = jnp.dot(attn_in, full_qkv, preferred_element_type=f32)
    cap_in = caption[0]
    full_text = gated(text_set, qkv_raw)
    text_raw = jnp.dot(cap_in, full_text, preferred_element_type=f32)
    mixed_heads, qkv_bf, tkv_bf, own_out, cross_out, lse = attend_pairs(
        caption_lens, qkv_raw, text_raw, cosine, sine, gain_lanes, tanh_lanes, head_dim
    )
    attn_part = jnp.einsum("rc,dc->rd", mixed_heads, full_out_t, preferred_element_type=f32)
    attn_part = attn_part.astype(bf16)
    attn_own, attn_came = swap_start(attn_part, groups, 1)

    late_in, late_cap, late_cot = gated((attn_in, cap_in, cotangent), attn_part)
    in_split = split_cols(late_in, size)
    cap_split = split_cols(late_cap, size)
    grad_out = late_cot.astype(f32)
    grad_ffn = (gate_two * grad_out).astype(bf16)
    ffn_split = split_cols(grad_ffn, size)
    full_ffn = gated(ffn_set, attn_part, in_split, cap_split, ffn_split)
    full_gu, full_down_t = full_ffn[:, : 2 * units], full_ffn[:, 2 * units :]
    dhidden = jnp.dot(grad_ffn, full_down_t, preferred_element_type=f32)
    attn_came = gated(attn_came, dhidden)
    attn_out = swap_end(attn_own, attn_came, groups)

    residual = resid_in + gate_one * attn_out
    factor_two = inv_rms(residual)
    normed_two = residual * factor_two
    ffn_in = (normed_two * gain_two * (1.0 + scale_two)).astype(bf16)
    gate_pre = jnp.dot(ffn_in, full_gu[:, :units], preferred_element_type=f32)
    up_pre = jnp.dot(ffn_in, full_gu[:, units:], preferred_element_type=f32)
    sig_gate = jax.nn.sigmoid(gate_pre)
    act_gate = gate_pre * sig_gate
    hidden = (act_gate * up_pre).astype(bf16)
    dgate_pre = (dhidden * up_pre * sig_gate * (1.0 + gate_pre * (1.0 - sig_gate))).astype(bf16)
    dup_pre = (dhidden * act_gate).astype(bf16)
    dboth = jnp.concatenate([dgate_pre, dup_pre], axis=1)
    dffn_part = jnp.einsum("rf,df->rd", dboth, full_gu, preferred_element_type=f32).astype(bf16)
    dffn_own, dffn_came = swap_start(dffn_part, groups, 1)

    hidden_l, dboth_l, ffn_in_l = gated((hidden, dboth, ffn_in), dffn_part)
    gu_split = split_cols(ffn_in_l, size)
    down_away, down_came = core_away(ffn_split, hidden_l, size)
    gu_away, gu_came = core_away(gu_split, dboth_l, size)
    hidden_l = gated(hidden, down_away, gu_away)
    ffn_part = jnp.einsum("rf,df->rd", hidden_l, full_down_t, preferred_element_type=f32)
    ffn_part = ffn_part.astype(bf16)
    ffn_own, ffn_came = swap_start(gated(ffn_part, dffn_part), groups, 1)
    down_came = gated(down_came, ffn_part)
    down_kept, down_x = side_start(core_keep(ffn_split, hidden, down_came, size), size)
    gu_came = gated(gu_came, down_kept)
    gu_kept, gu_x = side_start(core_keep(gu_split, dboth, gu_came, size), size)
    dffn_came = gated(dffn_came, gu_kept)
    dffn_in = swap_end(dffn_own, dffn_came, groups)

    gain_mul = gain_two * (1.0 + scale_two)
    weighed = jnp.sum(dffn_in * normed_two, axis=0)
    grad_gaintwo = weighed * (1.0 + scale_two[0])
    dscale_two = weighed * gain_two
    dresid = grad_out + norm_back(dffn_in * gain_mul, normed_two, factor_two)
    dgate_one = jnp.sum(dresid * attn_out, axis=0) * (1.0 - gate_one[0] ** 2)
    grad_attn = (gate_one * dresid).astype(bf16)
    dmixed = jnp.dot(grad_attn, full_out_t, preferred_element_type=f32).astype(bf16)
    out_split = split_cols(gated(grad_attn, dmixed), size)
    out_away, out_came = core_away(out_split, mixed_heads, size)
    down_x = gated(down_x, out_away)
    down_line = line_start(side_end(down_kept, down_x), size)
    out_came = gated(out_came, down_line[0])
    out_kept, out_x = side_start(core_keep(out_split, mixed_heads, out_came, size), size)

    split = pairs - pairs // 2
    windows = [(0, split), (split, pairs - split)]
    arrays = (caption_lens, qkv_bf, tkv_bf, qkv_raw, text_raw, own_out, cross_out, lse)
    qkv_cols = [(3 * LANES * a, 3 * LANES * (a + b)) for a, b in windows]
    text_cols = [(2 * LANES * a, 2 * LANES * (a + b)) for a, b in windows]
    dmixed_a = gated(dmixed, out_kept, down_line[0])
    dqkv_a, dtext_a, stats_a = attend_back_pairs(windows[0], arrays + (dmixed_a,), tables, head_dim)
    gu_x = gated(gu_x, dqkv_a)
    gu_line = line_start(side_end(gu_kept, gu_x), size)
    text_a_away, text_a_came = core_away(cap_split, gated(dtext_a, gu_line[0]), size)
    qkv_a_away, qkv_a_came = core_away(in_split, gated(dqkv_a, text_a_away), size)
    out_x = gated(out_x, qkv_a_away)
    out_line = line_start(side_end(out_kept, out_x), size)
    text_a_came = gated(text_a_came, out_line[0])
    text_a_kept, text_a_x = side_start(core_keep(cap_split, dtext_a, text_a_came, size), size)
    qkv_a_came = gated(qkv_a_came, text_a_kept)
    qkv_a_kept, qkv_a_x = side_start(core_keep(in_split, dqkv_a, qkv_a_came, size), size)
    dmixed_b = gated(dmixed, qkv_a_kept)
    dqkv_b, dtext_b, stats_b = attend_back_pairs(windows[1], arrays + (dmixed_b,), tables, head_dim)
    dqkv = jnp.concatenate([dqkv_a, dqkv_b], axis=1)
    dtext = jnp.concatenate([dtext_a, dtext_b], axis=1)
    dattn_part = jnp.einsum("rc,dc->rd", dqkv, full_qkv, preferred_element_type=f32).astype(bf16)
    dattn_own, dattn_came = swap_start(dattn_part, groups, 1)
    dtext_l, dqkv_l = gated((dtext_b, dqkv_b), dattn_part)
    text_b_away, text_b_came = core_away(cap_split, dtext_l, size)
    qkv_b_away, qkv_b_came = core_away(in_split, dqkv_l, size)
    text_a_x = gated(text_a_x, text_b_away, qkv_b_away)
    text_a_line = line_start(side_end(text_a_kept, text_a_x), size)
    text_b_came = gated(text_b_came, text_a_line[0])
    text_b_kept, text_b_x = side_start(core_keep(cap_split, dtext_b, text_b_came, size), size)
    qkv_b_came = gated(qkv_b_came, text_b_kept)
    qkv_b_kept, qkv_b_x = side_start(core_keep(in_split, dqkv_b, qkv_b_came, size), size)
    qkv_a_x = gated(qkv_a_x, qkv_b_kept)
    qkv_a_line = line_start(side_end(qkv_a_kept, qkv_a_x), size)
    caption_part = jnp.einsum(
        "bf,ef->be", gated(dtext, qkv_a_line[0]), full_text, preferred_element_type=f32
    )
    dcaption = tensor_scatter(caption_part.astype(bf16), groups)

    stats = jnp.concatenate([stats_a, stats_b], axis=1)
    stat_sums = stats[:4, :chan].reshape(4, heads_here, head_dim)
    xgate_here = jnp.sum(stat_sums[3], axis=1) * (1.0 - tanh_cross**2)
    grad_xgate = small_sum(xgate_here, "dp", size)
    ffn_came = gated(ffn_came, caption_part)
    ffn_out = swap_end(ffn_own, ffn_came, groups)
    output = (residual + gate_two * ffn_out).astype(bf16)
    dgate_two = jnp.sum(grad_out * ffn_out, axis=0) * (1.0 - gate_two[0] ** 2)
    down_t = line_end(gated(down_line, caption_part))
    gate_up = line_end(gated(gu_line, down_t))
    output_t = line_end(gated(out_line, gate_up))
    text_b_x = gated(text_b_x, output_t)
    text_b_line = line_start(side_end(text_b_kept, text_b_x), size)
    qkv_b_x = gated(qkv_b_x, text_b_line[0])
    qkv_b_line = line_start(side_end(qkv_b_kept, qkv_b_x), size)
    dattn_came = gated(dattn_came, qkv_b_line[0])
    dattn_in = swap_end(dattn_own, dattn_came, groups)
    weighed_one = jnp.sum(dattn_in * normed_one, axis=0)
    grad_gainone = weighed_one * (1.0 + scale_one[0])
    dscale_one = weighed_one * gain_one
    grad_latents = (
        dresid + norm_back(dattn_in * gain_one * (1.0 + scale_one), normed_one, factor_one)
    ).astype(bf16)
    text_a = line_end(gated(text_a_line, dattn_in))
    qkv_a = line_end(gated(qkv_a_line, dattn_in))

    dmod_all = jnp.concatenate([dscale_one, dgate_one, dscale_two, dgate_two]).astype(bf16)
    cols_here = modulation.shape[1]
    dmod_here = lax.dynamic_slice_in_dim(dmod_all, tensor_index * cols_here, cols_here, 0)
    dmod_set = small_gather(dmod_here[None].astype(f32), "dp", size).astype(bf16)
    grad_modul = jnp.einsum("bt,bc->tc", cond_here, dmod_set, preferred_element_type=f32)
    embed_part = jnp.einsum("bc,tc->bt", dmod_set, modulation, preferred_element_type=f32)
    embed_set = small_gather(embed_part[None], "dp", size)
    embed_row = lax.dynamic_index_in_dim(embed_set, dp_index, 1, keepdims=False).reshape(1, -1)
    embed_sum = small_sum(embed_row, "tensor", groups)
    embed_own = lax.dynamic_slice_in_dim(embed_all, dp_index, 1, 0)
    sig_own = jax.nn.sigmoid(embed_own)
    dembed_all = embed_sum * (sig_own * (1.0 + embed_own * (1.0 - sig_own)))
    width = embed_dim // groups
    dembed = lax.dynamic_slice_in_dim(dembed_all, tensor_index * width, width, 1)

    gains_heads = small_sum(jnp.sum(stat_sums[:3], axis=1), "tensor", groups)
    gains_set = jnp.concatenate(
        [
            grad_gainone.reshape(size, rows_w),
            grad_gaintwo.reshape(size, rows_w),
            gains_heads[0].reshape(size, head_part),
            gains_heads[1].reshape(size, head_part),
            gains_heads[2].reshape(size, head_part),
        ],
        axis=1,
    )
    gains_own = small_scatter(gains_set, "dp", size)[0]
    text_b = line_end(text_b_line)
    qkv_b = line_end(qkv_b_line)
    qkv_grads = jnp.concatenate([qkv_a, qkv_b], axis=1)
    text_grads = jnp.concatenate([text_a, text_b], axis=1)
    return (
        output,
        grad_latents,
        dcaption.astype(bf16)[None],
        dembed,
        *unpair_cols(qkv_grads, 3, chan),
        output_t[:, :chan].T,
        *unpair_cols(text_grads, 2, chan),
        gate_up[:, :units],
        gate_up[:, units:],
        down_t.T,
        grad_modul,
        gains_own[: cuts[0]],
        gains_own[cuts[0] : cuts[1]],
        gains_own[cuts[1] : cuts[2]],
        gains_own[cuts[2] : cuts[2] + head_part],
        gains_own[cuts[2] + head_part :],
        grad_xgate,
    )


def solution(mesh):
    in_specs = (
        P("dp", None),
        P("dp", None),
        P("dp", None, None),
        P("dp"),
        P("dp", None),
        P("dp", None),
        P("dp"),
        P("dp", "tensor"),
        P("dp", "tensor"),
        P("dp", "tensor"),
        P("tensor", "dp"),
        P("dp", "tensor"),
        P("dp", "tensor"),
        P("dp", "tensor"),
        P("dp", "tensor"),
        P("tensor", "dp"),
        P("dp", "tensor"),
        P("dp"),
        P("dp"),
        P("dp"),
        P("dp"),
        P("dp"),
        P("tensor"),
    )
    out_specs = (
        P("dp", None),
        P("dp", None),
        P("dp", None, "tensor"),
        P("dp", "tensor"),
        P("dp", "tensor"),
        P("dp", "tensor"),
        P("dp", "tensor"),
        P("tensor", "dp"),
        P("dp", "tensor"),
        P("dp", "tensor"),
        P("dp", "tensor"),
        P("dp", "tensor"),
        P("tensor", "dp"),
        P("dp", "tensor"),
        P("dp"),
        P("dp"),
        P("dp"),
        P("dp"),
        P("dp"),
        P("tensor"),
    )
    bound = functools.partial(local, mesh.shape["dp"], mesh.shape["tensor"])
    return jax.shard_map(bound, mesh=mesh, in_specs=in_specs, out_specs=out_specs, check_vma=False)
```

time: 1980 us -> 1020 us (0.52)
  waiting for transfers between devices: 1290 us -> 265 us
  starting transfers between devices: 1.64 us -> 185 us
  matrix products: 360 us -> 191 us
  blocking collectives: 118 us -> 0 us
  Pallas kernels: 0 us -> 109 us
  local copies, waits for them, and re-layouts: 28.8 us -> 127 us
  other arithmetic: 154 us -> 112 us
    reduce_scatter x11 -> x0, waiting for transfers between devices: 681 us -> none  [the longest x1 88.1 us: local(): lax.psum_scatter(grad_textval.astype(jnp.bfloat16), 'dp', scatter_dimensi...]
    all_gather x10 -> x2, waiting for transfers between devices: 355 us -> 0.01 us  [the longest x1 0.01 us: local(): text_set = lax.all_gather(text_shard, 'dp', axis=0, tiled=True)]
    ppermute x0 -> x84, waiting for transfers between devices: none -> 265 us  [the longest x4 56.1 us: swap_start(): return (own, [lax.ppermute(o, 'tensor', flip_perm(size, 1)) for o in own])]
    psum x3 -> x0, waiting for transfers between devices: 234 us -> none  [the longest x1 83.1 us: local(): lax.psum(jnp.dot(mixed_heads, full_output, preferred_element_type=jnp.flo...]
    ppermute x0 -> x84, starting transfers between devices: none -> 185 us  [the longest x21 123 us: line_start(): pieces.append(lax.ppermute(piece, 'dp', perm))]
    dot_general x41 -> x28, matrix products: 360 us -> 191 us  [the longest x7 33.4 us: core_away(): jnp.einsum('rm,rc->mc', parts[1], right, preferred_element_type=jnp.float32)]
    pallas_call x0 -> x3, Pallas kernels: none -> 109 us  [the longest x2 74 us: attend_back_pairs(): pl.pallas_call(functools.partial(attend_back_kernel, half, min(512, rows)...]
    unnamed x2 -> x0, blocking collectives: 68.6 us -> none
  transfers between devices with their start and end apart: 25 -> 86, of which waited for: 22 -> 37; matrix products, arithmetic and copies ran while one was open for 16% -> 31% of each run, Pallas kernels for 0% -> 7%
where the time goes in v1:
time: 1020 us; the launch traced here: 1010 us
  waiting for transfers between devices  265 us (26%)
  matrix products  191 us (19%)
  starting transfers between devices  185 us (18%)
  local copies, waits for them, and re-layouts  127 us (12%)
  other arithmetic  112 us (11%)
  Pallas kernels  109 us (11%)
  between operations  17.6 us (2%)
    ppermute x21, starting transfers between devices, line_start(): pieces.append(lax.ppermute(piece, 'dp', perm))  123 us
    pallas_call x2, Pallas kernels, attend_back_pairs(): pl.pallas_call(functools.partial(attend_back_kernel, half, min(512, rows)...  74 us
    ppermute x4, waiting for transfers between devices, swap_start(): return (own, [lax.ppermute(o, 'tensor', flip_perm(size, 1)) for o in own])  56.1 us
    ppermute x7, waiting for transfers between devices, side_start(): return (kept, lax.ppermute(away, 'dp', flip_perm(size, 2)))  56 us
    pallas_call x1, Pallas kernels, attend_pairs(): pl.pallas_call(functools.partial(attend_kernel, half, min(256, rows)), gr...  34.8 us
    dot_general x7, matrix products, core_away(): jnp.einsum('rm,rc->mc', parts[1], right, preferred_element_type=jnp.float32)  33.4 us
    ppermute x8, waiting for transfers between devices, small_scatter(): came = lax.ppermute(jnp.where(upper, low, high), name, flip_perm(size, bit))  29.9 us
    ppermute x3, waiting for transfers between devices, ring_gather(): fwd = lax.ppermute(fwd, 'dp', ahead)  29.5 us
  transfers between devices with their start and end apart: 86, of which 37 were waited for; matrix products, arithmetic and copies ran while one was open for 31% of the time, Pallas kernels for 7%

profile of v1, /device:TPU:0, one launch (start us, length us, event | category | flops | bytes accessed | tf_op | source)
XLA Modules:
  0.0 1007.4 jit_solution(4066111224512745830)
XLA Ops:
  57.5 24.1 %collective-permute-done.4 = f32[8,3072]{1,0:T(8,128)S(1)} collective-permute-done((f32[8,3072]{1,0:T(8,128)S(1)}, f32[8,3072]{1,0:T(8,128)S(1)}, u32[]{:S(2)}, u32[]{:S(2)}) %collective-permute-start.4) | collective-permute-done | bytes 98336 | tf_op jit(solution)/shard_map/ppermute | solution.py:529
  108.7 20.5 %collective-permute-done.14 = bf16[96,3072]{1,0:T(8,128)(2,1)S(1)} collective-permute-done((bf16[96,3072]{1,0:T(8,128)(2,1)}, bf16[96,3072]{1,0:T(8,128)(2,1)S(1)}, u32[]{:S(2)}, u32[]{:S(2)}) %collective-permute-start.14) | collective-permute-done | bytes 589856 | tf_op jit(solution)/shard_map/ppermute | solution.py:427
  172.6 13.0 %fusion.24.raw_ref = f32[1024,2304]{1,0:T(8,128)} fusion(bf16[1024,1536]{1,0:T(8,128)(2,1)S(1)} %fusion.8, bf16[1536,3072]{1,0:T(8,128)(2,1)} %bitcast.20), kind=kOutput, calls=%fused_computation.53 | convolution fusion | flops 7247757312 | bytes 19660800 | tf_op jit(solution)/shard_map/dot_general | solution.py:677
  195.6 34.8 %attend_fwd.1 = (bf16[1024,768]{1,0:T(8,128)(2,1)S(1)}, bf16[1024,2304]{1,0:T(8,128)(2,1)}, bf16[256,1536]{1,0:T(8,128)(2,1)S(1)}, f32[1024,768]{1,0:T(8,128)}, ...) custom-call(s32[1]{0:T(128)S(6)} %copy.138.len_ref, f32[1024,2304]{1,0:T(8,128)} %fusion.24.raw_ref, ...), custom_call_target="tpu_custom_call" | custom-call | tf_op jit(solution)/shard_map/attend_fwd/pallas_call | solution.py:158
  258.1 12.3 %fusion.29 = f32[1024,2048]{1,0:T(8,128)} fusion(bf16[1024,1536]{1,0:T(8,128)(2,1)} %fusion.16, bf16[1536,6144]{1,0:T(8,128)(2,1)} %all-gather.5.cloned.1.call-done), kind=kOutput, calls=%fused_computation.58 | convolution fusion | flops 6442450944 | bytes 17825792 | tf_op jit(solution)/shard_map/dot_general | solution.py:696
  270.4 37.3 %collective-permute-done.26 = bf16[1024,1536]{1,0:T(8,128)(2,1)} collective-permute-done((bf16[1024,1536]{1,0:T(8,128)(2,1)}, bf16[1024,1536]{1,0:T(8,128)(2,1)}, u32[]{:S(2)}, u32[]{:S(2)}) %collective-permute-start.26) | collective-permute-done | bytes 3145760 | tf_op jit(solution)/shard_map/ppermute | solution.py:500
  314.9 11.9 %fusion.18 = f32[1024,2048]{1,0:T(8,128)} fusion(bf16[1024,1536]{1,0:T(8,128)(2,1)S(1)} %multiply_convert_fusion.4, bf16[1536,6144]{1,0:T(8,128)(2,1)} %all-gather.5.cloned.1.call-done), kind=kOutput, calls=%fused_computation.44 | convolution fusion | flops 6442450944 | bytes 17825792 | tf_op jit(solution)/shard_map/dot_general | solution.py:705
  326.9 18.4 %multiply_convert_fusion.1 = (bf16[1024,2048]{1,0:T(8,128)(2,1)}, bf16[1024,2048]{1,0:T(8,128)(2,1)}, bf16[1024,2048]{1,0:T(8,128)(2,1)}) fusion(f32[1024,2048]{1,0:T(8,128)} %fusion.29, f32[1024,2048]{1,0:T(8,128)} %fusion.18, bf16[1024,1536]{1,0:T(8,128)(2,1)S(1)} %multiply_convert_fusion.4, bf16[1536,6144]{1,0:T(8,128)(2,1)} %all-gather.5.cloned.1.call-done), kind=kOutput, calls=%fused_computation.15 | convolution fusion | flops 6473908224 | bytes 38797312 | tf_op jit(solution)/shard_map/dot_general | solution.py:704
  345.3 20.3 %fusion.34 = bf16[1024,1536]{1,0:T(8,128)(2,1)} fusion(bf16[1536,6144]{1,0:T(8,128)(2,1)} %all-gather.5.cloned.1.call-done, bf16[1024,2048]{1,0:T(8,128)(2,1)} %get-tuple-element.244, bf16[1024,2048]{1,0:T(8,128)(2,1)} %get-tuple-element.243), kind=kOutput, calls=%fused_computation.63 | convolution fusion | flops 12903251968 | bytes 24117248 | tf_op jit(solution)/shard_map/rf,df->rd/dot_general | solution.py:712
  381.4 12.1 %convolution_convert_fusion = bf16[768,4096]{1,0:T(8,128)(2,1)} fusion(bf16[1024,768]{0,1:T(8,128)(2,1)S(1)} %bitcast.282, bf16[1024,4096]{1,0:T(8,128)(2,1)} %pad_maximum_fusion), kind=kOutput, calls=%fused_computation.19 | convolution fusion | flops 6445596672 | bytes 16252928 | tf_op jit(solution)/shard_map/rm,rc->mc/dot_general | solution.py:454
  406.8 11.2 %fusion.84 = f32[768,4096]{1,0:T(8,128)} fusion(bf16[1024,768]{0,1:T(8,128)(2,1)} %bitcast.279, bf16[1024,2048]{1,0:T(8,128)(2,1)S(1)} %copy-done.31, bf16[1024,2048]{1,0:T(8,128)(2,1)S(1)} %copy-done.30), kind=kOutput, calls=%fused_computation.294 | convolution fusion | flops 6459228160 | bytes 22544384 | tf_op jit(solution)/shard_map/rm,rc->mc/dot_general | solution.py:460
  418.0 11.6 %fusion.37 = bf16[1024,1536]{1,0:T(8,128)(2,1)} fusion(bf16[1024,2048]{1,0:T(8,128)(2,1)} %get-tuple-element.100, bf16[1536,6144]{1,0:T(8,128)(2,1)} %all-gather.5.cloned.1.call-done), kind=kOutput, calls=%fused_computation.64 | convolution fusion | flops 6444023808 | bytes 13631488 | tf_op jit(solution)/shard_map/rf,df->rd/dot_general | solution.py:720
  435.7 11.4 %add_convert_fusion = bf16[768,4096]{1,0:T(8,128)(2,1)} fusion(f32[768,4096]{1,0:T(8,128)} %fusion.84, bf16[768,4096]{1,0:T(8,128)(2,1)} %collective-permute-done.29), kind=kLoop, calls=%fused_computation | loop fusion | flops 9437184 | bytes 25165824 | tf_op jit(solution)/shard_map/convert_element_type | solution.py:461
  453.5 18.9 %collective-permute-done.28 = bf16[1024,1536]{1,0:T(8,128)(2,1)} collective-permute-done((bf16[1024,1536]{1,0:T(8,128)(2,1)}, bf16[1024,1536]{1,0:T(8,128)(2,1)}, u32[]{:S(2)}, u32[]{:S(2)}) %collective-permute-start.28) | collective-permute-done | bytes 3145760 | tf_op jit(solution)/shard_map/ppermute | solution.py:500
  508.0 36.9 %attend_bwd.2 = (bf16[1024,1152]{1,0:T(8,128)(2,1)}, bf16[256,768]{1,0:T(8,128)(2,1)S(1)}, f32[8,384]{1,0:T(8,128)S(1)}) custom-call(s32[1]{0:T(128)S(6)} %copy.138.len_ref, bf16[1024,2304]{1,0:T(8,128)(2,1)} %get-tuple-element.102.qkv_ref, bf16[256,1536]{1,0:T(8,128)(2,1)S(1)} %get-tuple-element.103.tkv_ref, f32[1024,2304]{1,0:T(8,128)} %fusion.24.raw_ref, ...), custom_call_target="tpu_custom_call" | custom-call | tf_op jit(solution)/shard_map/attend_bwd/pallas_call | solution.py:349
  582.1 37.2 %attend_bwd.3 = (bf16[1024,1152]{1,0:T(8,128)(2,1)}, bf16[256,768]{1,0:T(8,128)(2,1)S(1)}, f32[8,384]{1,0:T(8,128)S(1)}) custom-call(s32[1]{0:T(128)S(6)} %copy.138.len_ref, bf16[1024,2304]{1,0:T(8,128)(2,1)} %get-tuple-element.102.qkv_ref, bf16[256,1536]{1,0:T(8,128)(2,1)S(1)} %get-tuple-element.103.tkv_ref, f32[1024,2304]{1,0:T(8,128)} %fusion.24.raw_ref, ...), custom_call_target="tpu_custom_call" | custom-call | tf_op jit(solution)/shard_map/attend_bwd/pallas_call | solution.py:349
  619.3 11.8 %fusion.40 = bf16[1024,1536]{1,0:T(8,128)(2,1)} fusion(bf16[1536,3072]{1,0:T(8,128)(2,1)} %bitcast.20, bf16[1024,1152]{1,0:T(8,128)(2,1)} %get-tuple-element.125, bf16[1024,1152]{1,0:T(8,128)(2,1)S(1)} %copy-done.97), kind=kOutput, calls=%fused_computation.65 | convolution fusion | flops 7258767360 | bytes 14942208 | tf_op jit(solution)/shard_map/rc,dc->rd/dot_general | solution.py:766
  654.7 19.9 %collective-permute-done.81 = f32[12]{0:T(128)S(1)} collective-permute-done((f32[12]{0:T(128)S(1)}, f32[12]{0:T(128)S(1)}, u32[]{:S(2)}, u32[]{:S(2)}) %collective-permute-start.81) | collective-permute-done | bytes 80 | tf_op jit(solution)/shard_map/ppermute | solution.py:538
  700.6 13.6 %collective-permute-done.37 = bf16[4,96,1152]{2,1,0:T(8,128)(2,1)S(1)} collective-permute-done((bf16[4,96,1152]{2,1,0:T(8,128)(2,1)S(1)}, bf16[4,96,1152]{2,1,0:T(8,128)(2,1)S(1)}, u32[]{:S(2)}, u32[]{:S(2)}) %collective-permute-start.37) | collective-permute-done | bytes 884768 | tf_op jit(solution)/shard_map/ppermute | solution.py:471
  731.1 21.3 %collective-permute-start.44 = (bf16[96,768]{1,0:T(8,128)(2,1)S(1)}, bf16[96,768]{1,0:T(8,128)(2,1)S(1)}, u32[]{:S(2)}, u32[]{:S(2)}) collective-permute-start(bf16[96,768]{1,0:T(8,128)(2,1)S(1)} %copy-done.66), channel_id=1, source_target_pairs={{0,8},{2,10},{4,12},{6,14},{8,16},{10,18},{12,20},{14,22},{16,24},... | collective-permute-start | bytes 442376 | tf_op jit(solution)/shard_map/ppermute | solution.py:485
  753.5 20.5 %collective-permute-start.45 = (bf16[96,768]{1,0:T(8,128)(2,1)S(1)}, bf16[96,768]{1,0:T(8,128)(2,1)S(1)}, u32[]{:S(2)}, u32[]{:S(2)}) collective-permute-start(bf16[96,768]{1,0:T(8,128)(2,1)S(1)} %copy-done.65), channel_id=1, source_target_pairs={{0,16},{2,18},{4,20},{6,22},{8,24},{10,26},{12,28},{14,30},{16,0},... | collective-permute-start | bytes 442376 | tf_op jit(solution)/shard_map/ppermute | solution.py:485
  774.2 20.2 %collective-permute-start.46 = (bf16[96,768]{1,0:T(8,128)(2,1)S(1)}, bf16[96,768]{1,0:T(8,128)(2,1)S(1)}, u32[]{:S(2)}, u32[]{:S(2)}) collective-permute-start(bf16[96,768]{1,0:T(8,128)(2,1)S(1)} %copy-done.64), channel_id=1, source_target_pairs={{0,24},{2,26},{4,28},{6,30},{8,0},{10,2},{12,4},{14,6},{16,8},{18,... | collective-permute-start | bytes 442376 | tf_op jit(solution)/shard_map/ppermute | solution.py:485
  805.4 26.0 %collective-permute-done.43 = bf16[4,256,768]{2,1,0:T(8,128)(2,1)S(1)} collective-permute-done((bf16[4,256,768]{2,1,0:T(8,128)(2,1)S(1)}, bf16[4,256,768]{2,1,0:T(8,128)(2,1)S(1)}, u32[]{:S(2)}, u32[]{:S(2)}) %collective-permute-start.43) | collective-permute-done | bytes 1572896 | tf_op jit(solution)/shard_map/ppermute | solution.py:471
  889.7 16.0 %collective-permute-start.71 = (bf16[256,768]{1,0:T(8,128)(2,1)}, bf16[256,768]{1,0:T(8,128)(2,1)}, u32[]{:S(2)}, u32[]{:S(2)}) collective-permute-start(bf16[256,768]{1,0:T(8,128)(2,1)} %get-tuple-element.278), channel_id=1, source_target_pairs={{0,24},{2,26},{4,28},{6,30},{8,0},{10,2},{12,4},{14,6},{16,8},{18,... | collective-permute-start | bytes 1179656 | tf_op jit(solution)/shard_map/ppermute | solution.py:485
  (593 shorter events, 508.8 us)
Async XLA Ops:
  7.3 178.3 %all-gather.3.cloned.1.call-start = ((), (), s32[]{:S(2)}) async-start(), calls=%async_computation | async-start | bytes 13369344 | tf_op jit(solution)/shard_map/all_gather | solution.py:623
  10.8 247.2 %all-gather.5.cloned.1.call-start = ((), (), s32[]{:S(2)}) async-start(), calls=%async_computation.1 | async-start | bytes 20054016 | tf_op jit(solution)/shard_map/all_gather | solution.py:642
  39.3 65.4 %collective-permute-start.9 = (bf16[96,3072]{1,0:T(8,128)(2,1)}, bf16[96,3072]{1,0:T(8,128)(2,1)}, u32[]{:S(2)}, u32[]{:S(2)}) collective-permute-start(bf16[96,3072]{1,0:T(8,128)(2,1)} %pad_maximum_fusion.7), channel_id=1, source_target_pairs={{0,2},{2,0},{4,6},{6,4},{8,10},{10,8},{12,14},{14,12},{16,18},{18,... | collective-permute-start | bytes 1769480 | tf_op jit(solution)/shard_map/ppermute | solution.py:437
  39.3 63.1 %collective-permute-start.10 = (bf16[96,3072]{1,0:T(8,128)(2,1)}, bf16[96,3072]{1,0:T(8,128)(2,1)}, u32[]{:S(2)}, u32[]{:S(2)}) collective-permute-start(bf16[96,3072]{1,0:T(8,128)(2,1)} %pad_maximum_fusion.7), channel_id=1, source_target_pairs={{0,8},{2,10},{8,16},{10,18},{16,24},{18,26},{24,28},{26,30},{28,20... | collective-permute-start | bytes 1769480 | tf_op jit(solution)/shard_map/ppermute | solution.py:427
  41.0 61.7 %collective-permute-start.12 = (bf16[96,3072]{1,0:T(8,128)(2,1)}, bf16[96,3072]{1,0:T(8,128)(2,1)}, u32[]{:S(2)}, u32[]{:S(2)}) collective-permute-start(bf16[96,3072]{1,0:T(8,128)(2,1)} %pad_maximum_fusion.7), channel_id=1, source_target_pairs={{0,4},{2,6},{8,0},{10,2},{16,8},{18,10},{24,16},{26,18},{28,24},{3... | collective-permute-start | bytes 1769480 | tf_op jit(solution)/shard_map/ppermute | solution.py:428
  236.8 70.9 %collective-permute-start.26 = (bf16[1024,1536]{1,0:T(8,128)(2,1)}, bf16[1024,1536]{1,0:T(8,128)(2,1)}, u32[]{:S(2)}, u32[]{:S(2)}) collective-permute-start(bf16[1024,1536]{1,0:T(8,128)(2,1)} %convolution_convert_fusion.1), channel_id=1, source_target_pairs={{0,1},{1,0},{2,3},{3,2},{4,5},{5,4},{6,7},{7,6},{8,9},{9,8},{10,11... | collective-permute-start | bytes 9437192 | tf_op jit(solution)/shard_map/ppermute | solution.py:500
  393.5 42.2 %collective-permute-start.29 = (bf16[768,4096]{1,0:T(8,128)(2,1)}, bf16[768,4096]{1,0:T(8,128)(2,1)}, u32[]{:S(2)}, u32[]{:S(2)}) collective-permute-start(bf16[768,4096]{1,0:T(8,128)(2,1)} %convolution_convert_fusion), channel_id=1, source_target_pairs={{0,2},{2,0},{4,6},{6,4},{8,10},{10,8},{12,14},{14,12},{16,18},{18,... | collective-permute-start | bytes 18874376 | tf_op jit(solution)/shard_map/ppermute | solution.py:456
  401.9 70.4 %collective-permute-start.28 = (bf16[1024,1536]{1,0:T(8,128)(2,1)}, bf16[1024,1536]{1,0:T(8,128)(2,1)}, u32[]{:S(2)}, u32[]{:S(2)}) collective-permute-start(bf16[1024,1536]{1,0:T(8,128)(2,1)} %fusion.34), channel_id=1, source_target_pairs={{0,1},{1,0},{2,3},{3,2},{4,5},{5,4},{6,7},{7,6},{8,9},{9,8},{10,11... | collective-permute-start | bytes 9437192 | tf_op jit(solution)/shard_map/ppermute | solution.py:500
  434.7 67.3 %collective-permute-start.32 = (bf16[4,96,2048]{2,1,0:T(8,128)(2,1)}, bf16[4,96,2048]{2,1,0:T(8,128)(2,1)}, u32[]{:S(2)}, u32[]{:S(2)}) collective-permute-start(bf16[4,96,2048]{2,1,0:T(8,128)(2,1)} %get-tuple-element.258), channel_id=1, source_target_pairs={{0,4},{2,6},{4,0},{6,2},{8,12},{10,14},{12,8},{14,10},{16,20},{18,... | collective-permute-start | bytes 4718600 | tf_op jit(solution)/shard_map/ppermute | solution.py:471
  483.6 69.7 %collective-permute-start.33 = (bf16[4,96,4096]{2,1,0:T(8,128)(2,1)}, bf16[4,96,4096]{2,1,0:T(8,128)(2,1)}, u32[]{:S(2)}, u32[]{:S(2)}) collective-permute-start(bf16[4,96,4096]{2,1,0:T(8,128)(2,1)} %get-tuple-element.248), channel_id=1, source_target_pairs={{0,4},{2,6},{4,0},{6,2},{8,12},{10,14},{12,8},{14,10},{16,20},{18,... | collective-permute-start | bytes 9437192 | tf_op jit(solution)/shard_map/ppermute | solution.py:471
  633.8 56.3 %collective-permute-start.39 = (bf16[2048,768]{1,0:T(8,128)(2,1)}, bf16[2048,768]{1,0:T(8,128)(2,1)}, u32[]{:S(2)}, u32[]{:S(2)}) collective-permute-start(bf16[2048,768]{1,0:T(8,128)(2,1)} %convolution_convert_fusion.2), channel_id=1, source_target_pairs={{0,2},{2,0},{4,6},{6,4},{8,10},{10,8},{12,14},{14,12},{16,18},{18,... | collective-permute-start | bytes 9437192 | tf_op jit(solution)/shard_map/ppermute | solution.py:456
  636.2 47.4 %collective-permute-start.75 = (f32[3,64]{1,0:T(4,128)S(1)}, f32[3,64]{1,0:T(4,128)S(1)}, u32[]{:S(2)}, u32[]{:S(2)}) collective-permute-start(f32[3,64]{1,0:T(4,128)S(1)} %reduce_sum.104), channel_id=1, source_target_pairs={{0,1},{1,0},{2,3},{3,2},{4,5},{5,4},{6,7},{7,6},{8,9},{9,8},{10,11... | collective-permute-start | bytes 2312 | tf_op jit(solution)/shard_map/ppermute | solution.py:538
  637.7 49.1 %collective-permute-start.40 = (bf16[4,256,768]{2,1,0:T(8,128)(2,1)}, bf16[4,256,768]{2,1,0:T(8,128)(2,1)}, u32[]{:S(2)}, u32[]{:S(2)}) collective-permute-start(bf16[4,256,768]{2,1,0:T(8,128)(2,1)} %get-tuple-element.256), channel_id=1, source_target_pairs={{0,4},{2,6},{4,0},{6,2},{8,12},{10,14},{12,8},{14,10},{16,20},{18,... | collective-permute-start | bytes 4718600 | tf_op jit(solution)/shard_map/ppermute | solution.py:471
  643.8 51.9 %collective-permute-start.38 = (bf16[768,1152]{1,0:T(8,128)(2,1)}, bf16[768,1152]{1,0:T(8,128)(2,1)}, u32[]{:S(2)}, u32[]{:S(2)}) collective-permute-start(bf16[768,1152]{1,0:T(8,128)(2,1)} %convolution_convert_fusion.3), channel_id=1, source_target_pairs={{0,2},{2,0},{4,6},{6,4},{8,10},{10,8},{12,14},{14,12},{16,18},{18,... | collective-permute-start | bytes 5308424 | tf_op jit(solution)/shard_map/ppermute | solution.py:456
  682.6 116.3 %collective-permute-start.27 = (bf16[1024,1536]{1,0:T(8,128)(2,1)}, bf16[1024,1536]{1,0:T(8,128)(2,1)}, u32[]{:S(2)}, u32[]{:S(2)}) collective-permute-start(bf16[1024,1536]{1,0:T(8,128)(2,1)} %fusion.37), channel_id=1, source_target_pairs={{0,1},{1,0},{2,3},{3,2},{4,5},{5,4},{6,7},{7,6},{8,9},{9,8},{10,11... | collective-permute-start | bytes 9437192 | tf_op jit(solution)/shard_map/ppermute | solution.py:500
  690.1 41.0 %collective-permute-start.52 = (bf16[96,2048]{1,0:T(8,128)(2,1)S(1)}, bf16[96,2048]{1,0:T(8,128)(2,1)S(1)}, u32[]{:S(2)}, u32[]{:S(2)}) collective-permute-start(bf16[96,2048]{1,0:T(8,128)(2,1)S(1)} %copy-done.59), channel_id=1, source_target_pairs={{0,24},{2,26},{4,28},{6,30},{8,0},{10,2},{12,4},{14,6},{16,8},{18,... | collective-permute-start | bytes 1179656 | tf_op jit(solution)/shard_map/ppermute | solution.py:485
  715.8 58.4 %collective-permute-start.48 = (bf16[96,4096]{1,0:T(8,128)(2,1)S(1)}, bf16[96,4096]{1,0:T(8,128)(2,1)S(1)}, u32[]{:S(2)}, u32[]{:S(2)}) collective-permute-start(bf16[96,4096]{1,0:T(8,128)(2,1)S(1)} %copy-done.46), channel_id=1, source_target_pairs={{0,16},{2,18},{4,20},{6,22},{8,24},{10,26},{12,28},{14,30},{16,0},... | collective-permute-start | bytes 2359304 | tf_op jit(solution)/shard_map/ppermute | solution.py:485
  717.2 77.2 %collective-permute-start.49 = (bf16[96,4096]{1,0:T(8,128)(2,1)S(1)}, bf16[96,4096]{1,0:T(8,128)(2,1)S(1)}, u32[]{:S(2)}, u32[]{:S(2)}) collective-permute-start(bf16[96,4096]{1,0:T(8,128)(2,1)S(1)} %copy-done.45), channel_id=1, source_target_pairs={{0,24},{2,26},{4,28},{6,30},{8,0},{10,2},{12,4},{14,6},{16,8},{18,... | collective-permute-start | bytes 2359304 | tf_op jit(solution)/shard_map/ppermute | solution.py:485
  731.1 65.5 %collective-permute-start.44 = (bf16[96,768]{1,0:T(8,128)(2,1)S(1)}, bf16[96,768]{1,0:T(8,128)(2,1)S(1)}, u32[]{:S(2)}, u32[]{:S(2)}) collective-permute-start(bf16[96,768]{1,0:T(8,128)(2,1)S(1)} %copy-done.66), channel_id=1, source_target_pairs={{0,8},{2,10},{4,12},{6,14},{8,16},{10,18},{12,20},{14,22},{16,24},... | collective-permute-start | bytes 442376 | tf_op jit(solution)/shard_map/ppermute | solution.py:485
  753.5 44.7 %collective-permute-start.45 = (bf16[96,768]{1,0:T(8,128)(2,1)S(1)}, bf16[96,768]{1,0:T(8,128)(2,1)S(1)}, u32[]{:S(2)}, u32[]{:S(2)}) collective-permute-start(bf16[96,768]{1,0:T(8,128)(2,1)S(1)} %copy-done.65), channel_id=1, source_target_pairs={{0,16},{2,18},{4,20},{6,22},{8,24},{10,26},{12,28},{14,30},{16,0},... | collective-permute-start | bytes 442376 | tf_op jit(solution)/shard_map/ppermute | solution.py:485
  796.6 110.0 %collective-permute-start.41 = (bf16[1024,1536]{1,0:T(8,128)(2,1)S(1)}, bf16[1024,1536]{1,0:T(8,128)(2,1)S(1)}, u32[]{:S(2)}, u32[]{:S(2)}) collective-permute-start(bf16[1024,1536]{1,0:T(8,128)(2,1)S(1)} %copy-done.20), channel_id=1, source_target_pairs={{0,1},{1,0},{2,3},{3,2},{4,5},{5,4},{6,7},{7,6},{8,9},{9,8},{10,11... | collective-permute-start | bytes 9437192 | tf_op jit(solution)/shard_map/ppermute | solution.py:500
  798.2 66.3 %collective-permute-start.42 = (bf16[4,96,1152]{2,1,0:T(8,128)(2,1)S(1)}, bf16[4,96,1152]{2,1,0:T(8,128)(2,1)S(1)}, u32[]{:S(2)}, u32[]{:S(2)}) collective-permute-start(bf16[4,96,1152]{2,1,0:T(8,128)(2,1)S(1)} %get-tuple-element.270), channel_id=1, source_target_pairs={{0,4},{2,6},{4,0},{6,2},{8,12},{10,14},{12,8},{14,10},{16,20},{18,... | collective-permute-start | bytes 2654216 | tf_op jit(solution)/shard_map/ppermute | solution.py:471
  845.9 73.5 %collective-permute-start.69 = (bf16[256,768]{1,0:T(8,128)(2,1)}, bf16[256,768]{1,0:T(8,128)(2,1)}, u32[]{:S(2)}, u32[]{:S(2)}) collective-permute-start(bf16[256,768]{1,0:T(8,128)(2,1)} %get-tuple-element.280), channel_id=1, source_target_pairs={{0,8},{2,10},{4,12},{6,14},{8,16},{10,18},{12,20},{14,22},{16,24},... | collective-permute-start | bytes 1179656 | tf_op jit(solution)/shard_map/ppermute | solution.py:485
  924.9 42.8 %collective-permute-start.54 = (bf16[1,3072]{1,0:T(2,128)(2,1)}, bf16[1,3072]{1,0:T(2,128)(2,1)}, u32[]{:S(2)}, u32[]{:S(2)}) collective-permute-start(bf16[1,3072]{1,0:T(2,128)(2,1)} %convert.21), channel_id=1, source_target_pairs={{0,2},{2,0},{4,6},{6,4},{8,10},{10,8},{12,14},{14,12},{16,18},{18,... | collective-permute-start | bytes 18440 | tf_op jit(solution)/shard_map/ppermute | solution.py:514
  (166 other events, 3842.6 us)
Sparse Core Ops, SparseCore 0:
  11.0 128.0 all-gather.2
  140.6 108.4 all-gather.4

commit v2 on v1

v2 whole, which is shorter than its diff:
```python
import functools
import math

import jax
import jax.numpy as jnp
from jax import lax
from jax.experimental import pallas as pl
from jax.experimental.pallas import tpu as pltpu
from jax.sharding import PartitionSpec as P

EPSILON = 1e-06


def inv_rms(values):
    return lax.rsqrt(jnp.mean(values * values, axis=-1, keepdims=True) + EPSILON)


def time_embed(step_vals, embed_width):
    half_width = embed_width // 2
    frequency = jnp.exp(-math.log(10000.0) * jnp.arange(half_width, dtype=jnp.float32) / half_width)
    phases = step_vals.astype(jnp.float32)[:, None] * frequency
    return jnp.concatenate([jnp.cos(phases), jnp.sin(phases)], axis=1)


def norm_back(grad_hat, normed, factor):
    return factor * (grad_hat - normed * jnp.mean(grad_hat * normed, axis=-1, keepdims=True))


LANES = 128
LIGHT = pl.CostEstimate(flops=1, transcendentals=0, bytes_accessed=1)


def lane_ids(rows):
    return lax.broadcasted_iota(jnp.int32, (rows, LANES), 1)


def pair_matrix(same, half):
    row = lax.broadcasted_iota(jnp.int32, (LANES, LANES), 0) // half
    col = lax.broadcasted_iota(jnp.int32, (LANES, LANES), 1) // half
    return jnp.where((row == col) == same, 1.0, 0.0).astype(jnp.bfloat16)


def head_sums(values, matrix):
    high = values.astype(jnp.bfloat16)
    low = (values - high.astype(jnp.float32)).astype(jnp.bfloat16)
    return jnp.dot(high, matrix, preferred_element_type=jnp.float32) + jnp.dot(
        low, matrix, preferred_element_type=jnp.float32
    )


def swap_quarters(values, half):
    rows = values.shape[0]
    first = lane_ids(rows) % half < half // 2
    return jnp.where(
        first,
        pltpu.roll(values, LANES - half // 2, 1),
        pltpu.roll(values, half // 2, 1),
    )


def nt_dot(left, right):
    return lax.dot_general(
        left, right, (((1,), (1,)), ((), ())), preferred_element_type=jnp.float32
    )


def tn_dot(left, right):
    return lax.dot_general(
        left, right, (((0,), (0,)), ((), ())), preferred_element_type=jnp.float32
    )


def attend_kernel(half, block, fresh, *refs):
    f32, bf16 = jnp.float32, jnp.bfloat16
    matrix = pair_matrix(True, half)
    if fresh:
        len_ref, rawq_ref, rawk_ref, rawv_ref, text_ref, tval_ref = refs[:6]
        cos_ref, sin_ref, cosk_ref, sink_ref, gain_ref, tanh_ref = refs[6:12]
        mixed_ref, query_ref, own_ref, cross_ref, lse_ref, kv_ref, tkv_ref = refs[12:]
    else:
        len_ref, rawq_ref, kv_ref, tkv_ref, cos_ref, sin_ref, gain_ref, tanh_ref = refs[:8]
        mixed_ref, query_ref, own_ref, cross_ref, lse_ref = refs[12:]

    def hat(raw):
        return raw * lax.rsqrt(head_sums(raw * raw, matrix) * (1.0 / half) + EPSILON)

    def turned(raw, gain, cosine, sine):
        value = hat(raw) * gain
        return (value * cosine + swap_quarters(value, half) * sine).astype(bf16)

    query_ref[...] = turned(rawq_ref[...], gain_ref[0:1], cos_ref[...], sin_ref[...])
    if fresh:
        kv_ref[:, :LANES] = turned(rawk_ref[...], gain_ref[1:2], cosk_ref[...], sink_ref[...])
        kv_ref[:, LANES:] = rawv_ref[...].astype(bf16)
        tkv_ref[:, :LANES] = (hat(text_ref[...]) * gain_ref[2:3]).astype(bf16)
        tkv_ref[:, LANES:] = tval_ref[...].astype(bf16)
    key, value = kv_ref[:, :LANES], kv_ref[:, LANES:]
    tkey, tval = tkv_ref[:, :LANES], tkv_ref[:, LANES:]
    one = jnp.ones((), bf16)
    zero = jnp.zeros((), bf16)

    def pick(a, b):
        return jnp.where(lane_ids(a.shape[0]) < half, a, b)

    def fill(a, fillers, first):
        other = jnp.full(a.shape, fillers, bf16)
        return pick(a, other) if first else pick(other, a)

    value_ones = [fill(value, one, True), fill(value, one, False)]
    tval_ones = [fill(tval, one, True), fill(tval, one, False)]
    keep = lax.broadcasted_iota(jnp.int32, (block, tkey.shape[0]), 1) < len_ref[0]

    def step(i, _):
        here = pl.ds(pl.multiple_of(i * block, block), block)
        q_blk = query_ref[here, :] * jnp.asarray(half**-0.5, bf16)
        outs = []
        texts = []
        for head in range(2):
            q_one = fill(q_blk, zero, head == 0)
            e_self = jnp.exp(nt_dot(q_one, key)).astype(bf16)
            outs.append(jnp.dot(e_self, value_ones[head], preferred_element_type=f32))
            e_text = jnp.where(keep, jnp.exp(nt_dot(q_one, tkey)), 0.0).astype(bf16)
            texts.append(jnp.dot(e_text, tval_ones[head], preferred_element_type=f32))
        for n, (a, b) in enumerate((outs, texts)):
            total = pick(b, a)
            lse_ref[here, n * LANES : (n + 1) * LANES] = jnp.log(total)
            res = pick(a, b) / pltpu.roll(total, half, 1)
            if n == 0:
                own = res
                own_ref[here, :] = res
            else:
                cross_ref[here, :] = res
                mixed_ref[here, :] = (own + tanh_ref[0:1] * res).astype(bf16)
        return 0

    lax.fori_loop(0, query_ref.shape[0] // block, step, 0)


def attend_rows(part, cap_len, raw, text, tables, half, kept=None):
    cosine, sine, gains, tanh_lanes = tables
    rows, caps = raw.shape[0], text.shape[0]
    count = rows // 2
    width = raw.shape[1] // 3
    f32, bf16 = jnp.float32, jnp.bfloat16
    fresh = kept is None

    def piece(scale, shift, wide=1):
        return pl.BlockSpec((count, wide * LANES), lambda p: (part, scale * p + shift))

    table = pl.BlockSpec((count, LANES), lambda p: (part, 0))
    whole = pl.BlockSpec(memory_space=pl.ANY)
    smem = pl.BlockSpec(memory_space=pltpu.SMEM)
    kv_block = pl.BlockSpec((rows, 2 * LANES), lambda p: (0, p))
    tkv_block = pl.BlockSpec((caps, 2 * LANES), lambda p: (0, p))
    tail_specs = [fixed_block(8), lane_block(8, 1, 0)]
    out_specs = [
        pl.BlockSpec((count, LANES), lambda p: (0, p)),
        piece(1, 0),
        piece(1, 0),
        piece(1, 0),
        piece(1, 0, 2),
    ]
    out_shape = [
        jax.ShapeDtypeStruct((count, width), bf16),
        jax.ShapeDtypeStruct((rows, width), bf16),
        jax.ShapeDtypeStruct((rows, width), f32),
        jax.ShapeDtypeStruct((rows, width), f32),
        jax.ShapeDtypeStruct((rows, 2 * width), f32),
    ]
    if fresh:
        in_specs = [smem, piece(3, 0), lane_block(rows, 3, 1), lane_block(rows, 3, 2)]
        in_specs += [lane_block(caps, 2, 0), lane_block(caps, 2, 1)]
        in_specs += [table, table, fixed_block(rows), fixed_block(rows)] + tail_specs
        operands = (cap_len, raw, raw, raw, text, text, cosine, sine, cosine, sine)
        operands += (gains, tanh_lanes)
        out_specs += [kv_block, tkv_block]
        out_shape += [
            jax.ShapeDtypeStruct((rows, 2 * width), bf16),
            jax.ShapeDtypeStruct((caps, 2 * width), bf16),
        ]
        aliases = {}
    else:
        query, own, cross, lse, kv, tkv = kept
        in_specs = [smem, piece(3, 0), kv_block, tkv_block, table, table] + tail_specs
        in_specs += [whole] * 4
        operands = (cap_len, raw, kv, tkv, cosine, sine, gains, tanh_lanes)
        operands += (query, own, cross, lse)
        aliases = {8: 1, 9: 2, 10: 3, 11: 4}
    return pl.pallas_call(
        functools.partial(attend_kernel, half, min(256, count), fresh),
        grid=(width // LANES,),
        in_specs=in_specs,
        out_specs=out_specs,
        out_shape=out_shape,
        input_output_aliases=aliases,
        compiler_params=pltpu.CompilerParams(vmem_limit_bytes=50 * 2**20),
        cost_estimate=LIGHT,
        name="attend_fwd",
    )(*operands)


def pick_head(a, b, first, half):
    low = lane_ids(a.shape[0]) < half
    return jnp.where(low, a, b) if first else jnp.where(low, b, a)


def three_parts(value, half):
    spot = lane_ids(value.shape[0]) % half
    high = value.astype(jnp.bfloat16).astype(jnp.float32)
    rest = value - high
    mid = rest.astype(jnp.bfloat16).astype(jnp.float32)
    low = rest - mid
    parts = jnp.where(spot == 0, high, jnp.where(spot == 1, mid, jnp.where(spot == 2, low, 0.0)))
    return parts.astype(jnp.bfloat16)


def with_ones(value, first, half):
    ones = jnp.where(lane_ids(value.shape[0]) % half < 3, 1.0, 0.0).astype(jnp.bfloat16)
    return pick_head(value, ones, first, half)


def only_head(value, first, half):
    return pick_head(value, jnp.zeros(value.shape, jnp.bfloat16), first, half)


def norm_return(grad_in, raw, gain, half, turn):
    same = pair_matrix(True, half)
    inv = lax.rsqrt(head_sums(raw * raw, same) * (1.0 / half) + EPSILON)
    normed = raw * inv
    back = grad_in.astype(jnp.bfloat16).astype(jnp.float32)
    if turn is not None:
        back = back * turn[0][...] - swap_quarters(back, half) * turn[1][...]
    scaled = back * gain
    mean = head_sums(scaled * normed, same) * (1.0 / half)
    stat = jnp.sum(back * normed, axis=0, keepdims=True)
    return (inv * (scaled - normed * mean)).astype(jnp.bfloat16), stat


def score_grads(key_aug, val_aug, q_aug, o_aug, keep):
    probs = jnp.exp(nt_dot(key_aug, q_aug))
    if keep is not None:
        probs = jnp.where(keep, probs, 0.0)
    return probs.astype(jnp.bfloat16), (probs * nt_dot(val_aug, o_aug)).astype(jnp.bfloat16)


def cross_back_kernel(
    half,
    block,
    len_ref,
    query_ref,
    tkv_ref,
    text_ref,
    cross_ref,
    lse_ref,
    dmix_ref,
    gain_ref,
    tanh_ref,
    dq_ref,
    dtext_ref,
    stat_ref,
    qs_ref,
    os_ref,
    dk_ref,
    dv_ref,
):
    f32, bf16 = jnp.float32, jnp.bfloat16
    rows, caps = query_ref.shape[0], tkv_ref.shape[0]
    grad_f = dmix_ref[...].astype(f32)
    other = (grad_f * tanh_ref[0:1]).astype(bf16)
    delta = three_parts(
        -head_sums(other.astype(f32) * cross_ref[...], pair_matrix(False, half)), half
    )
    lse = three_parts(-lse_ref[...], half)
    query = query_ref[...] * jnp.asarray(half**-0.5, bf16)
    tkey, tval = tkv_ref[:, :LANES], tkv_ref[:, LANES:]
    for head in range(2):
        qs_ref[head] = pick_head(query, lse, head == 0, half)
        os_ref[head] = pick_head(other, delta, head == 0, half)
    key_aug = [with_ones(tkey, h == 0, half) for h in range(2)]
    val_aug = [with_ones(tval, h == 0, half) for h in range(2)]
    key_only = [only_head(tkey, h == 0, half) for h in range(2)]
    dk_ref[...] = jnp.zeros_like(dk_ref)
    dv_ref[...] = jnp.zeros_like(dv_ref)
    keep = lax.broadcasted_iota(jnp.int32, (caps, block), 0) < len_ref[0]

    def step(i, _):
        here = pl.ds(pl.multiple_of(i * block, block), block)
        dq = jnp.zeros((block, LANES), f32)
        for head in range(2):
            q_aug, o_aug = qs_ref[head, here], os_ref[head, here]
            probs, grads = score_grads(key_aug[head], val_aug[head], q_aug, o_aug, keep)
            dv_ref[...] += jnp.dot(
                probs, only_head(o_aug, head == 0, half), preferred_element_type=f32
            )
            dk_ref[...] += jnp.dot(
                grads, only_head(q_aug, head == 0, half), preferred_element_type=f32
            )
            dq += tn_dot(grads, key_only[head])
        dq_ref[here, :] = dq * half**-0.5
        return 0

    lax.fori_loop(0, rows // block, step, 0)
    res, stat_t = norm_return(dk_ref[...], text_ref[...], gain_ref[2:3], half, None)
    dtext_ref[:, :LANES] = res
    dtext_ref[:, LANES:] = dv_ref[...].astype(bf16)
    stat_x = jnp.sum(grad_f * cross_ref[...], axis=0, keepdims=True)
    stat_ref[...] = jnp.concatenate([stat_t, stat_x, jnp.zeros((6, LANES), f32)], axis=0)


def self_back_kernel(
    half,
    block,
    query_ref,
    key_ref,
    val_ref,
    rawq_ref,
    rawk_ref,
    own_ref,
    lse_ref,
    dmix_ref,
    dqc_ref,
    cos_ref,
    sin_ref,
    gain_ref,
    dqkv_ref,
    stat_ref,
    qs_ref,
    os_ref,
    dq_ref,
    dk_ref,
    dv_ref,
):
    f32, bf16 = jnp.float32, jnp.bfloat16
    rows = query_ref.shape[0]
    grad = dmix_ref[...]
    delta = three_parts(
        -head_sums(grad.astype(f32) * own_ref[...], pair_matrix(False, half)), half
    )
    lse = three_parts(-lse_ref[...], half)
    query = query_ref[...] * jnp.asarray(half**-0.5, bf16)
    key, value = key_ref[...], val_ref[...]
    for head in range(2):
        qs_ref[head] = pick_head(query, lse, head == 0, half)
        os_ref[head] = pick_head(grad, delta, head == 0, half)
    key_aug = [with_ones(key, h == 0, half) for h in range(2)]
    val_aug = [with_ones(value, h == 0, half) for h in range(2)]
    key_only = [only_head(key, h == 0, half) for h in range(2)]
    dk_ref[...] = jnp.zeros_like(dk_ref)
    dv_ref[...] = jnp.zeros_like(dv_ref)

    def step(i, _):
        here = pl.ds(pl.multiple_of(i * block, block), block)
        dq = jnp.zeros((block, LANES), f32)
        for head in range(2):
            q_aug, o_aug = qs_ref[head, here], os_ref[head, here]
            probs, grads = score_grads(key_aug[head], val_aug[head], q_aug, o_aug, None)
            dv_ref[...] += jnp.dot(
                probs, only_head(o_aug, head == 0, half), preferred_element_type=f32
            )
            dk_ref[...] += jnp.dot(
                grads, only_head(q_aug, head == 0, half), preferred_element_type=f32
            )
            dq += tn_dot(grads, key_only[head])
        dq_ref[here, :] = dqc_ref[here, :] + dq * half**-0.5
        return 0

    lax.fori_loop(0, rows // block, step, 0)
    turn = (cos_ref, sin_ref)
    res, stat_q = norm_return(dq_ref[...], rawq_ref[...], gain_ref[0:1], half, turn)
    dqkv_ref[:, :LANES] = res
    res, stat_k = norm_return(dk_ref[...], rawk_ref[...], gain_ref[1:2], half, turn)
    dqkv_ref[:, LANES : 2 * LANES] = res
    dqkv_ref[:, 2 * LANES :] = dv_ref[...].astype(bf16)
    stat_ref[...] = jnp.concatenate([stat_q, stat_k, jnp.zeros((6, LANES), f32)], axis=0)


def lane_block(rows, scale, shift):
    return pl.BlockSpec((rows, LANES), lambda p: (0, scale * p + shift))


def fixed_block(rows):
    return pl.BlockSpec((rows, LANES), lambda p: (0, 0))


def cross_back(cap_len, query, tkv, text, cross, lse, dmix, tables, half):
    gains, tanh_lanes = tables[2], tables[3]
    rows, caps = query.shape[0], text.shape[0]
    width = dmix.shape[1]
    f32, bf16 = jnp.float32, jnp.bfloat16
    return pl.pallas_call(
        functools.partial(cross_back_kernel, half, min(512, rows)),
        grid=(width // LANES,),
        in_specs=[
            pl.BlockSpec(memory_space=pltpu.SMEM),
            lane_block(rows, 1, 0),
            pl.BlockSpec((caps, 2 * LANES), lambda p: (0, p)),
            lane_block(caps, 2, 0),
            lane_block(rows, 1, 0),
            lane_block(rows, 2, 1),
            lane_block(rows, 1, 0),
            fixed_block(8),
            lane_block(8, 1, 0),
        ],
        out_specs=[
            lane_block(rows, 1, 0),
            pl.BlockSpec((caps, 2 * LANES), lambda p: (0, p)),
            lane_block(8, 1, 0),
        ],
        out_shape=[
            jax.ShapeDtypeStruct((rows, width), f32),
            jax.ShapeDtypeStruct((caps, 2 * width), bf16),
            jax.ShapeDtypeStruct((8, width), f32),
        ],
        scratch_shapes=[pltpu.VMEM((2, rows, LANES), bf16)] * 2
        + [pltpu.VMEM((caps, LANES), f32)] * 2,
        compiler_params=pltpu.CompilerParams(vmem_limit_bytes=40 * 2**20),
        cost_estimate=LIGHT,
        name="cross_bwd",
    )(cap_len, query, tkv, text, cross, lse, dmix, gains, tanh_lanes)


def self_back(window, query, kv, raw, own, lse, dmix, dq_cross, tables, half):
    cosine, sine, gains, _ = tables
    first, pairs = window
    rows = raw.shape[0]
    width = pairs * LANES
    f32, bf16 = jnp.float32, jnp.bfloat16
    return pl.pallas_call(
        functools.partial(self_back_kernel, half, min(512, rows)),
        grid=(pairs,),
        in_specs=[
            lane_block(rows, 1, first),
            lane_block(rows, 2, 2 * first),
            lane_block(rows, 2, 2 * first + 1),
            lane_block(rows, 3, 3 * first),
            lane_block(rows, 3, 3 * first + 1),
            lane_block(rows, 1, first),
            lane_block(rows, 2, 2 * first),
            lane_block(rows, 1, first),
            lane_block(rows, 1, first),
            fixed_block(rows),
            fixed_block(rows),
            fixed_block(8),
        ],
        out_specs=[pl.BlockSpec((rows, 3 * LANES), lambda p: (0, p)), lane_block(8, 1, 0)],
        out_shape=[
            jax.ShapeDtypeStruct((rows, 3 * width), bf16),
            jax.ShapeDtypeStruct((8, width), f32),
        ],
        scratch_shapes=[pltpu.VMEM((2, rows, LANES), bf16)] * 2
        + [pltpu.VMEM((rows, LANES), f32)] * 3,
        compiler_params=pltpu.CompilerParams(vmem_limit_bytes=50 * 2**20),
        cost_estimate=LIGHT,
        name="self_bwd",
    )(query, kv, kv, raw, raw, own, lse, dmix, dq_cross, cosine, sine, gains)


def feed_kernel(x_ref, grad_ref, gate_ref, up_ref, down_ref, hidden_ref, both_ref):
    f32, bf16 = jnp.float32, jnp.bfloat16
    gate = jnp.dot(x_ref[...], gate_ref[...], preferred_element_type=f32)
    up = jnp.dot(x_ref[...], up_ref[...], preferred_element_type=f32)
    dhidden = jnp.dot(grad_ref[...], down_ref[...], preferred_element_type=f32)
    sig = 1.0 / (1.0 + jnp.exp(-gate))
    act = gate * sig
    hidden_ref[...] = (act * up).astype(bf16)
    tile = gate_ref.shape[1]
    both_ref[:, :tile] = (dhidden * up * sig * (1.0 + gate * (1.0 - sig))).astype(bf16)
    both_ref[:, tile:] = (dhidden * act).astype(bf16)


def feed_forward(x, grad, weights, units, tile):
    rows, depth = x.shape
    count = units // tile
    bf16 = jnp.bfloat16

    def cols(scale, shift):
        return pl.BlockSpec((depth, tile), lambda j: (0, scale * j + shift))

    whole = pl.BlockSpec((rows, depth), lambda j: (0, 0))
    return pl.pallas_call(
        feed_kernel,
        grid=(count,),
        in_specs=[whole, whole, cols(2, 0), cols(2, 1), cols(1, 2 * count)],
        out_specs=[
            pl.BlockSpec((rows, tile), lambda j: (0, j)),
            pl.BlockSpec((rows, 2 * tile), lambda j: (0, j)),
        ],
        out_shape=[
            jax.ShapeDtypeStruct((rows, units), bf16),
            jax.ShapeDtypeStruct((rows, 2 * units), bf16),
        ],
        compiler_params=pltpu.CompilerParams(vmem_limit_bytes=58 * 2**20),
        cost_estimate=LIGHT,
        name="feed_forward",
    )(x, grad, weights, weights, weights)


def outer_kernel(size, bits, me_ref, left_ref, right_ref, keep_ref, away_ref, total_ref):
    total_ref[...] = tn_dot(left_ref[...], right_ref[...])
    rows = keep_ref.shape[0] // (size // 2)
    for place in range(size):
        slot = sum(((place >> (len(bits) - 1 - k)) & 1) << bit for k, bit in enumerate(bits))
        start = pl.multiple_of((me_ref[0] ^ slot) * rows, 16)
        block = total_ref[pl.ds(start, rows), :].astype(jnp.bfloat16)
        out_ref = keep_ref if place < size // 2 else away_ref
        spot = place % (size // 2)
        out_ref[spot * rows : (spot + 1) * rows, :] = block


def outer_grads(me, left, right, size, bits, tile):
    tokens, depth = left.shape
    cols = right.shape[1]
    half = jax.ShapeDtypeStruct((depth // 2, cols), jnp.bfloat16)
    return pl.pallas_call(
        functools.partial(outer_kernel, size, bits),
        grid=(cols // tile,),
        in_specs=[
            pl.BlockSpec(memory_space=pltpu.SMEM),
            pl.BlockSpec((tokens, depth), lambda j: (0, 0)),
            pl.BlockSpec((tokens, tile), lambda j: (0, j)),
        ],
        out_specs=[pl.BlockSpec((depth // 2, tile), lambda j: (0, j))] * 2,
        out_shape=[half, half],
        scratch_shapes=[pltpu.VMEM((depth, tile), jnp.float32)],
        compiler_params=pltpu.CompilerParams(vmem_limit_bytes=50 * 2**20),
        cost_estimate=LIGHT,
        name="outer_grads",
    )(me, left, right)


def product_kernel(turned, has_add, *refs):
    left_ref, right_ref = refs[:2]
    dot = nt_dot if turned else (lambda a, b: jnp.dot(a, b, preferred_element_type=jnp.float32))
    total = dot(left_ref[...], right_ref[...])
    if has_add:
        total = total + refs[2][...].astype(jnp.float32)
    refs[-1][...] = total.astype(refs[-1].dtype)


def product(left, right, cols, tile, dtype, turned=False, shift=0, add=None, part=(0, 1)):
    depth = left.shape[1]
    rows = left.shape[0] // part[1]
    if turned:
        right_block = pl.BlockSpec((tile, depth), lambda j: (j, shift))
    else:
        right_block = pl.BlockSpec((depth, tile), lambda j: (0, j + shift))
    in_specs = [pl.BlockSpec((rows, depth), lambda j: (part[0], 0)), right_block]
    if add is not None:
        in_specs.append(pl.BlockSpec((rows, tile), lambda j: (0, j)))
    return pl.pallas_call(
        functools.partial(product_kernel, turned, add is not None),
        grid=(cols // tile,),
        in_specs=in_specs,
        out_specs=pl.BlockSpec((rows, tile), lambda j: (0, j)),
        out_shape=jax.ShapeDtypeStruct((rows, cols), dtype),
        compiler_params=pltpu.CompilerParams(vmem_limit_bytes=58 * 2**20),
        cost_estimate=LIGHT,
        name="product",
    )(left, right, *([] if add is None else [add]))


def blank(shape, dtype):
    return pl.pallas_call(
        lambda out_ref: None,
        out_specs=pl.BlockSpec(memory_space=pl.ANY),
        out_shape=jax.ShapeDtypeStruct(shape, dtype),
        name="blank",
    )()


def gated(value, *tokens):
    return lax.optimization_barrier((value,) + tokens)[0]


def chip_ring(size):
    depth = size // 4
    return [2 * q if q < depth else 2 * (2 * depth - 1 - q) + 1 for q in range(size // 2)]


def ring_perm(size, step):
    order = chip_ring(size)
    count = len(order)
    return [
        (order[q] * 2 + c, order[(q + step) % count] * 2 + c) for q in range(count) for c in range(2)
    ]


def flip_perm(size, bit):
    return [(i, i ^ bit) for i in range(size)]


def ring_place(size):
    depth = size // 4
    index = lax.axis_index("dp")
    chip = index // 2
    level = chip // 2
    return jnp.where(chip % 2 == 0, level, 2 * depth - 1 - level), index % 2


def chip_at(place, size):
    depth = size // 4
    place = place % (2 * depth)
    return jnp.where(place < depth, 2 * place, 2 * (2 * depth - 1 - place) + 1)


def ring_gather(shard, size, hop):
    count = size // 2
    rows, cols = shard.shape
    half = cols // 2
    place, core = ring_place(size)
    swap = flip_perm(size, 1)
    ahead, behind = ring_perm(size, 1), ring_perm(size, -1)
    pieces = [(0, 0, shard)]
    fwd = bwd = shard
    for step in range(1, count // 2):
        fwd = lax.ppermute(fwd, "dp", ahead)
        bwd = lax.ppermute(bwd, "dp", behind)
        pieces += [(-step, 0, fwd), (step, 0, bwd)]
        token = hop(fwd, bwd)
        if token is not None:
            fwd, bwd = gated((fwd, bwd), token)
    last_f = lax.ppermute(fwd[:, :half], "dp", ahead)
    last_b = lax.ppermute(bwd[:, half:], "dp", behind)
    pieces += [(count // 2, 0, last_f), (count // 2, half, last_b)]
    full = blank((count, 2, rows, cols), shard.dtype)
    for offset, low, piece in pieces:
        other = lax.ppermute(piece, "dp", swap)
        chip = chip_at(place + offset, size)
        full = lax.dynamic_update_slice(full, piece[None, None], (chip, core, 0, low))
        full = lax.dynamic_update_slice(full, other[None, None], (chip, 1 - core, 0, low))
    return full.reshape(size * rows, cols)


class SmallScatter:
    def __init__(self, value, size):
        self.value, self.size, self.bit = value, size, 0

    def left(self):
        return self.value.shape[0] > 1

    def hop(self, *tokens):
        if not self.left():
            return None
        index = lax.axis_index("dp")
        value = gated(self.value, *tokens) if tokens else self.value
        pairs = value.reshape(value.shape[0] // 2, 2, value.shape[1])
        upper = (index >> self.bit) % 2 == 1
        away = jnp.where(upper, pairs[:, 0], pairs[:, 1])
        came = lax.ppermute(away, "dp", flip_perm(self.size, 1 << self.bit))
        self.value = jnp.where(upper, pairs[:, 1], pairs[:, 0]) + came
        self.bit += 1
        return came


class Halving:
    def __init__(self, size, bits, keep, away):
        self.size, self.bits, self.stage = size, bits, 0
        self.terms = [keep]
        self.out = away

    def start(self):
        bit = self.bits[self.stage]
        self.came = lax.ppermute(self.out, "dp", flip_perm(self.size, 1 << bit))
        self.stage += 1

    def land(self, *tokens):
        self.came = gated(self.came, *tokens)
        return self.came

    def finish(self, *tokens):
        self.terms.append(gated(self.came, *tokens) if tokens else self.came)
        rows = self.terms[-1].shape[0]
        last = self.stage == len(self.bits)
        half = rows if last else rows // 2
        low = 0 if last else half
        total = sum(term[low : low + half].astype(jnp.float32) for term in self.terms)
        self.out = total if last else total.astype(jnp.bfloat16)
        self.terms = [term[:half] for term in self.terms]
        return self.out

    def drain(self, *tokens):
        while self.stage < len(self.bits):
            self.finish(*tokens)
            self.start()
            tokens = ()
        self.terms.append(gated(self.came, *tokens) if tokens else self.came)
        rows = self.terms[-1].shape[0]
        return [term[:rows] for term in self.terms]


def swap_start(part, size, chunks):
    step = part.shape[0] // chunks
    own = [part[i * step : (i + 1) * step] for i in range(chunks)]
    if size == 2:
        return own, [lax.ppermute(o, "tensor", flip_perm(size, 1)) for o in own]
    return own, [lax.psum(o, "tensor") for o in own]


def swap_end(own, came, size):
    f32 = jnp.float32
    both = [o.astype(f32) + c.astype(f32) if size == 2 else c.astype(f32) for o, c in zip(own, came)]
    return jnp.concatenate(both, axis=0) if len(both) > 1 else both[0]


def small_gather(value, name, size, tokens=(), steps=None):
    index = lax.axis_index(name)
    for k in range(size.bit_length() - 1):
        bit = 1 << k
        if k < len(tokens):
            value = gated(value, tokens[k])
        came = lax.ppermute(value, name, flip_perm(size, bit))
        upper = (index // bit) % 2 == 1
        value = jnp.where(
            upper, jnp.concatenate([came, value], 0), jnp.concatenate([value, came], 0)
        )
        if steps is not None:
            steps.append(value)
    return value


def small_sum(value, name, size):
    bit = 1
    while bit < size:
        value = value + lax.ppermute(value, name, flip_perm(size, bit))
        bit *= 2
    return value


def tensor_scatter(part, size):
    if size == 2:
        index = lax.axis_index("tensor")
        width = part.shape[1] // 2
        away = lax.dynamic_slice_in_dim(part, (1 - index) * width, width, 1)
        kept = lax.dynamic_slice_in_dim(part, index * width, width, 1)
        came = lax.ppermute(away, "tensor", flip_perm(size, 1))
        return kept.astype(jnp.float32) + came.astype(jnp.float32)
    return lax.psum_scatter(part, "tensor", scatter_dimension=1, tiled=True).astype(jnp.float32)


def weave_kernel(tile, plan, *refs):
    out_ref = refs[-1]
    out_ref[...] = jnp.zeros_like(out_ref)
    for target, source, low, wide, turned in plan:
        if turned:
            out_ref[:, target : target + wide] = refs[source][low : low + wide, :].T
        else:
            out_ref[:, target : target + wide] = refs[source][:, low : low + wide]


def weave(arrays, tile, last=None):
    rows, cols = arrays[0].shape
    count = -(-cols // tile)
    plan = []
    target = 0
    for i in range(count):
        for source in range(len(arrays)):
            plan.append((target, source, i * tile, min(tile, cols - i * tile), False))
            target += tile
    operands = list(arrays)
    if last is not None:
        plan.append((target, len(arrays), 0, last.shape[0], True))
        target += last.shape[0] + -last.shape[0] % tile
        operands.append(last)
    return pl.pallas_call(
        functools.partial(weave_kernel, tile, plan),
        out_shape=jax.ShapeDtypeStruct((rows, target), arrays[0].dtype),
        compiler_params=pltpu.CompilerParams(vmem_limit_bytes=30 * 2**20),
        cost_estimate=LIGHT,
        name="weave",
    )(*operands)


def gather_sum_kernel(tile, count, terms, *refs):
    total = refs[0][...].astype(jnp.float32)
    for ref in refs[1:terms]:
        total = total + ref[...].astype(jnp.float32)
    outs = refs[terms:]
    cols = outs[0].shape[1]
    for i in range(-(-cols // tile)):
        wide = min(tile, cols - i * tile)
        for n, out_ref in enumerate(outs):
            start = (i * count + n) * tile
            out_ref[:, i * tile : i * tile + wide] = total[:, start : start + wide]


def gather_sum(terms, tile, count, cols):
    rows, wide = terms[0].shape
    block = rows
    while block * wide * (2 * len(terms) + 8) > 24 * 2**20 and block % 32 == 0:
        block //= 2
    return pl.pallas_call(
        functools.partial(gather_sum_kernel, tile, count, len(terms)),
        grid=(rows // block,),
        in_specs=[pl.BlockSpec((block, wide), lambda r: (r, 0)) for _ in terms],
        out_specs=[pl.BlockSpec((block, cols), lambda r: (r, 0))] * count,
        out_shape=[jax.ShapeDtypeStruct((rows, cols), jnp.float32)] * count,
        compiler_params=pltpu.CompilerParams(vmem_limit_bytes=58 * 2**20),
        cost_estimate=LIGHT,
        name="gather_sum",
    )(*terms)


def rotary_tables(row_pos, col_pos, quarter, repeat):
    frequency = jnp.exp(-math.log(10000.0) * jnp.arange(quarter, dtype=jnp.float32) / quarter)
    angles = jnp.concatenate(
        [
            row_pos.astype(jnp.float32)[:, None] * frequency,
            col_pos.astype(jnp.float32)[:, None] * frequency,
        ],
        axis=1,
    )
    sine = jnp.sin(angles)
    return jnp.tile(jnp.cos(angles), (1, 2 * repeat)), jnp.tile(
        jnp.concatenate([-sine, sine], axis=1), (1, repeat)
    )


def local(
    size,
    groups,
    latents,
    cotangent,
    caption,
    caption_lens,
    patch_row,
    patch_col,
    timestep,
    query_proj,
    key_proj,
    value_proj,
    output_proj,
    textkey_proj,
    textval_proj,
    gate_proj,
    up_proj,
    down_proj,
    modulation,
    attn_gain,
    ffn_gain,
    query_gain,
    key_gain,
    textkey_gain,
    cross_gate,
):
    f32, bf16 = jnp.float32, jnp.bfloat16
    rows_w, chan = query_proj.shape
    units = gate_proj.shape[1]
    head_part = query_gain.shape[0]
    head_dim = head_part * size
    heads_here = chan // head_dim
    model_dim = latents.shape[1]
    padded = chan + -chan % LANES
    pairs = padded // LANES
    dp_index = lax.axis_index("dp")
    tensor_index = lax.axis_index("tensor")

    small = jnp.concatenate(
        [
            attn_gain.astype(f32),
            ffn_gain.astype(f32),
            query_gain.astype(f32),
            key_gain.astype(f32),
            textkey_gain.astype(f32),
            timestep.astype(f32),
        ]
    )[None]
    steps = []
    small_all = small_gather(small, "dp", size, (), steps)
    textkey_l, textval_l = gated((textkey_proj, textval_proj), steps[0])
    text_shard = weave([textkey_l, textval_l], LANES)
    text_set = lax.all_gather(text_shard, "dp", axis=0, tiled=True)
    query_l, key_l, value_l, output_l = gated(
        (query_proj, key_proj, value_proj, output_proj), steps[1]
    )
    first = weave([query_l, key_l, value_l], LANES, output_l)
    cuts = [rows_w, 2 * rows_w, 2 * rows_w + head_part]
    gain_one = small_all[:, : cuts[0]].reshape(-1)
    gain_two = small_all[:, cuts[0] : cuts[1]].reshape(-1)
    gain_query = small_all[:, cuts[1] : cuts[2]].reshape(-1)
    gain_key = small_all[:, cuts[2] : cuts[2] + head_part].reshape(-1)
    gain_text = small_all[:, cuts[2] + head_part : cuts[2] + 2 * head_part].reshape(-1)
    steps_all = small_all[:, cuts[2] + 2 * head_part :].reshape(-1)
    embed_rows = modulation.shape[0]
    embed_dim = embed_rows * size
    embed_all = time_embed(steps_all, embed_dim)
    cond_all = (embed_all * jax.nn.sigmoid(embed_all)).astype(bf16)
    cond_here = lax.dynamic_slice_in_dim(cond_all, dp_index * embed_rows, embed_rows, 1)
    mod_part = jnp.dot(cond_here, modulation, preferred_element_type=f32)
    mod_sums = SmallScatter(mod_part, size)
    mod_sums.hop()
    full_qkvo = ring_gather(gated(first, small_all), size, mod_sums.hop)
    while mod_sums.left():
        mod_sums.hop()
    mod_here = mod_sums.value
    mod_all = small_gather(mod_here, "tensor", groups).reshape(1, -1)
    tile = 256
    blocks = units // tile
    gate_l, up_l, down_l = gated((gate_proj, up_proj, down_proj), first)
    third = weave([gate_l, up_l], tile, down_l)
    ffn_set = lax.all_gather(gated(third, small_all), "dp", axis=0, tiled=True)
    scale_one = mod_all[:, 0:model_dim]
    gate_one = jnp.tanh(mod_all[:, model_dim : 2 * model_dim])
    scale_two = mod_all[:, 2 * model_dim : 3 * model_dim]
    gate_two = jnp.tanh(mod_all[:, 3 * model_dim : 4 * model_dim])
    tanh_cross = jnp.tanh(cross_gate.astype(f32))
    tanh_lanes = jnp.pad(jnp.repeat(tanh_cross, head_dim), (0, padded - chan))
    tanh_lanes = jnp.broadcast_to(tanh_lanes[None], (8, padded))
    per_tile = LANES // head_dim
    gain_lanes = jnp.pad(
        jnp.tile(jnp.stack([gain_query, gain_key, gain_text]), (1, per_tile)), ((0, 5), (0, 0))
    )
    cosine, sine = rotary_tables(patch_row[0], patch_col[0], head_dim // 4, per_tile)
    tables = (cosine, sine, gain_lanes, tanh_lanes)

    resid_in = latents.astype(f32)
    factor_one = inv_rms(resid_in)
    normed_one = resid_in * factor_one
    attn_in = (normed_one * gain_one * (1.0 + scale_one)).astype(bf16)
    qkv_raw = product(attn_in, full_qkvo, 3 * padded, 3 * LANES, f32)
    cap_in = caption[0]
    full_text = gated(text_set, qkv_raw)
    text_raw = product(cap_in, full_text, 2 * padded, 256, f32)
    mixed_a, query_bf, own_out, cross_out, lse, kv_bf, tkv_bf = attend_rows(
        0, caption_lens, qkv_raw, text_raw, tables, head_dim
    )
    part_a = product(mixed_a, full_qkvo, model_dim, 512, bf16, True, 3)
    own_a, came_a = swap_start(part_a, groups, 1)
    kept = gated((query_bf, own_out, cross_out, lse, kv_bf, tkv_bf), part_a)
    mixed_b, query_bf, own_out, cross_out, lse = attend_rows(
        1, caption_lens, qkv_raw, text_raw, tables, head_dim, kept
    )
    attn_part = product(mixed_b, full_qkvo, model_dim, 512, bf16, True, 3)
    mixed_heads = jnp.concatenate([mixed_a, mixed_b], axis=0)
    mod_set = lax.all_gather(gated(modulation, attn_part), "dp", axis=0, tiled=True)

    grad_out = gated(cotangent, attn_part).astype(f32)
    grad_ffn = (gate_two * grad_out).astype(bf16)
    came_a = gated(came_a, grad_ffn)
    own_b, came_b = swap_start(gated(attn_part, came_a), groups, 1)
    came_b = gated(came_b, came_a)
    attn_out = jnp.concatenate(
        [swap_end(own_a, came_a, groups), swap_end(own_b, came_b, groups)], axis=0
    )
    me = dp_index.astype(jnp.int32)[None]
    depth_bits = list(range(2, size.bit_length() - 1))
    side_first = [0, 1] + depth_bits
    line_first = [0, 2, 1] + depth_bits[1:]

    residual = resid_in + gate_one * attn_out
    factor_two = inv_rms(residual)
    normed_two = residual * factor_two
    ffn_in = (normed_two * gain_two * (1.0 + scale_two)).astype(bf16)
    full_ffn = gated(ffn_set, attn_part)
    hidden, dboth = feed_forward(ffn_in, grad_ffn, full_ffn, units, tile)
    def staged(left, right, bits, tile_cols):
        return Halving(size, bits, *outer_grads(me, left, right, size, bits, tile_cols))

    dffn_one = product(dboth, full_ffn, model_dim, 512, bf16, True, 0, None, (0, 2))
    dffn_two = product(gated(dboth, dffn_one), full_ffn, model_dim, 512, bf16, True, 0, None, (1, 2))
    one_own, one_came = swap_start(dffn_one, groups, 1)
    down = staged(grad_ffn, gated(hidden, dffn_two), line_first, 512)
    down.start()
    one_came = gated(one_came, down.out)
    two_own, two_came = swap_start(gated(dffn_two, one_came), groups, 1)
    grown = staged(ffn_in, gated(dboth, down.out, one_came), side_first, 512)
    grown.start()
    ffn_part = product(gated(hidden, grown.out, mod_set), full_ffn, model_dim, 512, bf16, True, 2)
    two_came = gated(two_came, ffn_part)
    down.finish(two_came)
    down.start()
    grown.finish(down.out)
    grown.start()
    dffn_in = jnp.concatenate(
        [swap_end(one_own, one_came, groups), swap_end(two_own, two_came, groups)], axis=0
    )

    gain_mul = gain_two * (1.0 + scale_two)
    weighed = jnp.sum(dffn_in * normed_two, axis=0)
    grad_gaintwo = weighed * (1.0 + scale_two[0])
    dscale_two = weighed * gain_two
    dresid = grad_out + norm_back(dffn_in * gain_mul, normed_two, factor_two)
    dgate_one = jnp.sum(dresid * attn_out, axis=0) * (1.0 - gate_one[0] ** 2)
    grad_attn = (gate_one * dresid).astype(bf16)
    dmixed = product(grad_attn, full_qkvo, padded, LANES, bf16, False, 3 * padded // LANES)
    ffn_own, ffn_came = swap_start(gated(ffn_part, dmixed), groups, 1)
    dq_cross, dtext, stats_c = cross_back(
        caption_lens, query_bf, tkv_bf, text_raw, cross_out, lse, dmixed, tables, head_dim
    )
    down.finish(dq_cross)
    down.start()
    grown.finish(down.out)
    grown.start()
    text = staged(cap_in, gated(dtext, grown.out), side_first, 256)
    text.start()
    split = pairs - pairs // 2
    windows = [(0, split), (split, pairs - split)]
    common = (query_bf, kv_bf, qkv_raw, own_out, lse)
    dmixed_a = gated(dmixed, text.out)
    gate_part = jnp.sum(grad_out * gated(ffn_part, dmixed).astype(f32), axis=0)
    dqkv_a, stats_a = self_back(windows[0], *common, dmixed_a, dq_cross, tables, head_dim)
    down.finish(dqkv_a)
    down.start()
    grown.finish(down.out)
    grown.start()
    text.finish(grown.out)
    text.start()
    first_qkv = staged(attn_in, gated(dqkv_a, text.out), line_first, 3 * LANES)
    first_qkv.start()
    outp = staged(gated(grad_attn, first_qkv.out), mixed_heads, side_first, padded)
    outp.start()
    edge = 3 * LANES * split
    even = pairs == 2 * split
    wide_a = full_qkvo if even else full_qkvo[:, :edge]
    wide_b = full_qkvo if even else full_qkvo[:, edge : 3 * padded]
    dattn_a = product(gated(dqkv_a, outp.out), wide_a, model_dim, 512, f32, True)
    dmixed_b = gated(dmixed, dattn_a, gate_part)
    dqkv_b, stats_b = self_back(windows[1], *common, dmixed_b, dq_cross, tables, head_dim)
    landed = (down.land(dqkv_b), grown.land(dqkv_b), gated(ffn_came, dqkv_b))
    ffn_came = landed[2]
    dqkv_l = gated(dqkv_b, *landed)
    dattn_part = product(dqkv_l, wide_b, model_dim, 512, bf16, True, int(even), dattn_a)
    half_rows = dattn_part.shape[0] // 2
    high_own, high_came = swap_start(dattn_part[:half_rows], groups, 1)
    last_qkv = staged(attn_in, gated(dqkv_b, dattn_part), side_first, 3 * LANES)
    last_qkv.start()
    text.finish(last_qkv.out)
    text.start()
    first_qkv.finish(text.out)
    first_qkv.start()
    outp.finish(first_qkv.out)
    outp.start()
    caption_part = product(gated(dtext, outp.out), full_text, cap_in.shape[1], 1024, bf16, True)
    high_came = gated(high_came, caption_part)
    base_own, base_came = swap_start(gated(dattn_part[half_rows:], high_came), groups, 1)
    last_qkv.finish(high_came)
    last_qkv.start()
    weighed_part = jnp.sum(gated(dattn_part, last_qkv.out).astype(f32) * normed_one, axis=0)
    grad_gate, grad_up = gather_sum(grown.drain(last_qkv.out), tile, 2, units)
    down_terms = down.drain(grad_gate)
    down_t = sum(term.astype(f32) for term in down_terms)
    text.finish(down_t)
    text.start()
    outp.finish(text.out)
    outp.start()
    first_qkv.finish(outp.out)
    first_qkv.start()
    base_came = gated(base_came, first_qkv.out)
    stats = jnp.concatenate([stats_a, stats_b], axis=1)[:2]
    stat_sums = jnp.concatenate([stats, stats_c[:2]], axis=0)[:, :chan]
    stat_sums = jnp.sum(stat_sums.reshape(4, heads_here, head_dim), axis=(1,))
    xgate_rows = stats_c[1, :chan].reshape(heads_here, head_dim)
    xgate_here = jnp.sum(xgate_rows, axis=1) * (1.0 - tanh_cross**2)
    sums_part = jnp.concatenate([weighed_part, gate_part, stat_sums[:3].reshape(-1)])[None]
    sums = small_sum(gated(sums_part, base_came), "tensor", groups)[0]
    dattn_in = jnp.concatenate(
        [swap_end(high_own, high_came, groups), swap_end(base_own, base_came, groups)], axis=0
    )
    grad_latents = (
        dresid + norm_back(dattn_in * gain_one * (1.0 + scale_one), normed_one, factor_one)
    ).astype(bf16)
    last_qkv.finish(grad_latents)
    last_qkv.start()
    sums = gated(sums, last_qkv.out)
    weighed_one, head_gains = sums[:model_dim], sums[2 * model_dim :]
    dgate_two = sums[model_dim : 2 * model_dim] * (1.0 - gate_two[0] ** 2)
    grad_gainone = weighed_one * (1.0 + scale_one[0])
    dscale_one = weighed_one * gain_one
    dmod_all = jnp.concatenate([dscale_one, dgate_one, dscale_two, dgate_two])
    cols_here = modulation.shape[1]
    dmod_here = lax.dynamic_slice_in_dim(dmod_all, tensor_index * cols_here, cols_here, 0)
    row = jnp.concatenate([dmod_here, grad_gainone, grad_gaintwo, head_gains, xgate_here])
    row = row.astype(bf16).astype(f32)[None]
    dcaption = tensor_scatter(gated(caption_part, sums), groups)
    ffn_out = swap_end(ffn_own, gated(ffn_came, row), groups)
    output = (residual + gate_two * ffn_out).astype(bf16)
    embed_row = jnp.einsum(
        "bc,tc->bt", row[:, :cols_here].astype(bf16), mod_set, preferred_element_type=f32
    )
    first_qkv.finish(output)
    first_qkv.start()
    outp.finish(first_qkv.out)
    outp.start()
    rows_set = small_gather(row, "dp", size, [row, output, first_qkv.out, outp.out])
    grad_textkey, grad_textval = gather_sum(text.drain(outp.out), LANES, 2, chan)
    last_qkv.finish(grad_textkey)
    last_qkv.start()
    dmod_set = rows_set[:, :cols_here].astype(bf16)
    gain_sums = jnp.sum(rows_set[:, cols_here:], axis=0)
    grad_modul = jnp.einsum("bt,bc->tc", cond_here, dmod_set, preferred_element_type=f32)
    embed_sum = small_sum(embed_row, "tensor", groups)
    embed_own = lax.dynamic_slice_in_dim(embed_all, dp_index, 1, 0)
    sig_own = jax.nn.sigmoid(embed_own)
    dembed_all = embed_sum * (sig_own * (1.0 + embed_own * (1.0 - sig_own)))
    width = embed_dim // groups
    dembed = lax.dynamic_slice_in_dim(dembed_all, tensor_index * width, width, 1)
    output_t = sum(term.astype(f32) for term in outp.drain(last_qkv.out))
    wide = min(split * LANES, chan)
    parts_a = gather_sum(first_qkv.drain(output_t), LANES, 3, wide)
    parts_b = gather_sum(last_qkv.drain(parts_a[0]), LANES, 3, chan - wide)
    grad_query, grad_key, grad_value = [
        jnp.concatenate([one, two], axis=1) for one, two in zip(parts_a, parts_b)
    ]

    def own_part(start, width):
        return lax.dynamic_slice_in_dim(gain_sums, start + dp_index * width, width, 0)

    heads_at = 2 * model_dim
    gate_at = heads_at + 3 * head_dim
    return (
        output,
        grad_latents,
        dcaption.astype(bf16)[None],
        dembed,
        grad_query,
        grad_key,
        grad_value,
        output_t[:, :chan].T,
        grad_textkey,
        grad_textval,
        grad_gate,
        grad_up,
        down_t.T,
        grad_modul,
        own_part(0, rows_w),
        own_part(model_dim, rows_w),
        own_part(heads_at, head_part),
        own_part(heads_at + head_dim, head_part),
        own_part(heads_at + 2 * head_dim, head_part),
        gain_sums[gate_at:],
    )


def solution(mesh):
    in_specs = (
        P("dp", None),
        P("dp", None),
        P("dp", None, None),
        P("dp"),
        P("dp", None),
        P("dp", None),
        P("dp"),
        P("dp", "tensor"),
        P("dp", "tensor"),
        P("dp", "tensor"),
        P("tensor", "dp"),
        P("dp", "tensor"),
        P("dp", "tensor"),
        P("dp", "tensor"),
        P("dp", "tensor"),
        P("tensor", "dp"),
        P("dp", "tensor"),
        P("dp"),
        P("dp"),
        P("dp"),
        P("dp"),
        P("dp"),
        P("tensor"),
    )
    out_specs = (
        P("dp", None),
        P("dp", None),
        P("dp", None, "tensor"),
        P("dp", "tensor"),
        P("dp", "tensor"),
        P("dp", "tensor"),
        P("dp", "tensor"),
        P("tensor", "dp"),
        P("dp", "tensor"),
        P("dp", "tensor"),
        P("dp", "tensor"),
        P("dp", "tensor"),
        P("tensor", "dp"),
        P("dp", "tensor"),
        P("dp"),
        P("dp"),
        P("dp"),
        P("dp"),
        P("dp"),
        P("tensor"),
    )
    bound = functools.partial(local, mesh.shape["dp"], mesh.shape["tensor"])
    return jax.shard_map(bound, mesh=mesh, in_specs=in_specs, out_specs=out_specs, check_vma=False)
```

time: 1020 us -> 869 us (0.85)
  Pallas kernels: 109 us -> 332 us
  matrix products: 191 us -> 3.22 us
  starting transfers between devices: 185 us -> 52.5 us
  local copies, waits for them, and re-layouts: 127 us -> 74.8 us
  other arithmetic: 112 us -> 131 us
  waiting for transfers between devices: 265 us -> 250 us
    pallas_call x3 -> x31, Pallas kernels: 109 us -> 332 us  [the longest x11 104 us: product(): pl.pallas_call(functools.partial(product_kernel, turned, add is not None)...]
    dot_general x26 -> x1, matrix products: 190 us -> 1.72 us  [local(): jnp.einsum('bc,tc->bt', row[:, :cols_here].astype(bf16), mod_set, preferr...]
    ppermute x43 -> x28, starting transfers between devices: 149 us -> 24.2 us  [the longest x24 21.7 us: start(): self.came = lax.ppermute(self.out, 'dp', flip_perm(self.size, 1 << bit))]
    ppermute x43 -> x28, waiting for transfers between devices: 101 us -> 34.8 us  [the longest x24 29.9 us: start(): self.came = lax.ppermute(self.out, 'dp', flip_perm(self.size, 1 << bit))]
    ppermute x4 -> x7, waiting for transfers between devices: 56.1 us -> 101 us  [swap_start(): return (own, [lax.ppermute(o, 'tensor', flip_perm(size, 1)) for o in own])]
    ppermute x3, waiting for transfers between devices: 4.42 us -> 43.6 us  [ring_gather(): bwd = lax.ppermute(bwd, 'dp', behind)]
    ppermute x6 -> x2, waiting for transfers between devices: 27.4 us -> 0.01 us  [small_sum(): value = value + lax.ppermute(value, name, flip_perm(size, bit))]
    convert_element_type x15 -> x20, other arithmetic: 30.8 us -> 57.4 us  [the longest x18 48.4 us: finish(): self.out = total if last else total.astype(jnp.bfloat16)]
  transfers between devices with their start and end apart: 86 -> 67, of which waited for: 37 -> 26; matrix products, arithmetic and copies ran while one was open for 31% -> 21% of each run, Pallas kernels for 7% -> 37%
where the time goes in v2:
time: 869 us; the launch traced here: 860 us
  Pallas kernels  332 us (38%)
  waiting for transfers between devices  250 us (29%)
  other arithmetic  131 us (15%)
  local copies, waits for them, and re-layouts  74.8 us (9%)
  starting transfers between devices  52.5 us (6%)
  between operations  17.3 us (2%)
    pallas_call x11, Pallas kernels, product(): pl.pallas_call(functools.partial(product_kernel, turned, add is not None)...  104 us
    ppermute x7, waiting for transfers between devices, swap_start(): return (own, [lax.ppermute(o, 'tensor', flip_perm(size, 1)) for o in own])  101 us
    pallas_call x6, Pallas kernels, outer_grads(): pl.pallas_call(functools.partial(outer_kernel, size, bits), grid=(cols //...  63.4 us
    pallas_call x2, Pallas kernels, self_back(): pl.pallas_call(functools.partial(self_back_kernel, half, min(512, rows)),...  62.1 us
    convert_element_type x18, other arithmetic, finish(): self.out = total if last else total.astype(jnp.bfloat16)  48.4 us
    ppermute x3, waiting for transfers between devices, ring_gather(): fwd = lax.ppermute(fwd, 'dp', ahead)  45 us
    ppermute x3, waiting for transfers between devices, ring_gather(): bwd = lax.ppermute(bwd, 'dp', behind)  43.6 us
    pallas_call x2, Pallas kernels, attend_rows(): pl.pallas_call(functools.partial(attend_kernel, half, min(256, count), fr...  39.9 us
  transfers between devices with their start and end apart: 67, of which 26 were waited for; matrix products, arithmetic and copies ran while one was open for 21% of the time, Pallas kernels for 37%

profile of v2, /device:TPU:0, one launch (start us, length us, event | category | flops | bytes accessed | tf_op | source)
XLA Modules:
  0.0 860.2 jit_solution(16725235715201115350)
XLA Ops:
  42.9 24.8 %collective-permute-done.6 = bf16[96,3072]{1,0:T(8,128)(2,1)S(1)} collective-permute-done((bf16[96,3072]{1,0:T(8,128)(2,1)S(1)}, bf16[96,3072]{1,0:T(8,128)(2,1)S(1)}, u32[]{:S(2)}, u32[]{:S(2)}) %collective-permute-start.6) | collective-permute-done | bytes 589856 | tf_op jit(solution)/shard_map/ppermute | solution.py:617
  78.6 24.1 %collective-permute-done.8 = bf16[96,3072]{1,0:T(8,128)(2,1)} collective-permute-done((bf16[96,3072]{1,0:T(8,128)(2,1)}, bf16[96,3072]{1,0:T(8,128)(2,1)}, u32[]{:S(2)}, u32[]{:S(2)}) %collective-permute-start.8) | collective-permute-done | bytes 589856 | tf_op jit(solution)/shard_map/ppermute | solution.py:616
  102.6 14.2 %collective-permute-done.9 = bf16[96,3072]{1,0:T(8,128)(2,1)} collective-permute-done((bf16[96,3072]{1,0:T(8,128)(2,1)S(1)}, bf16[96,3072]{1,0:T(8,128)(2,1)}, u32[]{:S(2)}, u32[]{:S(2)}) %collective-permute-start.9) | collective-permute-done | bytes 589856 | tf_op jit(solution)/shard_map/ppermute | solution.py:617
  126.4 20.9 %collective-permute-done.11 = bf16[96,3072]{1,0:T(8,128)(2,1)S(1)} collective-permute-done((bf16[96,3072]{1,0:T(8,128)(2,1)}, bf16[96,3072]{1,0:T(8,128)(2,1)S(1)}, u32[]{:S(2)}, u32[]{:S(2)}) %collective-permute-start.11) | collective-permute-done | bytes 589856 | tf_op jit(solution)/shard_map/ppermute | solution.py:616
  179.4 14.9 %product.11.refs_1_.refs_2_.refs_3_.rawq_ref.rawk_ref = f32[1024,2304]{1,0:T(8,128)} custom-call(bf16[1024,1536]{1,0:T(8,128)(2,1)} %fusion.8.refs_0_.left_ref, bf16[1536,3072]{1,0:T(8,128)(2,1)} %bitcast.89), custom_call_target="tpu_custom_call" | custom-call | flops 1 | bytes 1 | tf_op jit(solution)/shard_map/product/pallas_call | solution.py:550
  194.3 9.7 %product.12.refs_4_.refs_5_.text_ref = f32[256,1536]{1,0:T(8,128)} custom-call(bf16[256,4096]{1,0:T(8,128)(2,1)} %bitcast.87, bf16[4096,1536]{1,0:T(8,128)(2,1)} %all-gather.4.cloned.1.call-done.refs_1_), custom_call_target="tpu_custom_call" | custom-call | flops 1 | bytes 1 | tf_op jit(solution)/shard_map/product/pallas_call | solution.py:550
  203.9 21.7 %attend_fwd.2 = (bf16[512,768]{1,0:T(8,128)(2,1)S(1)}, bf16[1024,768]{1,0:T(8,128)(2,1)}, f32[1024,768]{1,0:T(8,128)}, f32[1024,768]{1,0:T(8,128)}, f32[1024,153...) custom-call(s32[1]{0:T(128)S(6)} %copy.162.refs_0_.len_ref, ...), custom_call_target="tpu_custom_call" | custom-call | flops 1 | bytes 1 | tf_op jit(solution)/shard_map/attend_fwd/pallas_call | solution.py:189
  231.5 18.1 %attend_fwd.3 = (bf16[512,768]{1,0:T(8,128)(2,1)S(1)}, bf16[1024,768]{1,0:T(8,128)(2,1)}, f32[1024,768]{1,0:T(8,128)}, f32[1024,768]{1,0:T(8,128)}, f32[1024,1536]{1,0:T(8,128)}) custom-call(s32[1]{0:T(128)S(6)} %copy.162.refs_0_.len_ref, ...), custom_call_target="tpu_custom_call", output_to_operand_aliasing={{1}: (8, {}), {2}: (9, {}), {3}: (10, {}), {4}: (11, {})} | custom-call | flops 1 | bytes 1 | tf_op jit(solution)/shard_map/attend_fwd/pallas_call | solution.py:189
  270.8 34.2 %collective-permute-done.27 = bf16[512,1536]{1,0:T(8,128)(2,1)} collective-permute-done((bf16[512,1536]{1,0:T(8,128)(2,1)}, bf16[512,1536]{1,0:T(8,128)(2,1)}, u32[]{:S(2)}, u32[]{:S(2)}) %collective-permute-start.27) | collective-permute-done | bytes 1572896 | tf_op jit(solution)/shard_map/ppermute | solution.py:695
  316.2 26.8 %feed_forward.1 = (bf16[1024,2048]{1,0:T(8,128)(2,1)}, bf16[1024,4096]{1,0:T(8,128)(2,1)}) custom-call(bf16[1024,1536]{1,0:T(8,128)(2,1)} %multiply_convert_fusion.1.x_ref.left_ref, bf16[1024,1536]{1,0:T(8,128)(2,1)} %fusion.16.grad_ref.left_ref, bf16[1536,6144]{1,0:T(8,128)(2,1)} %all-gather.6.cloned.1.call-done.gate_ref.up_ref.down_ref.refs_1_, ...), custom_call_target="tpu_custom_call" | custom-call | flops 1 | bytes 1 | tf_op jit(solution)/shard_map/feed_forward/pallas_call | solution.py:480
  342.9 11.7 %product.15 = bf16[512,1536]{1,0:T(8,128)(2,1)} custom-call(bf16[1024,4096]{1,0:T(8,128)(2,1)} %get-tuple-element.198.refs_0_.right_ref, bf16[1536,6144]{1,0:T(8,128)(2,1)} %all-gather.6.cloned.1.call-done.gate_ref.up_ref.down_ref.refs_1_), custom_call_target="tpu_custom_call" | custom-call | flops 1 | bytes 1 | tf_op jit(solution)/shard_map/product/pallas_call | solution.py:550
  354.8 11.4 %product.16 = bf16[512,1536]{1,0:T(8,128)(2,1)} custom-call(bf16[1024,4096]{1,0:T(8,128)(2,1)} %get-tuple-element.198.refs_0_.right_ref, bf16[1536,6144]{1,0:T(8,128)(2,1)} %all-gather.6.cloned.1.call-done.gate_ref.up_ref.down_ref.refs_1_), custom_call_target="tpu_custom_call" | custom-call | flops 1 | bytes 1 | tf_op jit(solution)/shard_map/product/pallas_call | solution.py:550
  366.2 11.6 %outer_grads.6 = (bf16[768,2048]{1,0:T(8,128)(2,1)S(1)}, bf16[768,2048]{1,0:T(8,128)(2,1)}) custom-call(s32[1]{0:T(128)} %bitcast.31.me_ref, bf16[1024,1536]{1,0:T(8,128)(2,1)} %fusion.16.grad_ref.left_ref, bf16[1024,2048]{1,0:T(8,128)(2,1)} %get-tuple-element.201.right_ref.refs_0_), custom_call_target="tpu_custom_call" | custom-call | flops 1 | bytes 1 | tf_op jit(solution)/shard_map/outer_grads/pallas_call | solution.py:514
  377.8 12.3 %collective-permute-done.28 = bf16[512,1536]{1,0:T(8,128)(2,1)S(1)} collective-permute-done((bf16[512,1536]{1,0:T(8,128)(2,1)}, bf16[512,1536]{1,0:T(8,128)(2,1)S(1)}, u32[]{:S(2)}, u32[]{:S(2)}) %collective-permute-start.28) | collective-permute-done | bytes 1572896 | tf_op jit(solution)/shard_map/ppermute | solution.py:695
  390.1 19.0 %outer_grads.7 = (bf16[768,4096]{1,0:T(8,128)(2,1)}, bf16[768,4096]{1,0:T(8,128)(2,1)}) custom-call(s32[1]{0:T(128)} %bitcast.31.me_ref, bf16[1024,1536]{1,0:T(8,128)(2,1)S(1)} %copy-done, bf16[1024,4096]{1,0:T(8,128)(2,1)} %get-tuple-element.198.refs_0_.right_ref), custom_call_target="tpu_custom_call" | custom-call | flops 1 | bytes 1 | tf_op jit(solution)/shard_map/outer_grads/pallas_call | solution.py:514
  410.0 11.1 %product.17 = bf16[1024,1536]{1,0:T(8,128)(2,1)} custom-call(bf16[1024,2048]{1,0:T(8,128)(2,1)} %get-tuple-element.201.right_ref.refs_0_, bf16[1536,6144]{1,0:T(8,128)(2,1)} %all-gather.6.cloned.1.call-done.gate_ref.up_ref.down_ref.refs_1_), custom_call_target="tpu_custom_call" | custom-call | flops 1 | bytes 1 | tf_op jit(solution)/shard_map/product/pallas_call | solution.py:550
  421.6 24.8 %collective-permute-done.29 = bf16[512,1536]{1,0:T(8,128)(2,1)} collective-permute-done((bf16[512,1536]{1,0:T(8,128)(2,1)}, bf16[512,1536]{1,0:T(8,128)(2,1)}, u32[]{:S(2)}, u32[]{:S(2)}) %collective-permute-start.29) | collective-permute-done | bytes 1572896 | tf_op jit(solution)/shard_map/ppermute | solution.py:695
  486.5 21.2 %cross_bwd.1 = (f32[1024,768]{1,0:T(8,128)S(1)}, bf16[256,1536]{1,0:T(8,128)(2,1)S(1)}, f32[8,768]{1,0:T(8,128)S(1)}) custom-call(s32[1]{0:T(128)S(6)} %copy.162.refs_0_.len_ref, bf16[1024,768]{1,0:T(8,128)(2,1)S(1)} %copy-done.2, bf16[256,1536]{1,0:T(8,128)(2,1)S(1)} %get-tuple-element.177.refs_3_.tkv_ref, f32[256,1536]{1,0:T(8,128)S(1)} %copy-done.3, ...), custom_call_target="tpu_custom_call" | custom-call | flops 1 | bytes 1 | tf_op jit(solution)/shard_map/cross_bwd/pallas_call | solution.py:390
  511.1 12.8 %collective-permute-done.33 = bf16[384,4096]{1,0:T(8,128)(2,1)} collective-permute-done((bf16[384,4096]{1,0:T(8,128)(2,1)}, bf16[384,4096]{1,0:T(8,128)(2,1)}, u32[]{:S(2)}, u32[]{:S(2)}) %collective-permute-start.33) | collective-permute-done | bytes 3145760 | tf_op jit(solution)/shard_map/ppermute | solution.py:663
  537.1 31.3 %self_bwd.2 = (bf16[1024,1152]{1,0:T(8,128)(2,1)}, f32[8,384]{1,0:T(8,128)S(1)}) custom-call(bf16[1024,768]{1,0:T(8,128)(2,1)S(1)} %copy-done.2, bf16[1024,1536]{1,0:T(8,128)(2,1)} %get-tuple-element.176.refs_2_.key_ref.val_ref, bf16[1024,1536]{1,0:T(8,128)(2,1)} %get-tuple-element.176.refs_2_.key_ref.val_ref, ...), custom_call_target="tpu_custom_call" | custom-call | flops 1 | bytes 1 | tf_op jit(solution)/shard_map/self_bwd/pallas_call | solution.py:428
  627.8 30.7 %self_bwd.3 = (bf16[1024,1152]{1,0:T(8,128)(2,1)}, f32[8,384]{1,0:T(8,128)S(1)}) custom-call(bf16[1024,768]{1,0:T(8,128)(2,1)S(1)} %copy-done.2, bf16[1024,1536]{1,0:T(8,128)(2,1)} %get-tuple-element.176.refs_2_.key_ref.val_ref, bf16[1024,1536]{1,0:T(8,128)(2,1)} %get-tuple-element.176.refs_2_.key_ref.val_ref, ...), custom_call_target="tpu_custom_call" | custom-call | flops 1 | bytes 1 | tf_op jit(solution)/shard_map/self_bwd/pallas_call | solution.py:428
  658.5 9.8 %product.20 = bf16[1024,1536]{1,0:T(8,128)(2,1)} custom-call(bf16[1024,1152]{1,0:T(8,128)(2,1)} %get-tuple-element.236.refs_0_.right_ref, bf16[1536,3072]{1,0:T(8,128)(2,1)} %bitcast.94, f32[1024,1536]{1,0:T(8,128)} %product.19.refs_2_), custom_call_target="tpu_custom_call" | custom-call | flops 1 | bytes 1 | tf_op jit(solution)/shard_map/product/pallas_call | solution.py:550
  704.1 15.6 %collective-permute-done.41 = bf16[512,1536]{1,0:T(8,128)(2,1)} collective-permute-done((bf16[512,1536]{1,0:T(8,128)(2,1)}, bf16[512,1536]{1,0:T(8,128)(2,1)}, u32[]{:S(2)}, u32[]{:S(2)}) %collective-permute-start.41) | collective-permute-done | bytes 1572896 | tf_op jit(solution)/shard_map/ppermute | solution.py:695
  737.2 11.5 %collective-permute-done.48 = bf16[512,1536]{1,0:T(8,128)(2,1)} collective-permute-done((bf16[512,1536]{1,0:T(8,128)(2,1)}, bf16[512,1536]{1,0:T(8,128)(2,1)}, u32[]{:S(2)}, u32[]{:S(2)}) %collective-permute-start.48) | collective-permute-done | bytes 1572896 | tf_op jit(solution)/shard_map/ppermute | solution.py:663
  (492 shorter events, 398.5 us)
Async XLA Ops:
  7.2 187.1 %all-gather.4.cloned.1.call-start = ((), (), s32[]{:S(2)}) async-start(), calls=%async_computation | async-start | bytes 13369344 | tf_op jit(solution)/shard_map/all_gather | solution.py:871
  15.7 300.4 %all-gather.6.cloned.1.call-start = ((), (), s32[]{:S(2)}) async-start(), calls=%async_computation.1 | async-start | bytes 20054016 | tf_op jit(solution)/shard_map/all_gather | solution.py:900
  32.6 377.4 %all-gather.8.cloned.1.call-start = ((), (), s32[]{:S(2)}) async-start(), calls=%async_computation.2 | async-start | bytes 6684672 | tf_op jit(solution)/shard_map/all_gather | solution.py:934
  75.7 41.2 %collective-permute-start.9 = (bf16[96,3072]{1,0:T(8,128)(2,1)S(1)}, bf16[96,3072]{1,0:T(8,128)(2,1)}, u32[]{:S(2)}, u32[]{:S(2)}) collective-permute-start(bf16[96,3072]{1,0:T(8,128)(2,1)S(1)} %collective-permute-done.6), channel_id=1, source_target_pairs={{0,4},{2,6},{8,0},{10,2},{16,8},{18,10},{24,16},{26,18},{28,24},{3... | collective-permute-start | bytes 1769480 | tf_op jit(solution)/shard_map/ppermute | solution.py:617
  231.3 37.2 %collective-permute-start.26 = (bf16[512,1536]{1,0:T(8,128)(2,1)}, bf16[512,1536]{1,0:T(8,128)(2,1)}, u32[]{:S(2)}, u32[]{:S(2)}) collective-permute-start(bf16[512,1536]{1,0:T(8,128)(2,1)} %product.13), channel_id=1, source_target_pairs={{0,1},{1,0},{2,3},{3,2},{4,5},{5,4},{6,7},{7,6},{8,9},{9,8},{10,11... | collective-permute-start | bytes 4718600 | tf_op jit(solution)/shard_map/ppermute | solution.py:695
  409.1 40.5 %collective-permute-start.31 = (bf16[768,4096]{1,0:T(8,128)(2,1)}, bf16[768,4096]{1,0:T(8,128)(2,1)}, u32[]{:S(2)}, u32[]{:S(2)}) collective-permute-start(bf16[768,4096]{1,0:T(8,128)(2,1)} %get-tuple-element.199), channel_id=1, source_target_pairs={{0,2},{2,0},{4,6},{6,4},{8,10},{10,8},{12,14},{14,12},{16,18},{18,... | collective-permute-start | bytes 18874376 | tf_op jit(solution)/shard_map/ppermute | solution.py:663
  454.3 69.6 %collective-permute-start.33 = (bf16[384,4096]{1,0:T(8,128)(2,1)}, bf16[384,4096]{1,0:T(8,128)(2,1)}, u32[]{:S(2)}, u32[]{:S(2)}) collective-permute-start(bf16[384,4096]{1,0:T(8,128)(2,1)} %add_convert_fusion.1), channel_id=1, source_target_pairs={{0,4},{2,6},{4,0},{6,2},{8,12},{10,14},{12,8},{14,10},{16,20},{18,... | collective-permute-start | bytes 9437192 | tf_op jit(solution)/shard_map/ppermute | solution.py:663
  457.6 50.1 %collective-permute-start.34 = (bf16[384,2048]{1,0:T(8,128)(2,1)}, bf16[384,2048]{1,0:T(8,128)(2,1)}, u32[]{:S(2)}, u32[]{:S(2)}) collective-permute-start(bf16[384,2048]{1,0:T(8,128)(2,1)} %add_convert_fusion.4), channel_id=1, source_target_pairs={{0,8},{2,10},{4,12},{6,14},{8,0},{10,2},{12,4},{14,6},{16,24},{18,... | collective-permute-start | bytes 4718600 | tf_op jit(solution)/shard_map/ppermute | solution.py:663
  535.3 40.3 %collective-permute-start.35 = (bf16[2048,1536]{1,0:T(8,128)(2,1)}, bf16[2048,1536]{1,0:T(8,128)(2,1)}, u32[]{:S(2)}, u32[]{:S(2)}) collective-permute-start(bf16[2048,1536]{1,0:T(8,128)(2,1)} %get-tuple-element.218), channel_id=1, source_target_pairs={{0,2},{2,0},{4,6},{6,4},{8,10},{10,8},{12,14},{14,12},{16,18},{18,... | collective-permute-start | bytes 18874376 | tf_op jit(solution)/shard_map/ppermute | solution.py:663
  536.4 122.1 %collective-permute-start.30 = (bf16[1024,1536]{1,0:T(8,128)(2,1)}, bf16[1024,1536]{1,0:T(8,128)(2,1)}, u32[]{:S(2)}, u32[]{:S(2)}) collective-permute-start(bf16[1024,1536]{1,0:T(8,128)(2,1)} %product.17), channel_id=1, source_target_pairs={{0,1},{1,0},{2,3},{3,2},{4,5},{5,4},{6,7},{7,6},{8,9},{9,8},{10,11... | collective-permute-start | bytes 9437192 | tf_op jit(solution)/shard_map/ppermute | solution.py:695
  580.2 105.4 %collective-permute-start.44 = (bf16[1024,1536]{1,0:T(8,128)(2,1)}, bf16[1024,1536]{1,0:T(8,128)(2,1)}, u32[]{:S(2)}, u32[]{:S(2)}) collective-permute-start(bf16[1024,1536]{1,0:T(8,128)(2,1)} %add_convert_fusion), channel_id=1, source_target_pairs={{0,4},{2,6},{4,0},{6,2},{8,12},{10,14},{12,8},{14,10},{16,20},{18,... | collective-permute-start | bytes 9437192 | tf_op jit(solution)/shard_map/ppermute | solution.py:663
  587.6 70.9 %collective-permute-start.39 = (bf16[96,4096]{1,0:T(8,128)(2,1)}, bf16[96,4096]{1,0:T(8,128)(2,1)S(1)}, u32[]{:S(2)}, u32[]{:S(2)}) collective-permute-start(bf16[96,4096]{1,0:T(8,128)(2,1)} %add_convert_fusion.9), channel_id=1, source_target_pairs={{0,16},{2,18},{4,20},{6,22},{8,24},{10,26},{12,28},{14,30},{16,0},... | collective-permute-start | bytes 2359304 | tf_op jit(solution)/shard_map/ppermute | solution.py:663
  589.3 69.2 %collective-permute-start.38 = (bf16[96,2048]{1,0:T(8,128)(2,1)}, bf16[96,2048]{1,0:T(8,128)(2,1)S(1)}, u32[]{:S(2)}, u32[]{:S(2)}) collective-permute-start(bf16[96,2048]{1,0:T(8,128)(2,1)} %add_convert_fusion.14), channel_id=1, source_target_pairs={{0,16},{2,18},{4,20},{6,22},{8,24},{10,26},{12,28},{14,30},{16,0},... | collective-permute-start | bytes 1179656 | tf_op jit(solution)/shard_map/ppermute | solution.py:663
  601.1 88.7 %collective-permute-start.43 = (bf16[768,1152]{1,0:T(8,128)(2,1)}, bf16[768,1152]{1,0:T(8,128)(2,1)}, u32[]{:S(2)}, u32[]{:S(2)}) collective-permute-start(bf16[768,1152]{1,0:T(8,128)(2,1)} %get-tuple-element.226), channel_id=1, source_target_pairs={{0,2},{2,0},{4,6},{6,4},{8,10},{10,8},{12,14},{14,12},{16,18},{18,... | collective-permute-start | bytes 5308424 | tf_op jit(solution)/shard_map/ppermute | solution.py:663
  677.9 41.8 %collective-permute-start.40 = (bf16[768,1152]{1,0:T(8,128)(2,1)}, bf16[768,1152]{1,0:T(8,128)(2,1)}, u32[]{:S(2)}, u32[]{:S(2)}) collective-permute-start(bf16[768,1152]{1,0:T(8,128)(2,1)} %get-tuple-element.238), channel_id=1, source_target_pairs={{0,2},{2,0},{4,6},{6,4},{8,10},{10,8},{12,14},{14,12},{16,18},{18,... | collective-permute-start | bytes 5308424 | tf_op jit(solution)/shard_map/ppermute | solution.py:663
  693.3 62.4 %collective-permute-start.47 = (bf16[384,768]{1,0:T(8,128)(2,1)S(1)}, bf16[384,768]{1,0:T(8,128)(2,1)}, u32[]{:S(2)}, u32[]{:S(2)}) collective-permute-start(bf16[384,768]{1,0:T(8,128)(2,1)S(1)} %add_convert_fusion.11), channel_id=1, source_target_pairs={{0,4},{2,6},{4,0},{6,2},{8,12},{10,14},{12,8},{14,10},{16,20},{18,... | collective-permute-start | bytes 1769480 | tf_op jit(solution)/shard_map/ppermute | solution.py:663
  693.7 64.4 %collective-permute-start.46 = (bf16[384,1152]{1,0:T(8,128)(2,1)}, bf16[384,1152]{1,0:T(8,128)(2,1)}, u32[]{:S(2)}, u32[]{:S(2)}) collective-permute-start(bf16[384,1152]{1,0:T(8,128)(2,1)} %add_convert_fusion.7), channel_id=1, source_target_pairs={{0,8},{2,10},{4,12},{6,14},{8,0},{10,2},{12,4},{14,6},{16,24},{18,... | collective-permute-start | bytes 2654216 | tf_op jit(solution)/shard_map/ppermute | solution.py:663
  695.5 53.3 %collective-permute-start.48 = (bf16[512,1536]{1,0:T(8,128)(2,1)}, bf16[512,1536]{1,0:T(8,128)(2,1)}, u32[]{:S(2)}, u32[]{:S(2)}) collective-permute-start(bf16[512,1536]{1,0:T(8,128)(2,1)} %add_convert_fusion.2), channel_id=1, source_target_pairs={{0,8},{2,10},{4,12},{6,14},{8,0},{10,2},{12,4},{14,6},{16,24},{18,... | collective-permute-start | bytes 4718600 | tf_op jit(solution)/shard_map/ppermute | solution.py:663
  731.0 44.5 %collective-permute-start.50 = (bf16[384,1152]{1,0:T(8,128)(2,1)}, bf16[384,1152]{1,0:T(8,128)(2,1)S(1)}, u32[]{:S(2)}, u32[]{:S(2)}) collective-permute-start(bf16[384,1152]{1,0:T(8,128)(2,1)} %add_convert_fusion.6), channel_id=1, source_target_pairs={{0,4},{2,6},{4,0},{6,2},{8,12},{10,14},{12,8},{14,10},{16,20},{18,... | collective-permute-start | bytes 2654216 | tf_op jit(solution)/shard_map/ppermute | solution.py:663
  754.1 69.8 %collective-permute-start.58 = (bf16[256,1536]{1,0:T(8,128)(2,1)}, bf16[256,1536]{1,0:T(8,128)(2,1)}, u32[]{:S(2)}, u32[]{:S(2)}) collective-permute-start(bf16[256,1536]{1,0:T(8,128)(2,1)} %add_convert_fusion.8), channel_id=1, source_target_pairs={{0,16},{2,18},{4,20},{6,22},{8,24},{10,26},{12,28},{14,30},{16,0},... | collective-permute-start | bytes 2359304 | tf_op jit(solution)/shard_map/ppermute | solution.py:663
  757.5 44.2 %collective-permute-start.55 = (bf16[192,768]{1,0:T(8,128)(2,1)}, bf16[192,768]{1,0:T(8,128)(2,1)}, u32[]{:S(2)}, u32[]{:S(2)}) collective-permute-start(bf16[192,768]{1,0:T(8,128)(2,1)} %add_convert_fusion.15), channel_id=1, source_target_pairs={{0,8},{2,10},{4,12},{6,14},{8,0},{10,2},{12,4},{14,6},{16,24},{18,... | collective-permute-start | bytes 884744 | tf_op jit(solution)/shard_map/ppermute | solution.py:663
  760.2 39.5 %collective-permute-start.53 = (bf16[192,1152]{1,0:T(8,128)(2,1)}, bf16[192,1152]{1,0:T(8,128)(2,1)}, u32[]{:S(2)}, u32[]{:S(2)}) collective-permute-start(bf16[192,1152]{1,0:T(8,128)(2,1)} %add_convert_fusion.13), channel_id=1, source_target_pairs={{0,4},{2,6},{4,0},{6,2},{8,12},{10,14},{12,8},{14,10},{16,20},{18,... | collective-permute-start | bytes 1327112 | tf_op jit(solution)/shard_map/ppermute | solution.py:663
  780.3 47.3 %collective-permute-start.57 = (bf16[192,1152]{1,0:T(8,128)(2,1)}, bf16[192,1152]{1,0:T(8,128)(2,1)}, u32[]{:S(2)}, u32[]{:S(2)}) collective-permute-start(bf16[192,1152]{1,0:T(8,128)(2,1)} %add_convert_fusion.12), channel_id=1, source_target_pairs={{0,8},{2,10},{4,12},{6,14},{8,0},{10,2},{12,4},{14,6},{16,24},{18,... | collective-permute-start | bytes 1327112 | tf_op jit(solution)/shard_map/ppermute | solution.py:663
  807.0 43.6 %collective-permute-start.51 = (bf16[256,2048]{1,0:T(8,128)(2,1)S(1)}, bf16[256,2048]{1,0:T(8,128)(2,1)}, u32[]{:S(2)}, u32[]{:S(2)}) collective-permute-start(bf16[256,2048]{1,0:T(8,128)(2,1)S(1)} %constant_dynamic-slice_fusion.3), channel_id=1, source_target_pairs={{0,1},{1,0},{2,3},{3,2},{4,5},{5,4},{6,7},{7,6},{8,9},{9,8},{10,11... | collective-permute-start | bytes 3145736 | tf_op jit(solution)/shard_map/ppermute | solution.py:735
  (128 other events, 2088.1 us)
Sparse Core Ops, SparseCore 0:
  15.9 135.8 all-gather.3
  153.3 104.2 all-gather.5
  259.9 60.3 all-gather.7

commit v3 on v2

--- a/solution.py
+++ b/solution.py
@@ -140,7 +140,7 @@
     cosine, sine, gains, tanh_lanes = tables
     rows, caps = raw.shape[0], text.shape[0]
     count = rows // 2
-    width = raw.shape[1] // 3
+    width = tanh_lanes.shape[1]
     f32, bf16 = jnp.float32, jnp.bfloat16
     fresh = kept is None
 
@@ -455,8 +455,9 @@
     )(query, kv, kv, raw, raw, own, lse, dmix, dq_cross, cosine, sine, gains)
 
 
-def feed_kernel(x_ref, grad_ref, gate_ref, up_ref, down_ref, hidden_ref, both_ref):
+def feed_kernel(x_ref, grad_ref, gate_ref, up_ref, down_ref, *refs):
     f32, bf16 = jnp.float32, jnp.bfloat16
+    hidden_ref, both_ref = refs[-2:]
     gate = jnp.dot(x_ref[...], gate_ref[...], preferred_element_type=f32)
     up = jnp.dot(x_ref[...], up_ref[...], preferred_element_type=f32)
     dhidden = jnp.dot(grad_ref[...], down_ref[...], preferred_element_type=f32)
@@ -468,31 +469,39 @@
     both_ref[:, tile:] = (dhidden * act).astype(bf16)
 
 
-def feed_forward(x, grad, weights, units, tile):
-    rows, depth = x.shape
-    count = units // tile
+def feed_forward(part, x, grad, weights, units, tile, kept=()):
+    count, depth = x.shape
+    rows = grad.shape[0]
+    blocks = units // tile
     bf16 = jnp.bfloat16
 
     def cols(scale, shift):
         return pl.BlockSpec((depth, tile), lambda j: (0, scale * j + shift))
 
-    whole = pl.BlockSpec((rows, depth), lambda j: (0, 0))
     return pl.pallas_call(
         feed_kernel,
-        grid=(count,),
-        in_specs=[whole, whole, cols(2, 0), cols(2, 1), cols(1, 2 * count)],
+        grid=(blocks,),
+        in_specs=[
+            pl.BlockSpec((count, depth), lambda j: (0, 0)),
+            pl.BlockSpec((count, depth), lambda j: (part, 0)),
+            cols(2, 0),
+            cols(2, 1),
+            cols(1, 2 * blocks),
+        ]
+        + [pl.BlockSpec(memory_space=pl.ANY)] * len(kept),
         out_specs=[
-            pl.BlockSpec((rows, tile), lambda j: (0, j)),
-            pl.BlockSpec((rows, 2 * tile), lambda j: (0, j)),
+            pl.BlockSpec((count, tile), lambda j: (part, j)),
+            pl.BlockSpec((count, 2 * tile), lambda j: (part, j)),
         ],
         out_shape=[
             jax.ShapeDtypeStruct((rows, units), bf16),
             jax.ShapeDtypeStruct((rows, 2 * units), bf16),
         ],
+        input_output_aliases={5 + n: n for n in range(len(kept))},
         compiler_params=pltpu.CompilerParams(vmem_limit_bytes=58 * 2**20),
         cost_estimate=LIGHT,
         name="feed_forward",
-    )(x, grad, weights, weights, weights)
+    )(x, grad, weights, weights, weights, *kept)
 
 
 def outer_kernel(size, bits, me_ref, left_ref, right_ref, keep_ref, away_ref, total_ref):
@@ -559,76 +568,12 @@
     )(left, right, *([] if add is None else [add]))
 
 
-def blank(shape, dtype):
-    return pl.pallas_call(
-        lambda out_ref: None,
-        out_specs=pl.BlockSpec(memory_space=pl.ANY),
-        out_shape=jax.ShapeDtypeStruct(shape, dtype),
-        name="blank",
-    )()
-
-
 def gated(value, *tokens):
     return lax.optimization_barrier((value,) + tokens)[0]
 
 
-def chip_ring(size):
-    depth = size // 4
-    return [2 * q if q < depth else 2 * (2 * depth - 1 - q) + 1 for q in range(size // 2)]
-
-
-def ring_perm(size, step):
-    order = chip_ring(size)
-    count = len(order)
-    return [
-        (order[q] * 2 + c, order[(q + step) % count] * 2 + c) for q in range(count) for c in range(2)
-    ]
-
-
 def flip_perm(size, bit):
     return [(i, i ^ bit) for i in range(size)]
-
-
-def ring_place(size):
-    depth = size // 4
-    index = lax.axis_index("dp")
-    chip = index // 2
-    level = chip // 2
-    return jnp.where(chip % 2 == 0, level, 2 * depth - 1 - level), index % 2
-
-
-def chip_at(place, size):
-    depth = size // 4
-    place = place % (2 * depth)
-    return jnp.where(place < depth, 2 * place, 2 * (2 * depth - 1 - place) + 1)
-
-
-def ring_gather(shard, size, hop):
-    count = size // 2
-    rows, cols = shard.shape
-    half = cols // 2
-    place, core = ring_place(size)
-    swap = flip_perm(size, 1)
-    ahead, behind = ring_perm(size, 1), ring_perm(size, -1)
-    pieces = [(0, 0, shard)]
-    fwd = bwd = shard
-    for step in range(1, count // 2):
-        fwd = lax.ppermute(fwd, "dp", ahead)
-        bwd = lax.ppermute(bwd, "dp", behind)
-        pieces += [(-step, 0, fwd), (step, 0, bwd)]
-        token = hop(fwd, bwd)
-        if token is not None:
-            fwd, bwd = gated((fwd, bwd), token)
-    last_f = lax.ppermute(fwd[:, :half], "dp", ahead)
-    last_b = lax.ppermute(bwd[:, half:], "dp", behind)
-    pieces += [(count // 2, 0, last_f), (count // 2, half, last_b)]
-    full = blank((count, 2, rows, cols), shard.dtype)
-    for offset, low, piece in pieces:
-        other = lax.ppermute(piece, "dp", swap)
-        chip = chip_at(place + offset, size)
-        full = lax.dynamic_update_slice(full, piece[None, None], (chip, core, 0, low))
-        full = lax.dynamic_update_slice(full, other[None, None], (chip, 1 - core, 0, low))
-    return full.reshape(size * rows, cols)
 
 
 class SmallScatter:
@@ -656,6 +601,7 @@
     def __init__(self, size, bits, keep, away):
         self.size, self.bits, self.stage = size, bits, 0
         self.terms = [keep]
+        self.whole = [keep]
         self.out = away
 
     def start(self):
@@ -668,7 +614,9 @@
         return self.came
 
     def finish(self, *tokens):
-        self.terms.append(gated(self.came, *tokens) if tokens else self.came)
+        came = gated(self.came, *tokens) if tokens else self.came
+        self.terms.append(came)
+        self.whole.append(came)
         rows = self.terms[-1].shape[0]
         last = self.stage == len(self.bits)
         half = rows if last else rows // 2
@@ -683,9 +631,8 @@
             self.finish(*tokens)
             self.start()
             tokens = ()
-        self.terms.append(gated(self.came, *tokens) if tokens else self.came)
-        rows = self.terms[-1].shape[0]
-        return [term[:rows] for term in self.terms]
+        came = gated(self.came, *tokens) if tokens else self.came
+        return self.whole + [came]
 
 
 def swap_start(part, size, chunks):
@@ -770,34 +717,154 @@
     )(*operands)
 
 
-def gather_sum_kernel(tile, count, terms, *refs):
-    total = refs[0][...].astype(jnp.float32)
-    for ref in refs[1:terms]:
-        total = total + ref[...].astype(jnp.float32)
-    outs = refs[terms:]
+def gather_sum_kernel(tile, sizes, count, *refs):
+    outs = refs[-count:]
     cols = outs[0].shape[1]
-    for i in range(-(-cols // tile)):
-        wide = min(tile, cols - i * tile)
-        for n, out_ref in enumerate(outs):
-            start = (i * count + n) * tile
-            out_ref[:, i * tile : i * tile + wide] = total[:, start : start + wide]
-
-
-def gather_sum(terms, tile, count, cols):
-    rows, wide = terms[0].shape
+    low = 0
+    base = 0
+    for size in sizes:
+        total = refs[low][...].astype(jnp.float32)
+        for ref in refs[low + 1 : low + size]:
+            total = total + ref[...].astype(jnp.float32)
+        low += size
+        tiles = total.shape[1] // (tile * count)
+        for i in range(tiles):
+            start = base + i * tile
+            wide = min(tile, cols - start)
+            for n, out_ref in enumerate(outs):
+                at = (i * count + n) * tile
+                out_ref[:, start : start + wide] = total[:, at : at + wide]
+        base += tiles * tile
+
+
+def gather_sum(groups, tile, count, cols):
+    rows = groups[0][-1].shape[0]
+    terms = [term for group in groups for term in group]
+    wide = sum(term.shape[1] for term in terms) * 2 + count * cols * 4
     block = rows
-    while block * wide * (2 * len(terms) + 8) > 24 * 2**20 and block % 32 == 0:
+    while block * wide > 12 * 2**20 and block % 32 == 0:
         block //= 2
     return pl.pallas_call(
-        functools.partial(gather_sum_kernel, tile, count, len(terms)),
+        functools.partial(gather_sum_kernel, tile, [len(group) for group in groups], count),
         grid=(rows // block,),
-        in_specs=[pl.BlockSpec((block, wide), lambda r: (r, 0)) for _ in terms],
+        in_specs=[pl.BlockSpec((block, term.shape[1]), lambda r: (r, 0)) for term in terms],
         out_specs=[pl.BlockSpec((block, cols), lambda r: (r, 0))] * count,
         out_shape=[jax.ShapeDtypeStruct((rows, cols), jnp.float32)] * count,
         compiler_params=pltpu.CompilerParams(vmem_limit_bytes=58 * 2**20),
         cost_estimate=LIGHT,
         name="gather_sum",
     )(*terms)
+
+
+def fold_plan(rows, blocks, tall):
+    plan = []
+    for block in range(blocks):
+        low = block * rows
+        while low < (block + 1) * rows:
+            high = min((block + 1) * rows, (low // tall + 1) * tall)
+            plan.append((block, low - block * rows, low % tall, low // tall, high - low))
+            low = high
+    return plan
+
+
+def pack_kernel(rows, tall, wide, plans, *refs):
+    out_ref = refs[-1]
+    out_ref[...] = jnp.zeros_like(out_ref)
+    text_plan, rest_plan = plans
+    for target, source, low, width, _ in text_plan:
+        out_ref[:, target : target + width] = refs[source][:, low : low + width]
+    for block, at, row, col, count in fold_plan(rows, len(rest_plan), tall):
+        source, low, width, turned = rest_plan[block]
+        if turned:
+            piece = refs[source][low : low + width, :].T
+        else:
+            piece = refs[source][:, low : low + width]
+        start = wide + col * LANES
+        out_ref[row : row + count, start : start + width] = piece[at : at + count]
+
+
+def pack_weights(text, attention, last):
+    tall, cols = text[0].shape
+    rows = attention[0].shape[0]
+    tiles = -(-cols // LANES)
+    text_plan = []
+    rest_plan = []
+    for i in range(tiles):
+        width = min(LANES, cols - i * LANES)
+        for n in range(len(text)):
+            target = (i * len(text) + n) * LANES
+            text_plan.append((target, n, i * LANES, width, False))
+        for n in range(len(attention)):
+            rest_plan.append((len(text) + n, i * LANES, width, False))
+    for i in range(tiles):
+        width = min(LANES, cols - i * LANES)
+        rest_plan.append((len(text) + len(attention), i * LANES, width, True))
+    wide = tiles * len(text) * LANES
+    folded = len(rest_plan) * rows // tall * LANES
+    return pl.pallas_call(
+        functools.partial(pack_kernel, rows, tall, wide, (text_plan, rest_plan)),
+        out_shape=jax.ShapeDtypeStruct((tall, wide + folded), text[0].dtype),
+        compiler_params=pltpu.CompilerParams(vmem_limit_bytes=30 * 2**20),
+        cost_estimate=LIGHT,
+        name="pack_weights",
+    )(*text, *attention, last)
+
+
+def unfold_kernel(rows, tall, blocks, size, edge, left_ref, *refs):
+    full_ref, raw_ref = refs[-2:]
+    plan = fold_plan(rows, blocks, tall)
+
+    def place(d, _):
+        start = pl.multiple_of(d * rows, 16)
+        for block, at, row, col, count in plan:
+            full_ref[pl.ds(start + at, count), block * LANES : (block + 1) * LANES] = refs[col][
+                d, row : row + count, :
+            ]
+        return 0
+
+    lax.fori_loop(0, size, place, 0)
+    last = pl.program_id(0) == pl.num_programs(0) - 1
+
+    @pl.when(jnp.logical_not(last))
+    def _():
+        raw_ref[...] = jnp.dot(left_ref[...], full_ref[...], preferred_element_type=jnp.float32)
+
+    @pl.when(last)
+    def _():
+        raw_ref[:, :edge] = jnp.dot(
+            left_ref[...], full_ref[:, :edge], preferred_element_type=jnp.float32
+        )
+
+
+def unfold_product(left, packed, rows, tall, blocks, used, size):
+    period = math.lcm(rows, tall)
+    span, folds = period // rows, period // tall
+    steps = blocks // span
+    skip = packed.shape[1] // LANES - folds * steps
+    tokens = left.shape[0]
+    view = packed.reshape(size, tall, packed.shape[1])
+    return pl.pallas_call(
+        functools.partial(
+            unfold_kernel, rows, tall, span, size, (used - (steps - 1) * span) * LANES
+        ),
+        grid=(steps,),
+        in_specs=[pl.BlockSpec(left.shape, lambda j: (0, 0))]
+        + [
+            pl.BlockSpec((size, tall, LANES), lambda j, k=k: (0, 0, skip + folds * j + k))
+            for k in range(folds)
+        ],
+        out_specs=[
+            pl.BlockSpec((size * rows, span * LANES), lambda j: (0, j)),
+            pl.BlockSpec((tokens, span * LANES), lambda j: (0, j)),
+        ],
+        out_shape=[
+            jax.ShapeDtypeStruct((size * rows, blocks * LANES), packed.dtype),
+            jax.ShapeDtypeStruct((tokens, blocks * LANES), jnp.float32),
+        ],
+        compiler_params=pltpu.CompilerParams(vmem_limit_bytes=58 * 2**20),
+        cost_estimate=LIGHT,
+        name="unfold_product",
+    )(left, *[view] * folds)
 
 
 def rotary_tables(row_pos, col_pos, quarter, repeat):
@@ -866,13 +933,11 @@
     )[None]
     steps = []
     small_all = small_gather(small, "dp", size, (), steps)
-    textkey_l, textval_l = gated((textkey_proj, textval_proj), steps[0])
-    text_shard = weave([textkey_l, textval_l], LANES)
-    text_set = lax.all_gather(text_shard, "dp", axis=0, tiled=True)
-    query_l, key_l, value_l, output_l = gated(
-        (query_proj, key_proj, value_proj, output_proj), steps[1]
-    )
-    first = weave([query_l, key_l, value_l], LANES, output_l)
+    packed = pack_weights(
+        gated([textkey_proj, textval_proj], steps[0]), [query_proj, key_proj, value_proj], output_proj
+    )
+    packed_set = lax.all_gather(packed, "dp", axis=0, tiled=True)
+
     cuts = [rows_w, 2 * rows_w, 2 * rows_w + head_part]
     gain_one = small_all[:, : cuts[0]].reshape(-1)
     gain_two = small_all[:, cuts[0] : cuts[1]].reshape(-1)
@@ -887,15 +952,13 @@
     cond_here = lax.dynamic_slice_in_dim(cond_all, dp_index * embed_rows, embed_rows, 1)
     mod_part = jnp.dot(cond_here, modulation, preferred_element_type=f32)
     mod_sums = SmallScatter(mod_part, size)
-    mod_sums.hop()
-    full_qkvo = ring_gather(gated(first, small_all), size, mod_sums.hop)
     while mod_sums.left():
         mod_sums.hop()
     mod_here = mod_sums.value
     mod_all = small_gather(mod_here, "tensor", groups).reshape(1, -1)
     tile = 256
     blocks = units // tile
-    gate_l, up_l, down_l = gated((gate_proj, up_proj, down_proj), first)
+    gate_l, up_l, down_l = gated((gate_proj, up_proj, down_proj), small_all)
     third = weave([gate_l, up_l], tile, down_l)
     ffn_set = lax.all_gather(gated(third, small_all), "dp", axis=0, tiled=True)
     scale_one = mod_all[:, 0:model_dim]
@@ -916,10 +979,14 @@
     factor_one = inv_rms(resid_in)
     normed_one = resid_in * factor_one
     attn_in = (normed_one * gain_one * (1.0 + scale_one)).astype(bf16)
-    qkv_raw = product(attn_in, full_qkvo, 3 * padded, 3 * LANES, f32)
+    grad_out = cotangent.astype(f32)
+    grad_ffn = (gate_two * grad_out).astype(bf16)
+    full_text = gated(packed_set, attn_in, grad_ffn)
+    full_qkvo, qkv_raw = unfold_product(
+        attn_in, full_text, rows_w, packed.shape[0], 4 * pairs, 3 * pairs, size
+    )
     cap_in = caption[0]
-    full_text = gated(text_set, qkv_raw)
-    text_raw = product(cap_in, full_text, 2 * padded, 256, f32)
+    text_raw = product(gated(cap_in, qkv_raw), full_text, 2 * padded, 256, f32)
     mixed_a, query_bf, own_out, cross_out, lse, kv_bf, tkv_bf = attend_rows(
         0, caption_lens, qkv_raw, text_raw, tables, head_dim
     )
@@ -931,33 +998,41 @@
     )
     attn_part = product(mixed_b, full_qkvo, model_dim, 512, bf16, True, 3)
     mixed_heads = jnp.concatenate([mixed_a, mixed_b], axis=0)
-    mod_set = lax.all_gather(gated(modulation, attn_part), "dp", axis=0, tiled=True)
-
-    grad_out = gated(cotangent, attn_part).astype(f32)
-    grad_ffn = (gate_two * grad_out).astype(bf16)
-    came_a = gated(came_a, grad_ffn)
+    mod_set = lax.all_gather(gated(modulation, qkv_raw), "dp", axis=0, tiled=True)
+
+    came_a = gated(came_a, attn_part)
     own_b, came_b = swap_start(gated(attn_part, came_a), groups, 1)
-    came_b = gated(came_b, came_a)
-    attn_out = jnp.concatenate(
-        [swap_end(own_a, came_a, groups), swap_end(own_b, came_b, groups)], axis=0
-    )
+    half_rows = grad_ffn.shape[0] // 2
+    full_ffn = gated(ffn_set, attn_part)
+    gain_mul = gain_two * (1.0 + scale_two)
+
+    def feed_input(resid, own, came):
+        attn_sum = swap_end(own, came, groups)
+        total = resid + gate_one * attn_sum
+        factor = inv_rms(total)
+        normed = total * factor
+        return attn_sum, total, factor, normed, (normed * gain_mul).astype(bf16)
+
+    resid_a, resid_b = resid_in[:half_rows], resid_in[half_rows:]
+    attn_out_a, residual_a, factor_a, normed_a, feed_a = feed_input(resid_a, own_a, came_a)
+    kept = feed_forward(0, feed_a, grad_ffn, full_ffn, units, tile)
+    dffn_one = product(kept[1], full_ffn, model_dim, 512, bf16, True, 0, None, (0, 2))
+    one_own, one_came = swap_start(dffn_one, groups, 1)
+    came_b = gated(came_b, dffn_one)
+    attn_out_b, residual_b, factor_b, normed_b, feed_b = feed_input(resid_b, own_b, came_b)
+    hidden, dboth = feed_forward(
+        1, feed_b, grad_ffn, full_ffn, units, tile, gated(kept, dffn_one)
+    )
+    dffn_two = product(dboth, full_ffn, model_dim, 512, bf16, True, 0, None, (1, 2))
+    ffn_in = jnp.concatenate([feed_a, feed_b], axis=0)
     me = dp_index.astype(jnp.int32)[None]
     depth_bits = list(range(2, size.bit_length() - 1))
     side_first = [0, 1] + depth_bits
     line_first = [0, 2, 1] + depth_bits[1:]
 
-    residual = resid_in + gate_one * attn_out
-    factor_two = inv_rms(residual)
-    normed_two = residual * factor_two
-    ffn_in = (normed_two * gain_two * (1.0 + scale_two)).astype(bf16)
-    full_ffn = gated(ffn_set, attn_part)
-    hidden, dboth = feed_forward(ffn_in, grad_ffn, full_ffn, units, tile)
     def staged(left, right, bits, tile_cols):
         return Halving(size, bits, *outer_grads(me, left, right, size, bits, tile_cols))
 
-    dffn_one = product(dboth, full_ffn, model_dim, 512, bf16, True, 0, None, (0, 2))
-    dffn_two = product(gated(dboth, dffn_one), full_ffn, model_dim, 512, bf16, True, 0, None, (1, 2))
-    one_own, one_came = swap_start(dffn_one, groups, 1)
     down = staged(grad_ffn, gated(hidden, dffn_two), line_first, 512)
     down.start()
     one_came = gated(one_came, down.out)
@@ -965,23 +1040,37 @@
     grown = staged(ffn_in, gated(dboth, down.out, one_came), side_first, 512)
     grown.start()
     ffn_part = product(gated(hidden, grown.out, mod_set), full_ffn, model_dim, 512, bf16, True, 2)
-    two_came = gated(two_came, ffn_part)
+    grad_out_a, grad_out_b = grad_out[:half_rows], grad_out[half_rows:]
+
+    def feed_back(grad, own, came, normed, factor, attn_sum):
+        dffn = swap_end(own, came, groups)
+        dres = grad + norm_back(dffn * gain_mul, normed, factor)
+        sums_here = jnp.sum(dffn * normed, axis=0), jnp.sum(dres * attn_sum, axis=0)
+        return dres, (gate_one * dres).astype(bf16), sums_here
+
+    dres_a, grad_attn_a, sums_a = feed_back(
+        grad_out_a, one_own, one_came, normed_a, factor_a, attn_out_a
+    )
+    dmix_a = product(
+        gated(grad_attn_a, ffn_part), full_qkvo, padded, LANES, bf16, False, 3 * padded // LANES
+    )
+    two_came = gated(two_came, dmix_a)
     down.finish(two_came)
     down.start()
     grown.finish(down.out)
     grown.start()
-    dffn_in = jnp.concatenate(
-        [swap_end(one_own, one_came, groups), swap_end(two_own, two_came, groups)], axis=0
-    )
-
-    gain_mul = gain_two * (1.0 + scale_two)
-    weighed = jnp.sum(dffn_in * normed_two, axis=0)
+    dres_b, grad_attn_b, sums_b = feed_back(
+        grad_out_b, two_own, gated(two_came, grown.out), normed_b, factor_b, attn_out_b
+    )
+    dmix_b = product(grad_attn_b, full_qkvo, padded, LANES, bf16, False, 3 * padded // LANES)
+    dmixed = jnp.concatenate([dmix_a, dmix_b], axis=0)
+    grad_attn = jnp.concatenate([grad_attn_a, grad_attn_b], axis=0)
+    weighed = sums_a[0] + sums_b[0]
     grad_gaintwo = weighed * (1.0 + scale_two[0])
     dscale_two = weighed * gain_two
-    dresid = grad_out + norm_back(dffn_in * gain_mul, normed_two, factor_two)
-    dgate_one = jnp.sum(dresid * attn_out, axis=0) * (1.0 - gate_one[0] ** 2)
-    grad_attn = (gate_one * dresid).astype(bf16)
-    dmixed = product(grad_attn, full_qkvo, padded, LANES, bf16, False, 3 * padded // LANES)
+    dgate_one = (sums_a[1] + sums_b[1]) * (1.0 - gate_one[0] ** 2)
+    dresid = jnp.concatenate([dres_a, dres_b], axis=0)
+    residual = jnp.concatenate([residual_a, residual_b], axis=0)
     ffn_own, ffn_came = swap_start(gated(ffn_part, dmixed), groups, 1)
     dq_cross, dtext, stats_c = cross_back(
         caption_lens, query_bf, tkv_bf, text_raw, cross_out, lse, dmixed, tables, head_dim
@@ -996,7 +1085,6 @@
     windows = [(0, split), (split, pairs - split)]
     common = (query_bf, kv_bf, qkv_raw, own_out, lse)
     dmixed_a = gated(dmixed, text.out)
-    gate_part = jnp.sum(grad_out * gated(ffn_part, dmixed).astype(f32), axis=0)
     dqkv_a, stats_a = self_back(windows[0], *common, dmixed_a, dq_cross, tables, head_dim)
     down.finish(dqkv_a)
     down.start()
@@ -1004,7 +1092,7 @@
     grown.start()
     text.finish(grown.out)
     text.start()
-    first_qkv = staged(attn_in, gated(dqkv_a, text.out), line_first, 3 * LANES)
+    first_qkv = staged(attn_in, gated(dqkv_a, text.out), side_first, 3 * LANES)
     first_qkv.start()
     outp = staged(gated(grad_attn, first_qkv.out), mixed_heads, side_first, padded)
     outp.start()
@@ -1013,14 +1101,14 @@
     wide_a = full_qkvo if even else full_qkvo[:, :edge]
     wide_b = full_qkvo if even else full_qkvo[:, edge : 3 * padded]
     dattn_a = product(gated(dqkv_a, outp.out), wide_a, model_dim, 512, f32, True)
-    dmixed_b = gated(dmixed, dattn_a, gate_part)
+    dmixed_b = gated(dmixed, dattn_a)
     dqkv_b, stats_b = self_back(windows[1], *common, dmixed_b, dq_cross, tables, head_dim)
     landed = (down.land(dqkv_b), grown.land(dqkv_b), gated(ffn_came, dqkv_b))
     ffn_came = landed[2]
     dqkv_l = gated(dqkv_b, *landed)
     dattn_part = product(dqkv_l, wide_b, model_dim, 512, bf16, True, int(even), dattn_a)
-    half_rows = dattn_part.shape[0] // 2
-    high_own, high_came = swap_start(dattn_part[:half_rows], groups, 1)
+    cut = dattn_part.shape[0] * 5 // 8
+    high_own, high_came = swap_start(dattn_part[:cut], groups, 1)
     last_qkv = staged(attn_in, gated(dqkv_b, dattn_part), side_first, 3 * LANES)
     last_qkv.start()
     text.finish(last_qkv.out)
@@ -1029,22 +1117,30 @@
     first_qkv.start()
     outp.finish(first_qkv.out)
     outp.start()
-    caption_part = product(gated(dtext, outp.out), full_text, cap_in.shape[1], 1024, bf16, True)
-    high_came = gated(high_came, caption_part)
-    base_own, base_came = swap_start(gated(dattn_part[half_rows:], high_came), groups, 1)
+    last_qkv.finish(outp.out)
+    last_qkv.start()
+    caption_part = product(
+        gated(dtext, last_qkv.out), full_text, cap_in.shape[1], 1024, bf16, True
+    )
+    grad_gate, grad_up = gather_sum([grown.drain(caption_part)], tile, 2, units)
+    high_came = gated(high_came, grad_gate)
+    base_own, base_came = swap_start(gated(dattn_part[cut:], high_came), groups, 1)
     last_qkv.finish(high_came)
     last_qkv.start()
-    weighed_part = jnp.sum(gated(dattn_part, last_qkv.out).astype(f32) * normed_one, axis=0)
-    grad_gate, grad_up = gather_sum(grown.drain(last_qkv.out), tile, 2, units)
-    down_terms = down.drain(grad_gate)
-    down_t = sum(term.astype(f32) for term in down_terms)
-    text.finish(down_t)
+    outp.finish(last_qkv.out)
+    outp.start()
+    down_t = sum(term[:rows_w].astype(f32) for term in down.drain(outp.out))
+    ffn_out = swap_end(ffn_own, gated(ffn_came, down_t), groups)
+    output = (residual + gate_two * ffn_out).astype(bf16)
+    weighed_part = jnp.sum(gated(dattn_part, output).astype(f32) * normed_one, axis=0)
+    gate_part = jnp.sum(grad_out * gated(ffn_part, weighed_part).astype(f32), axis=0)
+    text.finish(gate_part)
     text.start()
-    outp.finish(text.out)
-    outp.start()
-    first_qkv.finish(outp.out)
+    first_qkv.finish(text.out)
     first_qkv.start()
-    base_came = gated(base_came, first_qkv.out)
+    last_qkv.finish(first_qkv.out)
+    last_qkv.start()
+    base_came = gated(base_came, last_qkv.out)
     stats = jnp.concatenate([stats_a, stats_b], axis=1)[:2]
     stat_sums = jnp.concatenate([stats, stats_c[:2]], axis=0)[:, :chan]
     stat_sums = jnp.sum(stat_sums.reshape(4, heads_here, head_dim), axis=(1,))
@@ -1058,9 +1154,11 @@
     grad_latents = (
         dresid + norm_back(dattn_in * gain_one * (1.0 + scale_one), normed_one, factor_one)
     ).astype(bf16)
-    last_qkv.finish(grad_latents)
-    last_qkv.start()
-    sums = gated(sums, last_qkv.out)
+    outp.finish(grad_latents)
+    outp.start()
+    first_qkv.finish(outp.out)
+    first_qkv.start()
+    sums = gated(sums, first_qkv.out)
     weighed_one, head_gains = sums[:model_dim], sums[2 * model_dim :]
     dgate_two = sums[model_dim : 2 * model_dim] * (1.0 - gate_two[0] ** 2)
     grad_gainone = weighed_one * (1.0 + scale_one[0])
@@ -1071,19 +1169,11 @@
     row = jnp.concatenate([dmod_here, grad_gainone, grad_gaintwo, head_gains, xgate_here])
     row = row.astype(bf16).astype(f32)[None]
     dcaption = tensor_scatter(gated(caption_part, sums), groups)
-    ffn_out = swap_end(ffn_own, gated(ffn_came, row), groups)
-    output = (residual + gate_two * ffn_out).astype(bf16)
     embed_row = jnp.einsum(
         "bc,tc->bt", row[:, :cols_here].astype(bf16), mod_set, preferred_element_type=f32
     )
-    first_qkv.finish(output)
-    first_qkv.start()
-    outp.finish(first_qkv.out)
-    outp.start()
-    rows_set = small_gather(row, "dp", size, [row, output, first_qkv.out, outp.out])
-    grad_textkey, grad_textval = gather_sum(text.drain(outp.out), LANES, 2, chan)
-    last_qkv.finish(grad_textkey)
-    last_qkv.start()
+    rows_set = small_gather(row, "dp", size)
+    grad_textkey, grad_textval = gather_sum([text.drain(row)], LANES, 2, chan)
     dmod_set = rows_set[:, :cols_here].astype(bf16)
     gain_sums = jnp.sum(rows_set[:, cols_here:], axis=0)
     grad_modul = jnp.einsum("bt,bc->tc", cond_here, dmod_set, preferred_element_type=f32)
@@ -1093,13 +1183,9 @@
     dembed_all = embed_sum * (sig_own * (1.0 + embed_own * (1.0 - sig_own)))
     width = embed_dim // groups
     dembed = lax.dynamic_slice_in_dim(dembed_all, tensor_index * width, width, 1)
-    output_t = sum(term.astype(f32) for term in outp.drain(last_qkv.out))
-    wide = min(split * LANES, chan)
-    parts_a = gather_sum(first_qkv.drain(output_t), LANES, 3, wide)
-    parts_b = gather_sum(last_qkv.drain(parts_a[0]), LANES, 3, chan - wide)
-    grad_query, grad_key, grad_value = [
-        jnp.concatenate([one, two], axis=1) for one, two in zip(parts_a, parts_b)
-    ]
+    output_t = sum(term[:rows_w].astype(f32) for term in outp.drain(grad_textkey))
+    parts = [last_qkv.drain(output_t), first_qkv.drain(output_t)][::-1]
+    grad_query, grad_key, grad_value = gather_sum(parts, LANES, 3, chan)
 
     def own_part(start, width):
         return lax.dynamic_slice_in_dim(gain_sums, start + dp_index * width, width, 0)

time: 869 us -> 779 us (0.90)
  waiting for transfers between devices: 250 us -> 182 us
  local copies, waits for them, and re-layouts: 74.8 us -> 41.7 us
  Pallas kernels: 332 us -> 345 us
    ppermute x17 -> x0, waiting for transfers between devices: 98.4 us -> none  [the longest x3 45 us: ring_gather(): fwd = lax.ppermute(fwd, 'dp', ahead)]
    all_gather x2, waiting for transfers between devices: 0.01 us -> 73.4 us  [the longest x1 73.4 us: local(): packed_set = lax.all_gather(packed, 'dp', axis=0, tiled=True)]
    ppermute x7, waiting for transfers between devices: 101 us -> 29.7 us  [swap_start(): return (own, [lax.ppermute(o, 'tensor', flip_perm(size, 1)) for o in own])]
    pallas_call x6 -> x7, Pallas kernels: 38.5 us -> 62.9 us  [the longest x2 34.5 us: feed_forward(): pl.pallas_call(feed_kernel, grid=(blocks,), in_specs=[pl.BlockSpec((count...]
    slice x19 -> x2, local copies, waits for them, and re-layouts: 27.8 us -> 5.29 us  [the longest x1 2.94 us: local(): high_own, high_came = swap_start(dattn_part[:cut], groups, 1)]
    dynamic_update_slice x18 -> x0, local copies, waits for them, and re-layouts: 19.4 us -> none  [the longest x9 10.7 us: ring_gather(): lax.dynamic_update_slice(full, piece[None, None], (chip, core, 0, low))]
    ppermute x9, waiting for transfers between devices: 15.2 us -> 26.7 us  [small_gather(): came = lax.ppermute(value, name, flip_perm(size, bit))]
    pallas_call x11, Pallas kernels: 104 us -> 94 us  [product(): pl.pallas_call(functools.partial(product_kernel, turned, add is not None)...]
  transfers between devices with their start and end apart: 67 -> 50, of which waited for: 26 -> 20; matrix products, arithmetic and copies ran while one was open for 21% -> 18% of each run, Pallas kernels for 37% -> 43%
where the time goes in v3:
time: 779 us; the launch traced here: 773 us
  Pallas kernels  345 us (44%)
  waiting for transfers between devices  182 us (23%)
  other arithmetic  127 us (16%)
  starting transfers between devices  53.9 us (7%)
  local copies, waits for them, and re-layouts  41.7 us (5%)
  between operations  16.9 us (2%)
    pallas_call x11, Pallas kernels, product(): pl.pallas_call(functools.partial(product_kernel, turned, add is not None)...  94 us
    all_gather x1, waiting for transfers between devices, local(): packed_set = lax.all_gather(packed, 'dp', axis=0, tiled=True)  73.4 us
    pallas_call x6, Pallas kernels, outer_grads(): pl.pallas_call(functools.partial(outer_kernel, size, bits), grid=(cols //...  63.9 us
    pallas_call x2, Pallas kernels, self_back(): pl.pallas_call(functools.partial(self_back_kernel, half, min(512, rows)),...  62.1 us
    convert_element_type x18, other arithmetic, finish(): self.out = total if last else total.astype(jnp.bfloat16)  49 us
    pallas_call x2, Pallas kernels, attend_rows(): pl.pallas_call(functools.partial(attend_kernel, half, min(256, count), fr...  40 us
    pallas_call x2, Pallas kernels, feed_forward(): pl.pallas_call(feed_kernel, grid=(blocks,), in_specs=[pl.BlockSpec((count...  34.5 us
    ppermute x7, waiting for transfers between devices, swap_start(): return (own, [lax.ppermute(o, 'tensor', flip_perm(size, 1)) for o in own])  29.7 us
  transfers between devices with their start and end apart: 50, of which 20 were waited for; matrix products, arithmetic and copies ran while one was open for 18% of the time, Pallas kernels for 43%

profile of v3, /device:TPU:0, one launch (start us, length us, event | category | flops | bytes accessed | tf_op | source)
XLA Modules:
  0.0 773.1 jit_solution(5756455338581852761)
XLA Ops:
  63.0 73.4 %all-gather.4.cloned.1.call-done.refs_1_ = bf16[4096,2688]{1,0:T(8,128)(2,1)} async-done(((bf16[256,2688]{1,0:T(8,128)(2,1)}), bf16[4096,2688]{1,0:T(8,128)(2,1)}) %all-gather.4.cloned.1.call-update) | async-done | bytes 22020112 | tf_op jit(solution)/shard_map/all_gather | solution.py:939
  136.4 17.0 %unfold_product.1 = (bf16[1536,3072]{1,0:T(8,128)(2,1)}, f32[1024,3072]{1,0:T(8,128)}) custom-call(bf16[1024,1536]{1,0:T(8,128)(2,1)} %get-tuple-element.307.left_ref, bf16[16,256,2688]{2,1,0:T(8,128)(2,1)} %bitcast.56, bf16[16,256,2688]{2,1,0:T(8,128)(2,1)} %bitcast.57, bf16[16,256,2688]{2,1,0:T(8,128)(2,1)} %bitcast.58), custom_call_target="tpu_custom_call" | custom-call | flops 1 | bytes 1 | tf_op jit(solution)/shard_map/unfold_product/pallas_call | solution.py:846
  155.8 9.8 %product.11.refs_4_.refs_5_.text_ref = f32[256,1536]{1,0:T(8,128)} custom-call(bf16[256,4096]{1,0:T(8,128)(2,1)} %bitcast.54, bf16[4096,2688]{1,0:T(8,128)(2,1)} %all-gather.4.cloned.1.call-done.refs_1_), custom_call_target="tpu_custom_call" | custom-call | flops 1 | bytes 1 | tf_op jit(solution)/shard_map/product/pallas_call | solution.py:559
  165.7 21.7 %attend_fwd.2 = (bf16[512,768]{1,0:T(8,128)(2,1)S(1)}, bf16[1024,768]{1,0:T(8,128)(2,1)}, f32[1024,768]{1,0:T(8,128)}, f32[1024,768]{1,0:T(8,128)}, f32[1024,153...) custom-call(s32[1]{0:T(128)S(6)} %copy.150.refs_0_.len_ref, ...), custom_call_target="tpu_custom_call" | custom-call | flops 1 | bytes 1 | tf_op jit(solution)/shard_map/attend_fwd/pallas_call | solution.py:189
  194.8 18.3 %attend_fwd.3 = (bf16[512,768]{1,0:T(8,128)(2,1)S(1)}, bf16[1024,768]{1,0:T(8,128)(2,1)}, f32[1024,768]{1,0:T(8,128)}, f32[1024,768]{1,0:T(8,128)}, f32[1024,1536]{1,0:T(8,128)}) custom-call(s32[1]{0:T(128)S(6)} %copy.150.refs_0_.len_ref, ...), custom_call_target="tpu_custom_call", output_to_operand_aliasing={{1}: (8, {}), {2}: (9, {}), {3}: (10, {}), {4}: (11, {})} | custom-call | flops 1 | bytes 1 | tf_op jit(solution)/shard_map/attend_fwd/pallas_call | solution.py:189
  218.9 11.6 %collective-permute-done.9 = bf16[512,1536]{1,0:T(8,128)(2,1)} collective-permute-done((bf16[512,1536]{1,0:T(8,128)(2,1)}, bf16[512,1536]{1,0:T(8,128)(2,1)}, u32[]{:S(2)}, u32[]{:S(2)}) %collective-permute-start.9) | collective-permute-done | bytes 1572896 | tf_op jit(solution)/shard_map/ppermute | solution.py:642
  243.4 17.3 %feed_forward.2 = (bf16[1024,2048]{1,0:T(8,128)(2,1)}, bf16[1024,4096]{1,0:T(8,128)(2,1)}) custom-call(bf16[512,1536]{1,0:T(8,128)(2,1)} %multiply_convert_fusion.5.x_ref, bf16[1024,1536]{1,0:T(8,128)(2,1)} %get-tuple-element.306.grad_ref.left_ref, bf16[1536,6144]{1,0:T(8,128)(2,1)} %all-gather.6.cloned.1.call-done.gate_ref.up_ref.down_ref.refs_1_, ...), custom_call_target="tpu_custom_call" | custom-call | flops 1 | bytes 1 | tf_op jit(solution)/shard_map/feed_forward/pallas_call | solution.py:481
  260.7 11.6 %product.14 = bf16[512,1536]{1,0:T(8,128)(2,1)} custom-call(bf16[1024,4096]{1,0:T(8,128)(2,1)} %get-tuple-element.170.refs_0_.refs_1_, bf16[1536,6144]{1,0:T(8,128)(2,1)} %all-gather.6.cloned.1.call-done.gate_ref.up_ref.down_ref.refs_1_), custom_call_target="tpu_custom_call" | custom-call | flops 1 | bytes 1 | tf_op jit(solution)/shard_map/product/pallas_call | solution.py:559
  280.2 17.2 %feed_forward.3 = (bf16[1024,2048]{1,0:T(8,128)(2,1)}, bf16[1024,4096]{1,0:T(8,128)(2,1)}) custom-call(bf16[512,1536]{1,0:T(8,128)(2,1)} %multiply_convert_fusion.4.x_ref, bf16[1024,1536]{1,0:T(8,128)(2,1)} %get-tuple-element.306.grad_ref.left_ref, ...), custom_call_target="tpu_custom_call", output_to_operand_aliasing={{0}: (5, {}), {1}: (6, {})} | custom-call | flops 1 | bytes 1 | tf_op jit(solution)/shard_map/feed_forward/pallas_call | solution.py:481
  297.3 11.6 %product.15 = bf16[512,1536]{1,0:T(8,128)(2,1)} custom-call(bf16[1024,4096]{1,0:T(8,128)(2,1)} %get-tuple-element.176.refs_0_.right_ref, bf16[1536,6144]{1,0:T(8,128)(2,1)} %all-gather.6.cloned.1.call-done.gate_ref.up_ref.down_ref.refs_1_), custom_call_target="tpu_custom_call" | custom-call | flops 1 | bytes 1 | tf_op jit(solution)/shard_map/product/pallas_call | solution.py:559
  308.9 11.5 %outer_grads.6 = (bf16[768,2048]{1,0:T(8,128)(2,1)S(1)}, bf16[768,2048]{1,0:T(8,128)(2,1)}) custom-call(s32[1]{0:T(128)} %bitcast.13.me_ref, bf16[1024,1536]{1,0:T(8,128)(2,1)} %get-tuple-element.306.grad_ref.left_ref, bf16[1024,2048]{1,0:T(8,128)(2,1)} %get-tuple-element.179.right_ref.refs_0_), custom_call_target="tpu_custom_call" | custom-call | flops 1 | bytes 1 | tf_op jit(solution)/shard_map/outer_grads/pallas_call | solution.py:523
  320.7 19.8 %outer_grads.7 = (bf16[768,4096]{1,0:T(8,128)(2,1)}, bf16[768,4096]{1,0:T(8,128)(2,1)}) custom-call(s32[1]{0:T(128)} %bitcast.13.me_ref, bf16[1024,1536]{1,0:T(8,128)(2,1)S(1)} %pad_maximum_fusion.left_ref, bf16[1024,4096]{1,0:T(8,128)(2,1)} %get-tuple-element.176.refs_0_.right_ref), custom_call_target="tpu_custom_call" | custom-call | flops 1 | bytes 1 | tf_op jit(solution)/shard_map/outer_grads/pallas_call | solution.py:523
  354.3 10.9 %product.16 = bf16[1024,1536]{1,0:T(8,128)(2,1)} custom-call(bf16[1024,2048]{1,0:T(8,128)(2,1)} %get-tuple-element.179.right_ref.refs_0_, bf16[1536,6144]{1,0:T(8,128)(2,1)} %all-gather.6.cloned.1.call-done.gate_ref.up_ref.down_ref.refs_1_), custom_call_target="tpu_custom_call" | custom-call | flops 1 | bytes 1 | tf_op jit(solution)/shard_map/product/pallas_call | solution.py:559
  412.0 21.3 %cross_bwd.1 = (f32[1024,768]{1,0:T(8,128)S(1)}, bf16[256,1536]{1,0:T(8,128)(2,1)S(1)}, f32[8,768]{1,0:T(8,128)S(1)}) custom-call(s32[1]{0:T(128)S(6)} %copy.150.refs_0_.len_ref, bf16[1024,768]{1,0:T(8,128)(2,1)S(1)} %copy-done, bf16[256,1536]{1,0:T(8,128)(2,1)S(1)} %copy-done.15, f32[256,1536]{1,0:T(8,128)S(1)} %copy-done.2, f32[1024,768]{1,0:T(8,128)S(1)} %copy-done.8, ...), custom_call_target="tpu_custom_call" | custom-call | flops 1 | bytes 1 | tf_op jit(solution)/shard_map/cross_bwd/pallas_call | solution.py:390
  436.8 20.9 %collective-permute-done.16.refs_2_ = bf16[384,4096]{1,0:T(8,128)(2,1)} collective-permute-done((bf16[384,4096]{1,0:T(8,128)(2,1)}, bf16[384,4096]{1,0:T(8,128)(2,1)}, u32[]{:S(2)}, u32[]{:S(2)}) %collective-permute-start.16) | collective-permute-done | bytes 3145760 | tf_op jit(solution)/shard_map/ppermute | solution.py:609
  472.9 31.0 %self_bwd.2 = (bf16[1024,1152]{1,0:T(8,128)(2,1)}, f32[8,384]{1,0:T(8,128)S(1)}) custom-call(bf16[1024,768]{1,0:T(8,128)(2,1)S(1)} %copy-done, bf16[1024,1536]{1,0:T(8,128)(2,1)} %get-tuple-element.152.refs_2_.key_ref.val_ref, bf16[1024,1536]{1,0:T(8,128)(2,1)} %get-tuple-element.152.refs_2_.key_ref.val_ref, ...), custom_call_target="tpu_custom_call" | custom-call | flops 1 | bytes 1 | tf_op jit(solution)/shard_map/self_bwd/pallas_call | solution.py:428
  520.1 9.1 %outer_grads.9 = (bf16[768,1152]{1,0:T(8,128)(2,1)S(1)}, bf16[768,1152]{1,0:T(8,128)(2,1)}) custom-call(s32[1]{0:T(128)} %bitcast.13.me_ref, bf16[1024,1536]{1,0:T(8,128)(2,1)} %get-tuple-element.307.left_ref, bf16[1024,1152]{1,0:T(8,128)(2,1)} %get-tuple-element.209.right_ref.refs_0_), custom_call_target="tpu_custom_call" | custom-call | flops 1 | bytes 1 | tf_op jit(solution)/shard_map/outer_grads/pallas_call | solution.py:523
  540.4 8.6 %product.19.refs_2_ = f32[1024,1536]{1,0:T(8,128)} custom-call(bf16[1024,1152]{1,0:T(8,128)(2,1)} %get-tuple-element.209.right_ref.refs_0_, bf16[1536,3072]{1,0:T(8,128)(2,1)} %get-tuple-element.145.refs_1_), custom_call_target="tpu_custom_call" | custom-call | flops 1 | bytes 1 | tf_op jit(solution)/shard_map/product/pallas_call | solution.py:559
  549.0 31.1 %self_bwd.3 = (bf16[1024,1152]{1,0:T(8,128)(2,1)}, f32[8,384]{1,0:T(8,128)S(1)}) custom-call(bf16[1024,768]{1,0:T(8,128)(2,1)S(1)} %copy-done, bf16[1024,1536]{1,0:T(8,128)(2,1)} %get-tuple-element.152.refs_2_.key_ref.val_ref, bf16[1024,1536]{1,0:T(8,128)(2,1)} %get-tuple-element.152.refs_2_.key_ref.val_ref, ...), custom_call_target="tpu_custom_call" | custom-call | flops 1 | bytes 1 | tf_op jit(solution)/shard_map/self_bwd/pallas_call | solution.py:428
  581.6 9.5 %product.20 = bf16[1024,1536]{1,0:T(8,128)(2,1)} custom-call(bf16[1024,1152]{1,0:T(8,128)(2,1)} %get-tuple-element.218.refs_0_.right_ref, bf16[1536,3072]{1,0:T(8,128)(2,1)} %get-tuple-element.145.refs_1_, f32[1024,1536]{1,0:T(8,128)} %product.19.refs_2_), custom_call_target="tpu_custom_call" | custom-call | flops 1 | bytes 1 | tf_op jit(solution)/shard_map/product/pallas_call | solution.py:559
  591.1 9.1 %outer_grads.11 = (bf16[768,1152]{1,0:T(8,128)(2,1)S(1)}, bf16[768,1152]{1,0:T(8,128)(2,1)}) custom-call(s32[1]{0:T(128)} %bitcast.13.me_ref, bf16[1024,1536]{1,0:T(8,128)(2,1)} %get-tuple-element.307.left_ref, bf16[1024,1152]{1,0:T(8,128)(2,1)} %get-tuple-element.218.refs_0_.right_ref), custom_call_target="tpu_custom_call" | custom-call | flops 1 | bytes 1 | tf_op jit(solution)/shard_map/outer_grads/pallas_call | solution.py:523
  639.5 11.4 %collective-permute-done.29 = bf16[640,1536]{1,0:T(8,128)(2,1)} collective-permute-done((bf16[640,1536]{1,0:T(8,128)(2,1)}, bf16[640,1536]{1,0:T(8,128)(2,1)}, u32[]{:S(2)}, u32[]{:S(2)}) %collective-permute-start.29) | collective-permute-done | bytes 1966112 | tf_op jit(solution)/shard_map/ppermute | solution.py:642
  723.8 16.1 %collective-permute-done.45 = f32[4,6348]{1,0:T(4,128)S(1)} collective-permute-done((f32[4,6348]{1,0:T(4,128)S(1)}, f32[4,6348]{1,0:T(4,128)S(1)}, u32[]{:S(2)}, u32[]{:S(2)}) %collective-permute-start.45) | collective-permute-done | bytes 101600 | tf_op jit(solution)/shard_map/ppermute | solution.py:658
  755.9 9.1 %collective-permute-done.37 = bf16[256,2048]{1,0:T(8,128)(2,1)S(1)} collective-permute-done((bf16[256,2048]{1,0:T(8,128)(2,1)S(1)}, bf16[256,2048]{1,0:T(8,128)(2,1)S(1)}, u32[]{:S(2)}, u32[]{:S(2)}) %collective-permute-start.37) | collective-permute-done | bytes 1048608 | tf_op jit(solution)/shard_map/ppermute | solution.py:682
  (487 shorter events, 327.5 us)
Async XLA Ops:
  7.2 129.1 %all-gather.4.cloned.1.call-start = ((), (), s32[]{:S(2)}) async-start(), calls=%async_computation | async-start | bytes 23396352 | tf_op jit(solution)/shard_map/all_gather | solution.py:939
  19.1 218.0 %all-gather.6.cloned.1.call-start = ((), (), s32[]{:S(2)}) async-start(), calls=%async_computation.1 | async-start | bytes 20054016 | tf_op jit(solution)/shard_map/all_gather | solution.py:963
  33.6 320.7 %all-gather.8.cloned.1.call-start = ((), (), s32[]{:S(2)}) async-start(), calls=%async_computation.2 | async-start | bytes 6684672 | tf_op jit(solution)/shard_map/all_gather | solution.py:1001
  193.3 37.2 %collective-permute-start.9 = (bf16[512,1536]{1,0:T(8,128)(2,1)}, bf16[512,1536]{1,0:T(8,128)(2,1)}, u32[]{:S(2)}, u32[]{:S(2)}) collective-permute-start(bf16[512,1536]{1,0:T(8,128)(2,1)} %product.12), channel_id=1, source_target_pairs={{0,1},{1,0},{2,3},{3,2},{4,5},{5,4},{6,7},{7,6},{8,9},{9,8},{10,11... | collective-permute-start | bytes 4718600 | tf_op jit(solution)/shard_map/ppermute | solution.py:642
  230.5 43.2 %collective-permute-start.10 = (bf16[512,1536]{1,0:T(8,128)(2,1)}, bf16[512,1536]{1,0:T(8,128)(2,1)}, u32[]{:S(2)}, u32[]{:S(2)}) collective-permute-start(bf16[512,1536]{1,0:T(8,128)(2,1)} %product.13), channel_id=1, source_target_pairs={{0,1},{1,0},{2,3},{3,2},{4,5},{5,4},{6,7},{7,6},{8,9},{9,8},{10,11... | collective-permute-start | bytes 4718600 | tf_op jit(solution)/shard_map/ppermute | solution.py:642
  272.2 48.2 %collective-permute-start.11 = (bf16[512,1536]{1,0:T(8,128)(2,1)}, bf16[512,1536]{1,0:T(8,128)(2,1)}, u32[]{:S(2)}, u32[]{:S(2)}) collective-permute-start(bf16[512,1536]{1,0:T(8,128)(2,1)} %product.14), channel_id=1, source_target_pairs={{0,1},{1,0},{2,3},{3,2},{4,5},{5,4},{6,7},{7,6},{8,9},{9,8},{10,11... | collective-permute-start | bytes 4718600 | tf_op jit(solution)/shard_map/ppermute | solution.py:642
  340.5 41.6 %collective-permute-start.13 = (bf16[768,4096]{1,0:T(8,128)(2,1)}, bf16[768,4096]{1,0:T(8,128)(2,1)}, u32[]{:S(2)}, u32[]{:S(2)}) collective-permute-start(bf16[768,4096]{1,0:T(8,128)(2,1)} %get-tuple-element.177), channel_id=1, source_target_pairs={{0,2},{2,0},{4,6},{6,4},{8,10},{10,8},{12,14},{14,12},{16,18},{18,... | collective-permute-start | bytes 18874376 | tf_op jit(solution)/shard_map/ppermute | solution.py:609
  340.5 38.1 %collective-permute-start.14 = (bf16[768,2048]{1,0:T(8,128)(2,1)}, bf16[768,2048]{1,0:T(8,128)(2,1)}, u32[]{:S(2)}, u32[]{:S(2)}) collective-permute-start(bf16[768,2048]{1,0:T(8,128)(2,1)} %get-tuple-element.174), channel_id=1, source_target_pairs={{0,2},{2,0},{4,6},{6,4},{8,10},{10,8},{12,14},{14,12},{16,18},{18,... | collective-permute-start | bytes 9437192 | tf_op jit(solution)/shard_map/ppermute | solution.py:609
  388.1 69.6 %collective-permute-start.16 = (bf16[384,4096]{1,0:T(8,128)(2,1)}, bf16[384,4096]{1,0:T(8,128)(2,1)}, u32[]{:S(2)}, u32[]{:S(2)}) collective-permute-start(bf16[384,4096]{1,0:T(8,128)(2,1)} %add_convert_fusion.1), channel_id=1, source_target_pairs={{0,4},{2,6},{4,0},{6,2},{8,12},{10,14},{12,8},{14,10},{16,20},{18,... | collective-permute-start | bytes 9437192 | tf_op jit(solution)/shard_map/ppermute | solution.py:609
  389.3 44.0 %collective-permute-start.17 = (bf16[384,2048]{1,0:T(8,128)(2,1)}, bf16[384,2048]{1,0:T(8,128)(2,1)}, u32[]{:S(2)}, u32[]{:S(2)}) collective-permute-start(bf16[384,2048]{1,0:T(8,128)(2,1)} %add_convert_fusion.4), channel_id=1, source_target_pairs={{0,8},{2,10},{4,12},{6,14},{8,0},{10,2},{12,4},{14,6},{16,24},{18,... | collective-permute-start | bytes 4718600 | tf_op jit(solution)/shard_map/ppermute | solution.py:609
  469.4 40.5 %collective-permute-start.18 = (bf16[2048,1536]{1,0:T(8,128)(2,1)}, bf16[2048,1536]{1,0:T(8,128)(2,1)}, u32[]{:S(2)}, u32[]{:S(2)}) collective-permute-start(bf16[2048,1536]{1,0:T(8,128)(2,1)} %get-tuple-element.198), channel_id=1, source_target_pairs={{0,2},{2,0},{4,6},{6,4},{8,10},{10,8},{12,14},{14,12},{16,18},{18,... | collective-permute-start | bytes 18874376 | tf_op jit(solution)/shard_map/ppermute | solution.py:609
  472.0 108.7 %collective-permute-start.15 = (bf16[1024,1536]{1,0:T(8,128)(2,1)}, bf16[1024,1536]{1,0:T(8,128)(2,1)}, u32[]{:S(2)}, u32[]{:S(2)}) collective-permute-start(bf16[1024,1536]{1,0:T(8,128)(2,1)} %product.16), channel_id=1, source_target_pairs={{0,1},{1,0},{2,3},{3,2},{4,5},{5,4},{6,7},{7,6},{8,9},{9,8},{10,11... | collective-permute-start | bytes 9437192 | tf_op jit(solution)/shard_map/ppermute | solution.py:642
  514.6 92.2 %collective-permute-start.24 = (bf16[1024,1536]{1,0:T(8,128)(2,1)}, bf16[1024,1536]{1,0:T(8,128)(2,1)}, u32[]{:S(2)}, u32[]{:S(2)}) collective-permute-start(bf16[1024,1536]{1,0:T(8,128)(2,1)} %add_convert_fusion), channel_id=1, source_target_pairs={{0,4},{2,6},{4,0},{6,2},{8,12},{10,14},{12,8},{14,10},{16,20},{18,... | collective-permute-start | bytes 9437192 | tf_op jit(solution)/shard_map/ppermute | solution.py:609
  517.6 63.1 %collective-permute-start.25 = (bf16[96,4096]{1,0:T(8,128)(2,1)S(1)}, bf16[96,4096]{1,0:T(8,128)(2,1)S(1)}, u32[]{:S(2)}, u32[]{:S(2)}) collective-permute-start(bf16[96,4096]{1,0:T(8,128)(2,1)S(1)} %copy-done.71), channel_id=1, source_target_pairs={{0,16},{2,18},{4,20},{6,22},{8,24},{10,26},{12,28},{14,30},{16,0},... | collective-permute-start | bytes 2359304 | tf_op jit(solution)/shard_map/ppermute | solution.py:609
  529.2 81.9 %collective-permute-start.23 = (bf16[768,1152]{1,0:T(8,128)(2,1)}, bf16[768,1152]{1,0:T(8,128)(2,1)}, u32[]{:S(2)}, u32[]{:S(2)}) collective-permute-start(bf16[768,1152]{1,0:T(8,128)(2,1)} %get-tuple-element.206), channel_id=1, source_target_pairs={{0,2},{2,0},{4,6},{6,4},{8,10},{10,8},{12,14},{14,12},{16,18},{18,... | collective-permute-start | bytes 5308424 | tf_op jit(solution)/shard_map/ppermute | solution.py:609
  531.4 49.3 %collective-permute-start.21 = (bf16[96,2048]{1,0:T(8,128)(2,1)S(1)}, bf16[96,2048]{1,0:T(8,128)(2,1)S(1)}, u32[]{:S(2)}, u32[]{:S(2)}) collective-permute-start(bf16[96,2048]{1,0:T(8,128)(2,1)S(1)} %copy-done.81), channel_id=1, source_target_pairs={{0,16},{2,18},{4,20},{6,22},{8,24},{10,26},{12,28},{14,30},{16,0},... | collective-permute-start | bytes 1179656 | tf_op jit(solution)/shard_map/ppermute | solution.py:609
  605.8 45.1 %collective-permute-start.29 = (bf16[640,1536]{1,0:T(8,128)(2,1)}, bf16[640,1536]{1,0:T(8,128)(2,1)}, u32[]{:S(2)}, u32[]{:S(2)}) collective-permute-start(bf16[640,1536]{1,0:T(8,128)(2,1)} %slice.490), channel_id=1, source_target_pairs={{0,1},{1,0},{2,3},{3,2},{4,5},{5,4},{6,7},{7,6},{8,9},{9,8},{10,11... | collective-permute-start | bytes 5898248 | tf_op jit(solution)/shard_map/ppermute | solution.py:642
  616.8 38.1 %collective-permute-start.28 = (bf16[384,1152]{1,0:T(8,128)(2,1)}, bf16[384,1152]{1,0:T(8,128)(2,1)}, u32[]{:S(2)}, u32[]{:S(2)}) collective-permute-start(bf16[384,1152]{1,0:T(8,128)(2,1)} %add_convert_fusion.6), channel_id=1, source_target_pairs={{0,4},{2,6},{4,0},{6,2},{8,12},{10,14},{12,8},{14,10},{16,20},{18,... | collective-permute-start | bytes 2654216 | tf_op jit(solution)/shard_map/ppermute | solution.py:609
  625.3 47.9 %collective-permute-start.33 = (bf16[512,1536]{1,0:T(8,128)(2,1)}, bf16[512,1536]{1,0:T(8,128)(2,1)S(1)}, u32[]{:S(2)}, u32[]{:S(2)}) collective-permute-start(bf16[512,1536]{1,0:T(8,128)(2,1)} %add_convert_fusion.2), channel_id=1, source_target_pairs={{0,8},{2,10},{4,12},{6,14},{8,0},{10,2},{12,4},{14,6},{16,24},{18,... | collective-permute-start | bytes 4718600 | tf_op jit(solution)/shard_map/ppermute | solution.py:609
  626.3 52.4 %collective-permute-start.32 = (bf16[384,1152]{1,0:T(8,128)(2,1)}, bf16[384,1152]{1,0:T(8,128)(2,1)S(1)}, u32[]{:S(2)}, u32[]{:S(2)}) collective-permute-start(bf16[384,1152]{1,0:T(8,128)(2,1)} %add_convert_fusion.7), channel_id=1, source_target_pairs={{0,4},{2,6},{4,0},{6,2},{8,12},{10,14},{12,8},{14,10},{16,20},{18,... | collective-permute-start | bytes 2654216 | tf_op jit(solution)/shard_map/ppermute | solution.py:609
  676.6 64.4 %collective-permute-start.41 = (bf16[256,1536]{1,0:T(8,128)(2,1)}, bf16[256,1536]{1,0:T(8,128)(2,1)}, u32[]{:S(2)}, u32[]{:S(2)}) collective-permute-start(bf16[256,1536]{1,0:T(8,128)(2,1)} %add_convert_fusion.8), channel_id=1, source_target_pairs={{0,16},{2,18},{4,20},{6,22},{8,24},{10,26},{12,28},{14,30},{16,0},... | collective-permute-start | bytes 2359304 | tf_op jit(solution)/shard_map/ppermute | solution.py:609
  683.0 64.0 %collective-permute-start.42 = (bf16[96,1152]{1,0:T(8,128)(2,1)}, bf16[96,1152]{1,0:T(8,128)(2,1)S(1)}, u32[]{:S(2)}, u32[]{:S(2)}) collective-permute-start(bf16[96,1152]{1,0:T(8,128)(2,1)} %add_convert_fusion.17), channel_id=1, source_target_pairs={{0,16},{2,18},{4,20},{6,22},{8,24},{10,26},{12,28},{14,30},{16,0},... | collective-permute-start | bytes 663560 | tf_op jit(solution)/shard_map/ppermute | solution.py:609
  696.6 48.5 %collective-permute-start.40 = (bf16[96,768]{1,0:T(8,128)(2,1)S(1)}, bf16[96,768]{1,0:T(8,128)(2,1)S(1)}, u32[]{:S(2)}, u32[]{:S(2)}) collective-permute-start(bf16[96,768]{1,0:T(8,128)(2,1)S(1)} %add_convert_fusion.18), channel_id=1, source_target_pairs={{0,16},{2,18},{4,20},{6,22},{8,24},{10,26},{12,28},{14,30},{16,0},... | collective-permute-start | bytes 442376 | tf_op jit(solution)/shard_map/ppermute | solution.py:609
  707.7 39.4 %collective-permute-start.39 = (bf16[96,1152]{1,0:T(8,128)(2,1)S(1)}, bf16[96,1152]{1,0:T(8,128)(2,1)S(1)}, u32[]{:S(2)}, u32[]{:S(2)}) collective-permute-start(bf16[96,1152]{1,0:T(8,128)(2,1)S(1)} %add_convert_fusion.16), channel_id=1, source_target_pairs={{0,16},{2,18},{4,20},{6,22},{8,24},{10,26},{12,28},{14,30},{16,0},... | collective-permute-start | bytes 663560 | tf_op jit(solution)/shard_map/ppermute | solution.py:609
  (141 other events, 1992.9 us)
Sparse Core Ops, SparseCore 0:
  19.3 117.0 all-gather.3
  138.0 99.1 all-gather.5
  239.4 61.8 all-gather.7

commit v4 on v3

--- a/solution.py
+++ b/solution.py
@@ -543,12 +543,17 @@
     total = dot(left_ref[...], right_ref[...])
     if has_add:
         total = total + refs[2][...].astype(jnp.float32)
-    refs[-1][...] = total.astype(refs[-1].dtype)
-
-
-def product(left, right, cols, tile, dtype, turned=False, shift=0, add=None, part=(0, 1)):
+    low = 0
+    for out_ref in refs[2 + has_add :]:
+        count = out_ref.shape[0]
+        out_ref[...] = total[low : low + count].astype(out_ref.dtype)
+        low += count
+
+
+def product(left, right, cols, tile, dtype, turned=False, shift=0, add=None, part=(0, 1), cut=0):
     depth = left.shape[1]
     rows = left.shape[0] // part[1]
+    counts = [cut, rows - cut] if cut else [rows]
     if turned:
         right_block = pl.BlockSpec((tile, depth), lambda j: (j, shift))
     else:
@@ -556,16 +561,17 @@
     in_specs = [pl.BlockSpec((rows, depth), lambda j: (part[0], 0)), right_block]
     if add is not None:
         in_specs.append(pl.BlockSpec((rows, tile), lambda j: (0, j)))
-    return pl.pallas_call(
+    outs = pl.pallas_call(
         functools.partial(product_kernel, turned, add is not None),
         grid=(cols // tile,),
         in_specs=in_specs,
-        out_specs=pl.BlockSpec((rows, tile), lambda j: (0, j)),
-        out_shape=jax.ShapeDtypeStruct((rows, cols), dtype),
+        out_specs=[pl.BlockSpec((count, tile), lambda j: (0, j)) for count in counts],
+        out_shape=[jax.ShapeDtypeStruct((count, cols), dtype) for count in counts],
         compiler_params=pltpu.CompilerParams(vmem_limit_bytes=58 * 2**20),
         cost_estimate=LIGHT,
         name="product",
     )(left, right, *([] if add is None else [add]))
+    return outs if cut else outs[0]
 
 
 def gated(value, *tokens):
@@ -663,6 +669,34 @@
         if steps is not None:
             steps.append(value)
     return value
+
+
+class Hops:
+    def __init__(self, value, size):
+        self.value, self.size, self.bit = value, size, 0
+
+    def start(self, *tokens):
+        if self.bit < self.size.bit_length() - 1:
+            value = gated(self.value, *tokens) if tokens else self.value
+            self.came = lax.ppermute(value, "dp", flip_perm(self.size, 1 << self.bit))
+
+    def finish(self, *tokens):
+        if self.bit < self.size.bit_length() - 1:
+            came = gated(self.came, *tokens) if tokens else self.came
+            upper = (lax.axis_index("dp") >> self.bit) % 2 == 1
+            self.value = jnp.where(
+                upper,
+                jnp.concatenate([came, self.value], 0),
+                jnp.concatenate([self.value, came], 0),
+            )
+            self.bit += 1
+        return self.value
+
+    def drain(self):
+        while self.bit < self.size.bit_length() - 1:
+            self.start()
+            self.finish()
+        return self.value
 
 
 def small_sum(value, name, size):
@@ -934,7 +968,7 @@
     steps = []
     small_all = small_gather(small, "dp", size, (), steps)
     packed = pack_weights(
-        gated([textkey_proj, textval_proj], steps[0]), [query_proj, key_proj, value_proj], output_proj
+        [textkey_proj, textval_proj], [query_proj, key_proj, value_proj], output_proj
     )
     packed_set = lax.all_gather(packed, "dp", axis=0, tiled=True)
 
@@ -1077,9 +1111,10 @@
     )
     down.finish(dq_cross)
     down.start()
-    grown.finish(down.out)
+    text = staged(cap_in, gated(dtext, down.out), side_first, 256)
+    grown.finish(text.out)
     grown.start()
-    text = staged(cap_in, gated(dtext, grown.out), side_first, 256)
+    text.out = gated(text.out, grown.out)
     text.start()
     split = pairs - pairs // 2
     windows = [(0, split), (split, pairs - split)]
@@ -1092,24 +1127,29 @@
     grown.start()
     text.finish(grown.out)
     text.start()
-    first_qkv = staged(attn_in, gated(dqkv_a, text.out), side_first, 3 * LANES)
-    first_qkv.start()
-    outp = staged(gated(grad_attn, first_qkv.out), mixed_heads, side_first, padded)
+    outp = staged(gated(grad_attn, text.out), mixed_heads, side_first, padded)
     outp.start()
+    first_qkv = staged(attn_in, gated(dqkv_a, outp.out), side_first, 3 * LANES)
     edge = 3 * LANES * split
     even = pairs == 2 * split
     wide_a = full_qkvo if even else full_qkvo[:, :edge]
     wide_b = full_qkvo if even else full_qkvo[:, edge : 3 * padded]
-    dattn_a = product(gated(dqkv_a, outp.out), wide_a, model_dim, 512, f32, True)
-    dmixed_b = gated(dmixed, dattn_a)
+    dattn_a = product(gated(dqkv_a, first_qkv.out), wide_a, model_dim, 512, f32, True)
+    outp.finish(dattn_a)
+    outp.start()
+    dmixed_b = gated(dmixed, outp.out)
     dqkv_b, stats_b = self_back(windows[1], *common, dmixed_b, dq_cross, tables, head_dim)
     landed = (down.land(dqkv_b), grown.land(dqkv_b), gated(ffn_came, dqkv_b))
     ffn_came = landed[2]
     dqkv_l = gated(dqkv_b, *landed)
-    dattn_part = product(dqkv_l, wide_b, model_dim, 512, bf16, True, int(even), dattn_a)
-    cut = dattn_part.shape[0] * 5 // 8
-    high_own, high_came = swap_start(dattn_part[:cut], groups, 1)
-    last_qkv = staged(attn_in, gated(dqkv_b, dattn_part), side_first, 3 * LANES)
+    cut = latents.shape[0] * 5 // 8
+    top, low = product(
+        dqkv_l, wide_b, model_dim, 512, bf16, True, int(even), dattn_a, (0, 1), cut
+    )
+    high_own, high_came = swap_start(top, groups, 1)
+    first_qkv.out = gated(first_qkv.out, low)
+    first_qkv.start()
+    last_qkv = staged(attn_in, gated(dqkv_b, low), side_first, 3 * LANES)
     last_qkv.start()
     text.finish(last_qkv.out)
     text.start()
@@ -1123,42 +1163,20 @@
         gated(dtext, last_qkv.out), full_text, cap_in.shape[1], 1024, bf16, True
     )
     grad_gate, grad_up = gather_sum([grown.drain(caption_part)], tile, 2, units)
-    high_came = gated(high_came, grad_gate)
-    base_own, base_came = swap_start(gated(dattn_part[cut:], high_came), groups, 1)
-    last_qkv.finish(high_came)
-    last_qkv.start()
-    outp.finish(last_qkv.out)
-    outp.start()
-    down_t = sum(term[:rows_w].astype(f32) for term in down.drain(outp.out))
-    ffn_out = swap_end(ffn_own, gated(ffn_came, down_t), groups)
-    output = (residual + gate_two * ffn_out).astype(bf16)
-    weighed_part = jnp.sum(gated(dattn_part, output).astype(f32) * normed_one, axis=0)
-    gate_part = jnp.sum(grad_out * gated(ffn_part, weighed_part).astype(f32), axis=0)
-    text.finish(gate_part)
-    text.start()
-    first_qkv.finish(text.out)
-    first_qkv.start()
-    last_qkv.finish(first_qkv.out)
-    last_qkv.start()
-    base_came = gated(base_came, last_qkv.out)
+    top_l, low_l, ffn_l = gated((top, low, ffn_part), grad_gate)
+    weighed_part = jnp.sum(top_l.astype(f32) * normed_one[:cut], axis=0)
+    weighed_part = weighed_part + jnp.sum(low_l.astype(f32) * normed_one[cut:], axis=0)
+    gate_part = jnp.sum(grad_out * ffn_l.astype(f32), axis=0)
     stats = jnp.concatenate([stats_a, stats_b], axis=1)[:2]
     stat_sums = jnp.concatenate([stats, stats_c[:2]], axis=0)[:, :chan]
     stat_sums = jnp.sum(stat_sums.reshape(4, heads_here, head_dim), axis=(1,))
     xgate_rows = stats_c[1, :chan].reshape(heads_here, head_dim)
     xgate_here = jnp.sum(xgate_rows, axis=1) * (1.0 - tanh_cross**2)
     sums_part = jnp.concatenate([weighed_part, gate_part, stat_sums[:3].reshape(-1)])[None]
-    sums = small_sum(gated(sums_part, base_came), "tensor", groups)[0]
-    dattn_in = jnp.concatenate(
-        [swap_end(high_own, high_came, groups), swap_end(base_own, base_came, groups)], axis=0
-    )
-    grad_latents = (
-        dresid + norm_back(dattn_in * gain_one * (1.0 + scale_one), normed_one, factor_one)
-    ).astype(bf16)
-    outp.finish(grad_latents)
-    outp.start()
-    first_qkv.finish(outp.out)
-    first_qkv.start()
-    sums = gated(sums, first_qkv.out)
+    sums = small_sum(sums_part, "tensor", groups)[0]
+    high_came = gated(high_came, sums_part)
+    base_own, base_came = swap_start(gated(low, high_came), groups, 1)
+    sums = gated(sums, high_came)
     weighed_one, head_gains = sums[:model_dim], sums[2 * model_dim :]
     dgate_two = sums[model_dim : 2 * model_dim] * (1.0 - gate_two[0] ** 2)
     grad_gainone = weighed_one * (1.0 + scale_one[0])
@@ -1168,12 +1186,43 @@
     dmod_here = lax.dynamic_slice_in_dim(dmod_all, tensor_index * cols_here, cols_here, 0)
     row = jnp.concatenate([dmod_here, grad_gainone, grad_gaintwo, head_gains, xgate_here])
     row = row.astype(bf16).astype(f32)[None]
-    dcaption = tensor_scatter(gated(caption_part, sums), groups)
+    hops = Hops(row, size)
+    hops.start()
+    text.finish(row)
+    text.start()
+    first_qkv.finish(text.out)
+    first_qkv.start()
+    last_qkv.finish(first_qkv.out)
+    last_qkv.start()
+    hops.finish(last_qkv.out)
+    hops.start()
+    outp.finish(hops.value)
+    outp.start()
+    down_t = sum(term[:rows_w].astype(f32) for term in down.drain(outp.out))
+    hops.finish(down_t)
+    hops.start()
+    ffn_out = swap_end(ffn_own, gated(ffn_came, hops.value), groups)
+    output = (residual + gate_two * ffn_out).astype(bf16)
+    first_qkv.finish(output)
+    first_qkv.start()
+    last_qkv.finish(first_qkv.out)
+    last_qkv.start()
+    hops.finish(last_qkv.out)
+    hops.start()
+    base_came = gated(base_came, hops.value)
+    dcaption = tensor_scatter(gated(caption_part, base_came), groups)
+    dattn_in = jnp.concatenate(
+        [swap_end(high_own, high_came, groups), swap_end(base_own, base_came, groups)], axis=0
+    )
+    grad_latents = (
+        dresid + norm_back(dattn_in * gain_one * (1.0 + scale_one), normed_one, factor_one)
+    ).astype(bf16)
     embed_row = jnp.einsum(
         "bc,tc->bt", row[:, :cols_here].astype(bf16), mod_set, preferred_element_type=f32
     )
-    rows_set = small_gather(row, "dp", size)
-    grad_textkey, grad_textval = gather_sum([text.drain(row)], LANES, 2, chan)
+    grad_textkey, grad_textval = gather_sum([text.drain(grad_latents)], LANES, 2, chan)
+    hops.finish(grad_textkey)
+    rows_set = hops.drain()
     dmod_set = rows_set[:, :cols_here].astype(bf16)
     gain_sums = jnp.sum(rows_set[:, cols_here:], axis=0)
     grad_modul = jnp.einsum("bt,bc->tc", cond_here, dmod_set, preferred_element_type=f32)

time: 779 us -> 753 us (0.967)
  waiting for transfers between devices: 182 us -> 156 us
    ppermute x9 -> x5, waiting for transfers between devices: 26.7 us -> 6.89 us  [small_gather(): came = lax.ppermute(value, name, flip_perm(size, bit))]
    ppermute x24, waiting for transfers between devices: 28.8 us -> 40.8 us  [start(): self.came = lax.ppermute(self.out, 'dp', flip_perm(self.size, 1 << bit))]
    ppermute x7, waiting for transfers between devices: 29.7 us -> 19.6 us  [swap_start(): return (own, [lax.ppermute(o, 'tensor', flip_perm(size, 1)) for o in own])]
    ppermute x0 -> x4, waiting for transfers between devices: none -> 9.1 us  [start(): self.came = lax.ppermute(value, 'dp', flip_perm(self.size, 1 << self.bit))]
    unnamed x235 -> x225, local copies, waits for them, and re-layouts: 24.9 us -> 26.1 us
  transfers between devices with their start and end apart: 50 -> 50, of which waited for: 20 -> 20; matrix products, arithmetic and copies ran while one was open for 18% -> 18% of each run, Pallas kernels for 43% -> 46%
where the time goes in v4:
time: 753 us; the launch traced here: 746 us
  Pallas kernels  346 us (46%)
  waiting for transfers between devices  156 us (21%)
  other arithmetic  134 us (18%)
  starting transfers between devices  53.6 us (7%)
  local copies, waits for them, and re-layouts  35.1 us (5%)
  between operations  16.8 us (2%)
    pallas_call x11, Pallas kernels, product(): pl.pallas_call(functools.partial(product_kernel, turned, add is not None)...  94.9 us
    all_gather x1, waiting for transfers between devices, local(): packed_set = lax.all_gather(packed, 'dp', axis=0, tiled=True)  66.3 us
    pallas_call x6, Pallas kernels, outer_grads(): pl.pallas_call(functools.partial(outer_kernel, size, bits), grid=(cols //...  63.6 us
    pallas_call x2, Pallas kernels, self_back(): pl.pallas_call(functools.partial(self_back_kernel, half, min(512, rows)),...  62 us
    convert_element_type x18, other arithmetic, finish(): self.out = total if last else total.astype(jnp.bfloat16)  48.9 us
    ppermute x24, waiting for transfers between devices, start(): self.came = lax.ppermute(self.out, 'dp', flip_perm(self.size, 1 << bit))  40.8 us
    pallas_call x2, Pallas kernels, attend_rows(): pl.pallas_call(functools.partial(attend_kernel, half, min(256, count), fr...  40 us
    pallas_call x2, Pallas kernels, feed_forward(): pl.pallas_call(feed_kernel, grid=(blocks,), in_specs=[pl.BlockSpec((count...  34.2 us
  transfers between devices with their start and end apart: 50, of which 20 were waited for; matrix products, arithmetic and copies ran while one was open for 18% of the time, Pallas kernels for 46%

profile of v4, /device:TPU:0, one launch (start us, length us, event | category | flops | bytes accessed | tf_op | source)
XLA Modules:
  0.0 746.3 jit_solution(10863365662532094982)
XLA Ops:
  65.8 66.3 %all-gather.4.cloned.1.call-done.refs_1_ = bf16[4096,2688]{1,0:T(8,128)(2,1)} async-done(((bf16[256,2688]{1,0:T(8,128)(2,1)}), bf16[4096,2688]{1,0:T(8,128)(2,1)}) %all-gather.4.cloned.1.call-update) | async-done | bytes 22020112 | tf_op jit(solution)/shard_map/all_gather | solution.py:973
  132.2 17.5 %unfold_product.1 = (bf16[1536,3072]{1,0:T(8,128)(2,1)}, f32[1024,3072]{1,0:T(8,128)}) custom-call(bf16[1024,1536]{1,0:T(8,128)(2,1)} %get-tuple-element.291.left_ref, bf16[16,256,2688]{2,1,0:T(8,128)(2,1)} %bitcast.56, bf16[16,256,2688]{2,1,0:T(8,128)(2,1)} %bitcast.57, bf16[16,256,2688]{2,1,0:T(8,128)(2,1)} %bitcast.58), custom_call_target="tpu_custom_call" | custom-call | flops 1 | bytes 1 | tf_op jit(solution)/shard_map/unfold_product/pallas_call | solution.py:880
  152.2 10.0 %product.11.refs_4_.refs_5_.text_ref = f32[256,1536]{1,0:T(8,128)} custom-call(bf16[256,4096]{1,0:T(8,128)(2,1)} %bitcast.54, bf16[4096,2688]{1,0:T(8,128)(2,1)} %all-gather.4.cloned.1.call-done.refs_1_), custom_call_target="tpu_custom_call" | custom-call | flops 1 | bytes 1 | tf_op jit(solution)/shard_map/product/pallas_call | solution.py:564
  162.2 21.8 %attend_fwd.2 = (bf16[512,768]{1,0:T(8,128)(2,1)S(1)}, bf16[1024,768]{1,0:T(8,128)(2,1)}, f32[1024,768]{1,0:T(8,128)}, f32[1024,768]{1,0:T(8,128)}, f32[1024,153...) custom-call(s32[1]{0:T(128)S(6)} %copy.150.refs_0_.len_ref, ...), custom_call_target="tpu_custom_call" | custom-call | flops 1 | bytes 1 | tf_op jit(solution)/shard_map/attend_fwd/pallas_call | solution.py:189
  191.5 18.2 %attend_fwd.3 = (bf16[512,768]{1,0:T(8,128)(2,1)S(1)}, bf16[1024,768]{1,0:T(8,128)(2,1)}, f32[1024,768]{1,0:T(8,128)}, f32[1024,768]{1,0:T(8,128)}, f32[1024,1536]{1,0:T(8,128)}) custom-call(s32[1]{0:T(128)S(6)} %copy.150.refs_0_.len_ref, ...), custom_call_target="tpu_custom_call", output_to_operand_aliasing={{1}: (8, {}), {2}: (9, {}), {3}: (10, {}), {4}: (11, {})} | custom-call | flops 1 | bytes 1 | tf_op jit(solution)/shard_map/attend_fwd/pallas_call | solution.py:189
  215.5 11.0 %collective-permute-done.9 = bf16[512,1536]{1,0:T(8,128)(2,1)} collective-permute-done((bf16[512,1536]{1,0:T(8,128)(2,1)}, bf16[512,1536]{1,0:T(8,128)(2,1)}, u32[]{:S(2)}, u32[]{:S(2)}) %collective-permute-start.9) | collective-permute-done | bytes 1572896 | tf_op jit(solution)/shard_map/ppermute | solution.py:648
  239.1 17.0 %feed_forward.2 = (bf16[1024,2048]{1,0:T(8,128)(2,1)}, bf16[1024,4096]{1,0:T(8,128)(2,1)}) custom-call(bf16[512,1536]{1,0:T(8,128)(2,1)} %multiply_convert_fusion.5.x_ref, bf16[1024,1536]{1,0:T(8,128)(2,1)} %multiply_convert_fusion.grad_ref.left_ref, bf16[1536,6144]{1,0:T(8,128)(2,1)} %all-gather.6.cloned.1.call-done.gate_ref.up_ref.down_ref.refs_1_, ...), custom_call_target="tpu_custom_call" | custom-call | flops 1 | bytes 1 | tf_op jit(solution)/shard_map/feed_forward/pallas_call | solution.py:481
  256.2 12.0 %product.14 = bf16[512,1536]{1,0:T(8,128)(2,1)} custom-call(bf16[1024,4096]{1,0:T(8,128)(2,1)} %get-tuple-element.174.refs_0_.refs_1_, bf16[1536,6144]{1,0:T(8,128)(2,1)} %all-gather.6.cloned.1.call-done.gate_ref.up_ref.down_ref.refs_1_), custom_call_target="tpu_custom_call" | custom-call | flops 1 | bytes 1 | tf_op jit(solution)/shard_map/product/pallas_call | solution.py:564
  275.9 17.1 %feed_forward.3 = (bf16[1024,2048]{1,0:T(8,128)(2,1)}, bf16[1024,4096]{1,0:T(8,128)(2,1)}) custom-call(bf16[512,1536]{1,0:T(8,128)(2,1)} %multiply_convert_fusion.4.x_ref, bf16[1024,1536]{1,0:T(8,128)(2,1)} %multiply_convert_fusion.grad_ref.left_ref, ...), custom_call_target="tpu_custom_call", output_to_operand_aliasing={{0}: (5, {}), {1}: (6, {})} | custom-call | flops 1 | bytes 1 | tf_op jit(solution)/shard_map/feed_forward/pallas_call | solution.py:481
  293.1 11.6 %product.15 = bf16[512,1536]{1,0:T(8,128)(2,1)} custom-call(bf16[1024,4096]{1,0:T(8,128)(2,1)} %get-tuple-element.180.refs_0_.right_ref, bf16[1536,6144]{1,0:T(8,128)(2,1)} %all-gather.6.cloned.1.call-done.gate_ref.up_ref.down_ref.refs_1_), custom_call_target="tpu_custom_call" | custom-call | flops 1 | bytes 1 | tf_op jit(solution)/shard_map/product/pallas_call | solution.py:564
  304.6 11.6 %outer_grads.6 = (bf16[768,2048]{1,0:T(8,128)(2,1)S(1)}, bf16[768,2048]{1,0:T(8,128)(2,1)}) custom-call(s32[1]{0:T(128)} %bitcast.13.me_ref, bf16[1024,1536]{1,0:T(8,128)(2,1)} %multiply_convert_fusion.grad_ref.left_ref, bf16[1024,2048]{1,0:T(8,128)(2,1)} %get-tuple-element.183.right_ref.refs_0_), custom_call_target="tpu_custom_call" | custom-call | flops 1 | bytes 1 | tf_op jit(solution)/shard_map/outer_grads/pallas_call | solution.py:523
  316.5 19.6 %outer_grads.7 = (bf16[768,4096]{1,0:T(8,128)(2,1)}, bf16[768,4096]{1,0:T(8,128)(2,1)}) custom-call(s32[1]{0:T(128)} %bitcast.13.me_ref, bf16[1024,1536]{1,0:T(8,128)(2,1)S(1)} %pad_maximum_fusion.left_ref, bf16[1024,4096]{1,0:T(8,128)(2,1)} %get-tuple-element.180.refs_0_.right_ref), custom_call_target="tpu_custom_call" | custom-call | flops 1 | bytes 1 | tf_op jit(solution)/shard_map/outer_grads/pallas_call | solution.py:523
  350.1 11.0 %product.16 = bf16[1024,1536]{1,0:T(8,128)(2,1)} custom-call(bf16[1024,2048]{1,0:T(8,128)(2,1)} %get-tuple-element.183.right_ref.refs_0_, bf16[1536,6144]{1,0:T(8,128)(2,1)} %all-gather.6.cloned.1.call-done.gate_ref.up_ref.down_ref.refs_1_), custom_call_target="tpu_custom_call" | custom-call | flops 1 | bytes 1 | tf_op jit(solution)/shard_map/product/pallas_call | solution.py:564
  407.5 21.2 %cross_bwd.1 = (f32[1024,768]{1,0:T(8,128)S(1)}, bf16[256,1536]{1,0:T(8,128)(2,1)S(1)}, f32[8,768]{1,0:T(8,128)S(1)}) custom-call(s32[1]{0:T(128)S(6)} %copy.150.refs_0_.len_ref, bf16[1024,768]{1,0:T(8,128)(2,1)S(1)} %copy-done, bf16[256,1536]{1,0:T(8,128)(2,1)S(1)} %copy-done.15, f32[256,1536]{1,0:T(8,128)S(1)} %copy-done.2, f32[1024,768]{1,0:T(8,128)S(1)} %copy-done.8, ...), custom_call_target="tpu_custom_call" | custom-call | flops 1 | bytes 1 | tf_op jit(solution)/shard_map/cross_bwd/pallas_call | solution.py:390
  441.4 11.8 %collective-permute-done.17.refs_2_ = bf16[384,4096]{1,0:T(8,128)(2,1)} collective-permute-done((bf16[384,4096]{1,0:T(8,128)(2,1)}, bf16[384,4096]{1,0:T(8,128)(2,1)}, u32[]{:S(2)}, u32[]{:S(2)}) %collective-permute-start.17) | collective-permute-done | bytes 3145760 | tf_op jit(solution)/shard_map/ppermute | solution.py:615
  459.9 31.2 %self_bwd.2 = (bf16[1024,1152]{1,0:T(8,128)(2,1)}, f32[8,384]{1,0:T(8,128)S(1)}) custom-call(bf16[1024,768]{1,0:T(8,128)(2,1)S(1)} %copy-done, bf16[1024,1536]{1,0:T(8,128)(2,1)} %get-tuple-element.156.refs_2_.key_ref.val_ref, bf16[1024,1536]{1,0:T(8,128)(2,1)} %get-tuple-element.156.refs_2_.key_ref.val_ref, ...), custom_call_target="tpu_custom_call" | custom-call | flops 1 | bytes 1 | tf_op jit(solution)/shard_map/self_bwd/pallas_call | solution.py:428
  516.4 9.1 %outer_grads.10 = (bf16[768,1152]{1,0:T(8,128)(2,1)S(1)}, bf16[768,1152]{1,0:T(8,128)(2,1)}) custom-call(s32[1]{0:T(128)} %bitcast.13.me_ref, bf16[1024,1536]{1,0:T(8,128)(2,1)} %get-tuple-element.291.left_ref, bf16[1024,1152]{1,0:T(8,128)(2,1)} %get-tuple-element.215.right_ref.refs_0_), custom_call_target="tpu_custom_call" | custom-call | flops 1 | bytes 1 | tf_op jit(solution)/shard_map/outer_grads/pallas_call | solution.py:523
  526.9 8.7 %product.19.refs_2_ = f32[1024,1536]{1,0:T(8,128)} custom-call(bf16[1024,1152]{1,0:T(8,128)(2,1)} %get-tuple-element.215.right_ref.refs_0_, bf16[1536,3072]{1,0:T(8,128)(2,1)} %get-tuple-element.149.refs_1_), custom_call_target="tpu_custom_call" | custom-call | flops 1 | bytes 1 | tf_op jit(solution)/shard_map/product/pallas_call | solution.py:564
  537.6 30.8 %self_bwd.3 = (bf16[1024,1152]{1,0:T(8,128)(2,1)}, f32[8,384]{1,0:T(8,128)S(1)}) custom-call(bf16[1024,768]{1,0:T(8,128)(2,1)S(1)} %copy-done, bf16[1024,1536]{1,0:T(8,128)(2,1)} %get-tuple-element.156.refs_2_.key_ref.val_ref, bf16[1024,1536]{1,0:T(8,128)(2,1)} %get-tuple-element.156.refs_2_.key_ref.val_ref, ...), custom_call_target="tpu_custom_call" | custom-call | flops 1 | bytes 1 | tf_op jit(solution)/shard_map/self_bwd/pallas_call | solution.py:428
  568.5 9.4 %product.20 = (bf16[640,1536]{1,0:T(8,128)(2,1)}, bf16[384,1536]{1,0:T(8,128)(2,1)}) custom-call(bf16[1024,1152]{1,0:T(8,128)(2,1)} %get-tuple-element.225.refs_0_.right_ref, bf16[1536,3072]{1,0:T(8,128)(2,1)} %get-tuple-element.149.refs_1_, f32[1024,1536]{1,0:T(8,128)} %product.19.refs_2_), custom_call_target="tpu_custom_call" | custom-call | flops 1 | bytes 1 | tf_op jit(solution)/shard_map/product/pallas_call | solution.py:564
  579.6 9.1 %outer_grads.11 = (bf16[768,1152]{1,0:T(8,128)(2,1)S(1)}, bf16[768,1152]{1,0:T(8,128)(2,1)}) custom-call(s32[1]{0:T(128)} %bitcast.13.me_ref, bf16[1024,1536]{1,0:T(8,128)(2,1)} %get-tuple-element.291.left_ref, bf16[1024,1152]{1,0:T(8,128)(2,1)} %get-tuple-element.225.refs_0_.right_ref), custom_call_target="tpu_custom_call" | custom-call | flops 1 | bytes 1 | tf_op jit(solution)/shard_map/outer_grads/pallas_call | solution.py:523
  671.8 11.2 %collective-permute-done.39.refs_3_ = bf16[192,1152]{1,0:T(8,128)(2,1)S(1)} collective-permute-done((bf16[192,1152]{1,0:T(8,128)(2,1)S(1)}, bf16[192,1152]{1,0:T(8,128)(2,1)S(1)}, u32[]{:S(2)}, u32[]{:S(2)}) %collective-permute-start.39) | collective-permute-done | bytes 442400 | tf_op jit(solution)/shard_map/ppermute | solution.py:615
  687.5 11.7 %collective-permute-done.38.refs_8_ = bf16[192,1152]{1,0:T(8,128)(2,1)S(1)} collective-permute-done((bf16[192,1152]{1,0:T(8,128)(2,1)S(1)}, bf16[192,1152]{1,0:T(8,128)(2,1)S(1)}, u32[]{:S(2)}, u32[]{:S(2)}) %collective-permute-start.38) | collective-permute-done | bytes 442400 | tf_op jit(solution)/shard_map/ppermute | solution.py:615
  718.9 9.1 %collective-permute-done.46 = f32[8,6348]{1,0:T(8,128)S(1)} collective-permute-done((f32[8,6348]{1,0:T(8,128)S(1)}, f32[8,6348]{1,0:T(8,128)S(1)}, u32[]{:S(2)}, u32[]{:S(2)}) %collective-permute-start.46) | collective-permute-done | bytes 203168 | tf_op jit(solution)/shard_map/ppermute | solution.py:681
  (478 shorter events, 321.4 us)
Async XLA Ops:
  7.2 125.0 %all-gather.4.cloned.1.call-start = ((), (), s32[]{:S(2)}) async-start(), calls=%async_computation | async-start | bytes 23396352 | tf_op jit(solution)/shard_map/all_gather | solution.py:973
  14.6 218.3 %all-gather.6.cloned.1.call-start = ((), (), s32[]{:S(2)}) async-start(), calls=%async_computation.1 | async-start | bytes 20054016 | tf_op jit(solution)/shard_map/all_gather | solution.py:997
  31.4 318.7 %all-gather.8.cloned.1.call-start = ((), (), s32[]{:S(2)}) async-start(), calls=%async_computation.2 | async-start | bytes 6684672 | tf_op jit(solution)/shard_map/all_gather | solution.py:1035
  226.5 43.1 %collective-permute-start.10 = (bf16[512,1536]{1,0:T(8,128)(2,1)}, bf16[512,1536]{1,0:T(8,128)(2,1)}, u32[]{:S(2)}, u32[]{:S(2)}) collective-permute-start(bf16[512,1536]{1,0:T(8,128)(2,1)} %product.13), channel_id=1, source_target_pairs={{0,1},{1,0},{2,3},{3,2},{4,5},{5,4},{6,7},{7,6},{8,9},{9,8},{10,11... | collective-permute-start | bytes 4718600 | tf_op jit(solution)/shard_map/ppermute | solution.py:648
  268.2 48.1 %collective-permute-start.11 = (bf16[512,1536]{1,0:T(8,128)(2,1)}, bf16[512,1536]{1,0:T(8,128)(2,1)}, u32[]{:S(2)}, u32[]{:S(2)}) collective-permute-start(bf16[512,1536]{1,0:T(8,128)(2,1)} %product.14), channel_id=1, source_target_pairs={{0,1},{1,0},{2,3},{3,2},{4,5},{5,4},{6,7},{7,6},{8,9},{9,8},{10,11... | collective-permute-start | bytes 4718600 | tf_op jit(solution)/shard_map/ppermute | solution.py:648
  336.1 41.5 %collective-permute-start.13 = (bf16[768,4096]{1,0:T(8,128)(2,1)}, bf16[768,4096]{1,0:T(8,128)(2,1)}, u32[]{:S(2)}, u32[]{:S(2)}) collective-permute-start(bf16[768,4096]{1,0:T(8,128)(2,1)} %get-tuple-element.181), channel_id=1, source_target_pairs={{0,2},{2,0},{4,6},{6,4},{8,10},{10,8},{12,14},{14,12},{16,18},{18,... | collective-permute-start | bytes 18874376 | tf_op jit(solution)/shard_map/ppermute | solution.py:615
  336.1 38.1 %collective-permute-start.14 = (bf16[768,2048]{1,0:T(8,128)(2,1)}, bf16[768,2048]{1,0:T(8,128)(2,1)}, u32[]{:S(2)}, u32[]{:S(2)}) collective-permute-start(bf16[768,2048]{1,0:T(8,128)(2,1)} %get-tuple-element.178), channel_id=1, source_target_pairs={{0,2},{2,0},{4,6},{6,4},{8,10},{10,8},{12,14},{14,12},{16,18},{18,... | collective-permute-start | bytes 9437192 | tf_op jit(solution)/shard_map/ppermute | solution.py:615
  383.6 69.6 %collective-permute-start.17 = (bf16[384,4096]{1,0:T(8,128)(2,1)}, bf16[384,4096]{1,0:T(8,128)(2,1)}, u32[]{:S(2)}, u32[]{:S(2)}) collective-permute-start(bf16[384,4096]{1,0:T(8,128)(2,1)} %add_convert_fusion.1), channel_id=1, source_target_pairs={{0,4},{2,6},{4,0},{6,2},{8,12},{10,14},{12,8},{14,10},{16,20},{18,... | collective-permute-start | bytes 9437192 | tf_op jit(solution)/shard_map/ppermute | solution.py:615
  384.8 45.7 %collective-permute-start.16 = (bf16[384,2048]{1,0:T(8,128)(2,1)}, bf16[384,2048]{1,0:T(8,128)(2,1)}, u32[]{:S(2)}, u32[]{:S(2)}) collective-permute-start(bf16[384,2048]{1,0:T(8,128)(2,1)} %add_convert_fusion.4), channel_id=1, source_target_pairs={{0,8},{2,10},{4,12},{6,14},{8,0},{10,2},{12,4},{14,6},{16,24},{18,... | collective-permute-start | bytes 4718600 | tf_op jit(solution)/shard_map/ppermute | solution.py:615
  456.4 40.7 %collective-permute-start.18 = (bf16[2048,1536]{1,0:T(8,128)(2,1)}, bf16[2048,1536]{1,0:T(8,128)(2,1)}, u32[]{:S(2)}, u32[]{:S(2)}) collective-permute-start(bf16[2048,1536]{1,0:T(8,128)(2,1)} %get-tuple-element.204), channel_id=1, source_target_pairs={{0,2},{2,0},{4,6},{6,4},{8,10},{10,8},{12,14},{14,12},{16,18},{18,... | collective-permute-start | bytes 18874376 | tf_op jit(solution)/shard_map/ppermute | solution.py:615
  456.5 37.0 %collective-permute-start.19 = (bf16[192,4096]{1,0:T(8,128)(2,1)S(1)}, bf16[192,4096]{1,0:T(8,128)(2,1)S(1)}, u32[]{:S(2)}, u32[]{:S(2)}) collective-permute-start(bf16[192,4096]{1,0:T(8,128)(2,1)S(1)} %add_convert_fusion.3), channel_id=1, source_target_pairs={{0,8},{2,10},{4,12},{6,14},{8,0},{10,2},{12,4},{14,6},{16,24},{18,... | collective-permute-start | bytes 4718600 | tf_op jit(solution)/shard_map/ppermute | solution.py:615
  459.2 109.3 %collective-permute-start.15 = (bf16[1024,1536]{1,0:T(8,128)(2,1)}, bf16[1024,1536]{1,0:T(8,128)(2,1)}, u32[]{:S(2)}, u32[]{:S(2)}) collective-permute-start(bf16[1024,1536]{1,0:T(8,128)(2,1)} %product.16), channel_id=1, source_target_pairs={{0,1},{1,0},{2,3},{3,2},{4,5},{5,4},{6,7},{7,6},{8,9},{9,8},{10,11... | collective-permute-start | bytes 9437192 | tf_op jit(solution)/shard_map/ppermute | solution.py:648
  501.6 90.6 %collective-permute-start.27 = (bf16[1024,1536]{1,0:T(8,128)(2,1)}, bf16[1024,1536]{1,0:T(8,128)(2,1)}, u32[]{:S(2)}, u32[]{:S(2)}) collective-permute-start(bf16[1024,1536]{1,0:T(8,128)(2,1)} %add_convert_fusion), channel_id=1, source_target_pairs={{0,4},{2,6},{4,0},{6,2},{8,12},{10,14},{12,8},{14,10},{16,20},{18,... | collective-permute-start | bytes 9437192 | tf_op jit(solution)/shard_map/ppermute | solution.py:615
  512.2 56.2 %collective-permute-start.23 = (bf16[96,4096]{1,0:T(8,128)(2,1)}, bf16[96,4096]{1,0:T(8,128)(2,1)}, u32[]{:S(2)}, u32[]{:S(2)}) collective-permute-start(bf16[96,4096]{1,0:T(8,128)(2,1)} %add_convert_fusion.9), channel_id=1, source_target_pairs={{0,16},{2,18},{4,20},{6,22},{8,24},{10,26},{12,28},{14,30},{16,0},... | collective-permute-start | bytes 2359304 | tf_op jit(solution)/shard_map/ppermute | solution.py:615
  514.5 53.9 %collective-permute-start.22 = (bf16[96,2048]{1,0:T(8,128)(2,1)}, bf16[96,2048]{1,0:T(8,128)(2,1)S(1)}, u32[]{:S(2)}, u32[]{:S(2)}) collective-permute-start(bf16[96,2048]{1,0:T(8,128)(2,1)} %add_convert_fusion.14), channel_id=1, source_target_pairs={{0,16},{2,18},{4,20},{6,22},{8,24},{10,26},{12,28},{14,30},{16,0},... | collective-permute-start | bytes 1179656 | tf_op jit(solution)/shard_map/ppermute | solution.py:615
  590.9 44.8 %collective-permute-start.29 = (bf16[640,1536]{1,0:T(8,128)(2,1)}, bf16[640,1536]{1,0:T(8,128)(2,1)}, u32[]{:S(2)}, u32[]{:S(2)}) collective-permute-start(bf16[640,1536]{1,0:T(8,128)(2,1)} %get-tuple-element.237), channel_id=1, source_target_pairs={{0,1},{1,0},{2,3},{3,2},{4,5},{5,4},{6,7},{7,6},{8,9},{9,8},{10,11... | collective-permute-start | bytes 5898248 | tf_op jit(solution)/shard_map/ppermute | solution.py:648
  596.3 54.8 %collective-permute-start.33 = (bf16[512,1536]{1,0:T(8,128)(2,1)}, bf16[512,1536]{1,0:T(8,128)(2,1)}, u32[]{:S(2)}, u32[]{:S(2)}) collective-permute-start(bf16[512,1536]{1,0:T(8,128)(2,1)} %add_convert_fusion.2), channel_id=1, source_target_pairs={{0,8},{2,10},{4,12},{6,14},{8,0},{10,2},{12,4},{14,6},{16,24},{18,... | collective-permute-start | bytes 4718600 | tf_op jit(solution)/shard_map/ppermute | solution.py:615
  599.5 53.8 %collective-permute-start.32 = (bf16[384,1152]{1,0:T(8,128)(2,1)}, bf16[384,1152]{1,0:T(8,128)(2,1)}, u32[]{:S(2)}, u32[]{:S(2)}) collective-permute-start(bf16[384,1152]{1,0:T(8,128)(2,1)} %add_convert_fusion.7), channel_id=1, source_target_pairs={{0,4},{2,6},{4,0},{6,2},{8,12},{10,14},{12,8},{14,10},{16,20},{18,... | collective-permute-start | bytes 2654216 | tf_op jit(solution)/shard_map/ppermute | solution.py:615
  610.5 46.6 %collective-permute-start.31 = (bf16[384,1152]{1,0:T(8,128)(2,1)}, bf16[384,1152]{1,0:T(8,128)(2,1)}, u32[]{:S(2)}, u32[]{:S(2)}) collective-permute-start(bf16[384,1152]{1,0:T(8,128)(2,1)} %add_convert_fusion.6), channel_id=1, source_target_pairs={{0,4},{2,6},{4,0},{6,2},{8,12},{10,14},{12,8},{14,10},{16,20},{18,... | collective-permute-start | bytes 2654216 | tf_op jit(solution)/shard_map/ppermute | solution.py:615
  611.5 49.2 %collective-permute-start.35 = (bf16[192,768]{1,0:T(8,128)(2,1)}, bf16[192,768]{1,0:T(8,128)(2,1)}, u32[]{:S(2)}, u32[]{:S(2)}) collective-permute-start(bf16[192,768]{1,0:T(8,128)(2,1)} %add_convert_fusion.15), channel_id=1, source_target_pairs={{0,8},{2,10},{4,12},{6,14},{8,0},{10,2},{12,4},{14,6},{16,24},{18,... | collective-permute-start | bytes 884744 | tf_op jit(solution)/shard_map/ppermute | solution.py:615
  648.4 55.7 %collective-permute-start.36 = (bf16[384,1536]{1,0:T(8,128)(2,1)}, bf16[384,1536]{1,0:T(8,128)(2,1)S(1)}, u32[]{:S(2)}, u32[]{:S(2)}) collective-permute-start(bf16[384,1536]{1,0:T(8,128)(2,1)} %get-tuple-element.253), channel_id=1, source_target_pairs={{0,1},{1,0},{2,3},{3,2},{4,5},{5,4},{6,7},{7,6},{8,9},{9,8},{10,11... | collective-permute-start | bytes 3538952 | tf_op jit(solution)/shard_map/ppermute | solution.py:648
  653.3 61.4 %collective-permute-start.44 = (bf16[256,1536]{1,0:T(8,128)(2,1)S(1)}, bf16[256,1536]{1,0:T(8,128)(2,1)}, u32[]{:S(2)}, u32[]{:S(2)}) collective-permute-start(bf16[256,1536]{1,0:T(8,128)(2,1)S(1)} %add_convert_fusion.8), channel_id=1, source_target_pairs={{0,16},{2,18},{4,20},{6,22},{8,24},{10,26},{12,28},{14,30},{16,0},... | collective-permute-start | bytes 2359304 | tf_op jit(solution)/shard_map/ppermute | solution.py:615
  659.3 39.9 %collective-permute-start.38 = (bf16[192,1152]{1,0:T(8,128)(2,1)S(1)}, bf16[192,1152]{1,0:T(8,128)(2,1)S(1)}, u32[]{:S(2)}, u32[]{:S(2)}) collective-permute-start(bf16[192,1152]{1,0:T(8,128)(2,1)S(1)} %add_convert_fusion.12), channel_id=1, source_target_pairs={{0,8},{2,10},{4,12},{6,14},{8,0},{10,2},{12,4},{14,6},{16,24},{18,... | collective-permute-start | bytes 1327112 | tf_op jit(solution)/shard_map/ppermute | solution.py:615
  665.8 62.2 %collective-permute-start.43 = (bf16[96,768]{1,0:T(8,128)(2,1)}, bf16[96,768]{1,0:T(8,128)(2,1)}, u32[]{:S(2)}, u32[]{:S(2)}) collective-permute-start(bf16[96,768]{1,0:T(8,128)(2,1)} %add_convert_fusion.18), channel_id=1, source_target_pairs={{0,16},{2,18},{4,20},{6,22},{8,24},{10,26},{12,28},{14,30},{16,0},... | collective-permute-start | bytes 442376 | tf_op jit(solution)/shard_map/ppermute | solution.py:615
  (136 other events, 1858.4 us)
Sparse Core Ops, SparseCore 0:
  14.7 117.4 all-gather.3
  133.8 99.0 all-gather.5
  235.1 61.8 all-gather.7

commit v5 on v4

--- a/solution.py
+++ b/solution.py
@@ -1188,13 +1188,13 @@
     row = row.astype(bf16).astype(f32)[None]
     hops = Hops(row, size)
     hops.start()
-    text.finish(row)
-    text.start()
-    first_qkv.finish(text.out)
+    first_qkv.finish(row)
     first_qkv.start()
     last_qkv.finish(first_qkv.out)
     last_qkv.start()
-    hops.finish(last_qkv.out)
+    text.finish(last_qkv.out)
+    text.start()
+    hops.finish(text.out)
     hops.start()
     outp.finish(hops.value)
     outp.start()
@@ -1221,11 +1221,6 @@
         "bc,tc->bt", row[:, :cols_here].astype(bf16), mod_set, preferred_element_type=f32
     )
     grad_textkey, grad_textval = gather_sum([text.drain(grad_latents)], LANES, 2, chan)
-    hops.finish(grad_textkey)
-    rows_set = hops.drain()
-    dmod_set = rows_set[:, :cols_here].astype(bf16)
-    gain_sums = jnp.sum(rows_set[:, cols_here:], axis=0)
-    grad_modul = jnp.einsum("bt,bc->tc", cond_here, dmod_set, preferred_element_type=f32)
     embed_sum = small_sum(embed_row, "tensor", groups)
     embed_own = lax.dynamic_slice_in_dim(embed_all, dp_index, 1, 0)
     sig_own = jax.nn.sigmoid(embed_own)
@@ -1235,6 +1230,12 @@
     output_t = sum(term[:rows_w].astype(f32) for term in outp.drain(grad_textkey))
     parts = [last_qkv.drain(output_t), first_qkv.drain(output_t)][::-1]
     grad_query, grad_key, grad_value = gather_sum(parts, LANES, 3, chan)
+
+    hops.finish(grad_query)
+    rows_set = hops.drain()
+    dmod_set = rows_set[:, :cols_here].astype(bf16)
+    gain_sums = jnp.sum(rows_set[:, cols_here:], axis=0)
+    grad_modul = jnp.einsum("bt,bc->tc", cond_here, dmod_set, preferred_element_type=f32)
 
     def own_part(start, width):
         return lax.dynamic_slice_in_dim(gain_sums, start + dp_index * width, width, 0)

time: 753 us -> 750 us (level)
  transfers between devices with their start and end apart: 50 -> 50, of which waited for: 20 -> 22; matrix products, arithmetic and copies ran while one was open for 18% -> 19% of each run, Pallas kernels for 46% -> 46%
where the time goes in v5:
time: 750 us; the launch traced here: 742 us
  Pallas kernels  346 us (46%)
  waiting for transfers between devices  153 us (20%)
  other arithmetic  135 us (18%)
  starting transfers between devices  52 us (7%)
  local copies, waits for them, and re-layouts  35.1 us (5%)
  between operations  16.8 us (2%)
    pallas_call x11, Pallas kernels, product(): pl.pallas_call(functools.partial(product_kernel, turned, add is not None)...  94.9 us
    all_gather x1, waiting for transfers between devices, local(): packed_set = lax.all_gather(packed, 'dp', axis=0, tiled=True)  66.3 us
    pallas_call x6, Pallas kernels, outer_grads(): pl.pallas_call(functools.partial(outer_kernel, size, bits), grid=(cols //...  63.6 us
    pallas_call x2, Pallas kernels, self_back(): pl.pallas_call(functools.partial(self_back_kernel, half, min(512, rows)),...  62 us
    convert_element_type x18, other arithmetic, finish(): self.out = total if last else total.astype(jnp.bfloat16)  49.3 us
    ppermute x24, waiting for transfers between devices, start(): self.came = lax.ppermute(self.out, 'dp', flip_perm(self.size, 1 << bit))  43.9 us
    pallas_call x2, Pallas kernels, attend_rows(): pl.pallas_call(functools.partial(attend_kernel, half, min(256, count), fr...  40 us
    pallas_call x2, Pallas kernels, feed_forward(): pl.pallas_call(feed_kernel, grid=(blocks,), in_specs=[pl.BlockSpec((count...  34.2 us
  transfers between devices with their start and end apart: 50, of which 22 were waited for; matrix products, arithmetic and copies ran while one was open for 19% of the time, Pallas kernels for 46%

profile of v5, /device:TPU:0, one launch (start us, length us, event | category | flops | bytes accessed | tf_op | source)
XLA Modules:
  0.0 742.3 jit_solution(17783688398700997837)
XLA Ops:
  65.8 66.3 %all-gather.4.cloned.1.call-done.refs_1_ = bf16[4096,2688]{1,0:T(8,128)(2,1)} async-done(((bf16[256,2688]{1,0:T(8,128)(2,1)}), bf16[4096,2688]{1,0:T(8,128)(2,1)}) %all-gather.4.cloned.1.call-update) | async-done | bytes 22020112 | tf_op jit(solution)/shard_map/all_gather | solution.py:973
  132.2 17.5 %unfold_product.1 = (bf16[1536,3072]{1,0:T(8,128)(2,1)}, f32[1024,3072]{1,0:T(8,128)}) custom-call(bf16[1024,1536]{1,0:T(8,128)(2,1)} %get-tuple-element.291.left_ref, bf16[16,256,2688]{2,1,0:T(8,128)(2,1)} %bitcast.56, bf16[16,256,2688]{2,1,0:T(8,128)(2,1)} %bitcast.57, bf16[16,256,2688]{2,1,0:T(8,128)(2,1)} %bitcast.58), custom_call_target="tpu_custom_call" | custom-call | flops 1 | bytes 1 | tf_op jit(solution)/shard_map/unfold_product/pallas_call | solution.py:880
  152.2 10.0 %product.11.refs_4_.refs_5_.text_ref = f32[256,1536]{1,0:T(8,128)} custom-call(bf16[256,4096]{1,0:T(8,128)(2,1)} %bitcast.54, bf16[4096,2688]{1,0:T(8,128)(2,1)} %all-gather.4.cloned.1.call-done.refs_1_), custom_call_target="tpu_custom_call" | custom-call | flops 1 | bytes 1 | tf_op jit(solution)/shard_map/product/pallas_call | solution.py:564
  162.2 21.8 %attend_fwd.2 = (bf16[512,768]{1,0:T(8,128)(2,1)S(1)}, bf16[1024,768]{1,0:T(8,128)(2,1)}, f32[1024,768]{1,0:T(8,128)}, f32[1024,768]{1,0:T(8,128)}, f32[1024,153...) custom-call(s32[1]{0:T(128)S(6)} %copy.150.refs_0_.len_ref, ...), custom_call_target="tpu_custom_call" | custom-call | flops 1 | bytes 1 | tf_op jit(solution)/shard_map/attend_fwd/pallas_call | solution.py:189
  191.5 18.2 %attend_fwd.3 = (bf16[512,768]{1,0:T(8,128)(2,1)S(1)}, bf16[1024,768]{1,0:T(8,128)(2,1)}, f32[1024,768]{1,0:T(8,128)}, f32[1024,768]{1,0:T(8,128)}, f32[1024,1536]{1,0:T(8,128)}) custom-call(s32[1]{0:T(128)S(6)} %copy.150.refs_0_.len_ref, ...), custom_call_target="tpu_custom_call", output_to_operand_aliasing={{1}: (8, {}), {2}: (9, {}), {3}: (10, {}), {4}: (11, {})} | custom-call | flops 1 | bytes 1 | tf_op jit(solution)/shard_map/attend_fwd/pallas_call | solution.py:189
  215.5 11.0 %collective-permute-done.9 = bf16[512,1536]{1,0:T(8,128)(2,1)} collective-permute-done((bf16[512,1536]{1,0:T(8,128)(2,1)}, bf16[512,1536]{1,0:T(8,128)(2,1)}, u32[]{:S(2)}, u32[]{:S(2)}) %collective-permute-start.9) | collective-permute-done | bytes 1572896 | tf_op jit(solution)/shard_map/ppermute | solution.py:648
  239.1 17.0 %feed_forward.2 = (bf16[1024,2048]{1,0:T(8,128)(2,1)}, bf16[1024,4096]{1,0:T(8,128)(2,1)}) custom-call(bf16[512,1536]{1,0:T(8,128)(2,1)} %multiply_convert_fusion.5.x_ref, bf16[1024,1536]{1,0:T(8,128)(2,1)} %multiply_convert_fusion.grad_ref.left_ref, bf16[1536,6144]{1,0:T(8,128)(2,1)} %all-gather.6.cloned.1.call-done.gate_ref.up_ref.down_ref.refs_1_, ...), custom_call_target="tpu_custom_call" | custom-call | flops 1 | bytes 1 | tf_op jit(solution)/shard_map/feed_forward/pallas_call | solution.py:481
  256.2 12.0 %product.14 = bf16[512,1536]{1,0:T(8,128)(2,1)} custom-call(bf16[1024,4096]{1,0:T(8,128)(2,1)} %get-tuple-element.174.refs_0_.refs_1_, bf16[1536,6144]{1,0:T(8,128)(2,1)} %all-gather.6.cloned.1.call-done.gate_ref.up_ref.down_ref.refs_1_), custom_call_target="tpu_custom_call" | custom-call | flops 1 | bytes 1 | tf_op jit(solution)/shard_map/product/pallas_call | solution.py:564
  275.9 17.1 %feed_forward.3 = (bf16[1024,2048]{1,0:T(8,128)(2,1)}, bf16[1024,4096]{1,0:T(8,128)(2,1)}) custom-call(bf16[512,1536]{1,0:T(8,128)(2,1)} %multiply_convert_fusion.4.x_ref, bf16[1024,1536]{1,0:T(8,128)(2,1)} %multiply_convert_fusion.grad_ref.left_ref, ...), custom_call_target="tpu_custom_call", output_to_operand_aliasing={{0}: (5, {}), {1}: (6, {})} | custom-call | flops 1 | bytes 1 | tf_op jit(solution)/shard_map/feed_forward/pallas_call | solution.py:481
  293.1 11.6 %product.15 = bf16[512,1536]{1,0:T(8,128)(2,1)} custom-call(bf16[1024,4096]{1,0:T(8,128)(2,1)} %get-tuple-element.180.refs_0_.right_ref, bf16[1536,6144]{1,0:T(8,128)(2,1)} %all-gather.6.cloned.1.call-done.gate_ref.up_ref.down_ref.refs_1_), custom_call_target="tpu_custom_call" | custom-call | flops 1 | bytes 1 | tf_op jit(solution)/shard_map/product/pallas_call | solution.py:564
  304.6 11.6 %outer_grads.6 = (bf16[768,2048]{1,0:T(8,128)(2,1)S(1)}, bf16[768,2048]{1,0:T(8,128)(2,1)}) custom-call(s32[1]{0:T(128)} %bitcast.13.me_ref, bf16[1024,1536]{1,0:T(8,128)(2,1)} %multiply_convert_fusion.grad_ref.left_ref, bf16[1024,2048]{1,0:T(8,128)(2,1)} %get-tuple-element.183.right_ref.refs_0_), custom_call_target="tpu_custom_call" | custom-call | flops 1 | bytes 1 | tf_op jit(solution)/shard_map/outer_grads/pallas_call | solution.py:523
  316.5 19.6 %outer_grads.7 = (bf16[768,4096]{1,0:T(8,128)(2,1)}, bf16[768,4096]{1,0:T(8,128)(2,1)}) custom-call(s32[1]{0:T(128)} %bitcast.13.me_ref, bf16[1024,1536]{1,0:T(8,128)(2,1)S(1)} %pad_maximum_fusion.left_ref, bf16[1024,4096]{1,0:T(8,128)(2,1)} %get-tuple-element.180.refs_0_.right_ref), custom_call_target="tpu_custom_call" | custom-call | flops 1 | bytes 1 | tf_op jit(solution)/shard_map/outer_grads/pallas_call | solution.py:523
  350.1 11.0 %product.16 = bf16[1024,1536]{1,0:T(8,128)(2,1)} custom-call(bf16[1024,2048]{1,0:T(8,128)(2,1)} %get-tuple-element.183.right_ref.refs_0_, bf16[1536,6144]{1,0:T(8,128)(2,1)} %all-gather.6.cloned.1.call-done.gate_ref.up_ref.down_ref.refs_1_), custom_call_target="tpu_custom_call" | custom-call | flops 1 | bytes 1 | tf_op jit(solution)/shard_map/product/pallas_call | solution.py:564
  407.5 21.2 %cross_bwd.1 = (f32[1024,768]{1,0:T(8,128)S(1)}, bf16[256,1536]{1,0:T(8,128)(2,1)S(1)}, f32[8,768]{1,0:T(8,128)S(1)}) custom-call(s32[1]{0:T(128)S(6)} %copy.150.refs_0_.len_ref, bf16[1024,768]{1,0:T(8,128)(2,1)S(1)} %copy-done, bf16[256,1536]{1,0:T(8,128)(2,1)S(1)} %copy-done.15, f32[256,1536]{1,0:T(8,128)S(1)} %copy-done.2, f32[1024,768]{1,0:T(8,128)S(1)} %copy-done.8, ...), custom_call_target="tpu_custom_call" | custom-call | flops 1 | bytes 1 | tf_op jit(solution)/shard_map/cross_bwd/pallas_call | solution.py:390
  433.0 8.4 %outer_grads.8 = (bf16[2048,1536]{1,0:T(8,128)(2,1)}, bf16[2048,1536]{1,0:T(8,128)(2,1)}) custom-call(s32[1]{0:T(128)} %bitcast.13.me_ref, bf16[256,4096]{1,0:T(8,128)(2,1)S(1)} %bitcast.55, bf16[256,1536]{1,0:T(8,128)(2,1)S(1)} %get-tuple-element.234.right_ref.refs_0_), custom_call_target="tpu_custom_call" | custom-call | flops 1 | bytes 1 | tf_op jit(solution)/shard_map/outer_grads/pallas_call | solution.py:523
  441.4 11.8 %collective-permute-done.17.refs_2_ = bf16[384,4096]{1,0:T(8,128)(2,1)} collective-permute-done((bf16[384,4096]{1,0:T(8,128)(2,1)}, bf16[384,4096]{1,0:T(8,128)(2,1)}, u32[]{:S(2)}, u32[]{:S(2)}) %collective-permute-start.17) | collective-permute-done | bytes 3145760 | tf_op jit(solution)/shard_map/ppermute | solution.py:615
  459.9 31.2 %self_bwd.2 = (bf16[1024,1152]{1,0:T(8,128)(2,1)}, f32[8,384]{1,0:T(8,128)S(1)}) custom-call(bf16[1024,768]{1,0:T(8,128)(2,1)S(1)} %copy-done, bf16[1024,1536]{1,0:T(8,128)(2,1)} %get-tuple-element.156.refs_2_.key_ref.val_ref, bf16[1024,1536]{1,0:T(8,128)(2,1)} %get-tuple-element.156.refs_2_.key_ref.val_ref, ...), custom_call_target="tpu_custom_call" | custom-call | flops 1 | bytes 1 | tf_op jit(solution)/shard_map/self_bwd/pallas_call | solution.py:428
  516.4 9.1 %outer_grads.10 = (bf16[768,1152]{1,0:T(8,128)(2,1)S(1)}, bf16[768,1152]{1,0:T(8,128)(2,1)}) custom-call(s32[1]{0:T(128)} %bitcast.13.me_ref, bf16[1024,1536]{1,0:T(8,128)(2,1)} %get-tuple-element.291.left_ref, bf16[1024,1152]{1,0:T(8,128)(2,1)} %get-tuple-element.215.right_ref.refs_0_), custom_call_target="tpu_custom_call" | custom-call | flops 1 | bytes 1 | tf_op jit(solution)/shard_map/outer_grads/pallas_call | solution.py:523
  526.9 8.7 %product.19.refs_2_ = f32[1024,1536]{1,0:T(8,128)} custom-call(bf16[1024,1152]{1,0:T(8,128)(2,1)} %get-tuple-element.215.right_ref.refs_0_, bf16[1536,3072]{1,0:T(8,128)(2,1)} %get-tuple-element.149.refs_1_), custom_call_target="tpu_custom_call" | custom-call | flops 1 | bytes 1 | tf_op jit(solution)/shard_map/product/pallas_call | solution.py:564
  537.6 30.8 %self_bwd.3 = (bf16[1024,1152]{1,0:T(8,128)(2,1)}, f32[8,384]{1,0:T(8,128)S(1)}) custom-call(bf16[1024,768]{1,0:T(8,128)(2,1)S(1)} %copy-done, bf16[1024,1536]{1,0:T(8,128)(2,1)} %get-tuple-element.156.refs_2_.key_ref.val_ref, bf16[1024,1536]{1,0:T(8,128)(2,1)} %get-tuple-element.156.refs_2_.key_ref.val_ref, ...), custom_call_target="tpu_custom_call" | custom-call | flops 1 | bytes 1 | tf_op jit(solution)/shard_map/self_bwd/pallas_call | solution.py:428
  568.5 9.4 %product.20 = (bf16[640,1536]{1,0:T(8,128)(2,1)}, bf16[384,1536]{1,0:T(8,128)(2,1)}) custom-call(bf16[1024,1152]{1,0:T(8,128)(2,1)} %get-tuple-element.225.refs_0_.right_ref, bf16[1536,3072]{1,0:T(8,128)(2,1)} %get-tuple-element.149.refs_1_, f32[1024,1536]{1,0:T(8,128)} %product.19.refs_2_), custom_call_target="tpu_custom_call" | custom-call | flops 1 | bytes 1 | tf_op jit(solution)/shard_map/product/pallas_call | solution.py:564
  579.6 9.1 %outer_grads.11 = (bf16[768,1152]{1,0:T(8,128)(2,1)S(1)}, bf16[768,1152]{1,0:T(8,128)(2,1)}) custom-call(s32[1]{0:T(128)} %bitcast.13.me_ref, bf16[1024,1536]{1,0:T(8,128)(2,1)} %get-tuple-element.291.left_ref, bf16[1024,1152]{1,0:T(8,128)(2,1)} %get-tuple-element.225.refs_0_.right_ref), custom_call_target="tpu_custom_call" | custom-call | flops 1 | bytes 1 | tf_op jit(solution)/shard_map/outer_grads/pallas_call | solution.py:523
  613.5 8.5 %product.21 = bf16[256,4096]{1,0:T(8,128)(2,1)} custom-call(bf16[256,1536]{1,0:T(8,128)(2,1)} %copy-done.13, bf16[4096,2688]{1,0:T(8,128)(2,1)} %all-gather.4.cloned.1.call-done.refs_1_), custom_call_target="tpu_custom_call" | custom-call | flops 1 | bytes 1 | tf_op jit(solution)/shard_map/product/pallas_call | solution.py:564
  672.0 7.6 %collective-permute-done.39.refs_3_ = bf16[192,1152]{1,0:T(8,128)(2,1)S(1)} collective-permute-done((bf16[192,1152]{1,0:T(8,128)(2,1)S(1)}, bf16[192,1152]{1,0:T(8,128)(2,1)S(1)}, u32[]{:S(2)}, u32[]{:S(2)}) %collective-permute-start.39) | collective-permute-done | bytes 442400 | tf_op jit(solution)/shard_map/ppermute | solution.py:615
  (478 shorter events, 325.0 us)
Async XLA Ops:
  7.2 125.0 %all-gather.4.cloned.1.call-start = ((), (), s32[]{:S(2)}) async-start(), calls=%async_computation | async-start | bytes 23396352 | tf_op jit(solution)/shard_map/all_gather | solution.py:973
  14.6 218.3 %all-gather.6.cloned.1.call-start = ((), (), s32[]{:S(2)}) async-start(), calls=%async_computation.1 | async-start | bytes 20054016 | tf_op jit(solution)/shard_map/all_gather | solution.py:997
  31.4 318.7 %all-gather.8.cloned.1.call-start = ((), (), s32[]{:S(2)}) async-start(), calls=%async_computation.2 | async-start | bytes 6684672 | tf_op jit(solution)/shard_map/all_gather | solution.py:1035
  226.5 43.1 %collective-permute-start.10 = (bf16[512,1536]{1,0:T(8,128)(2,1)}, bf16[512,1536]{1,0:T(8,128)(2,1)}, u32[]{:S(2)}, u32[]{:S(2)}) collective-permute-start(bf16[512,1536]{1,0:T(8,128)(2,1)} %product.13), channel_id=1, source_target_pairs={{0,1},{1,0},{2,3},{3,2},{4,5},{5,4},{6,7},{7,6},{8,9},{9,8},{10,11... | collective-permute-start | bytes 4718600 | tf_op jit(solution)/shard_map/ppermute | solution.py:648
  268.2 48.1 %collective-permute-start.11 = (bf16[512,1536]{1,0:T(8,128)(2,1)}, bf16[512,1536]{1,0:T(8,128)(2,1)}, u32[]{:S(2)}, u32[]{:S(2)}) collective-permute-start(bf16[512,1536]{1,0:T(8,128)(2,1)} %product.14), channel_id=1, source_target_pairs={{0,1},{1,0},{2,3},{3,2},{4,5},{5,4},{6,7},{7,6},{8,9},{9,8},{10,11... | collective-permute-start | bytes 4718600 | tf_op jit(solution)/shard_map/ppermute | solution.py:648
  336.1 41.5 %collective-permute-start.13 = (bf16[768,4096]{1,0:T(8,128)(2,1)}, bf16[768,4096]{1,0:T(8,128)(2,1)}, u32[]{:S(2)}, u32[]{:S(2)}) collective-permute-start(bf16[768,4096]{1,0:T(8,128)(2,1)} %get-tuple-element.181), channel_id=1, source_target_pairs={{0,2},{2,0},{4,6},{6,4},{8,10},{10,8},{12,14},{14,12},{16,18},{18,... | collective-permute-start | bytes 18874376 | tf_op jit(solution)/shard_map/ppermute | solution.py:615
  336.1 38.1 %collective-permute-start.14 = (bf16[768,2048]{1,0:T(8,128)(2,1)}, bf16[768,2048]{1,0:T(8,128)(2,1)}, u32[]{:S(2)}, u32[]{:S(2)}) collective-permute-start(bf16[768,2048]{1,0:T(8,128)(2,1)} %get-tuple-element.178), channel_id=1, source_target_pairs={{0,2},{2,0},{4,6},{6,4},{8,10},{10,8},{12,14},{14,12},{16,18},{18,... | collective-permute-start | bytes 9437192 | tf_op jit(solution)/shard_map/ppermute | solution.py:615
  383.6 69.6 %collective-permute-start.17 = (bf16[384,4096]{1,0:T(8,128)(2,1)}, bf16[384,4096]{1,0:T(8,128)(2,1)}, u32[]{:S(2)}, u32[]{:S(2)}) collective-permute-start(bf16[384,4096]{1,0:T(8,128)(2,1)} %add_convert_fusion.1), channel_id=1, source_target_pairs={{0,4},{2,6},{4,0},{6,2},{8,12},{10,14},{12,8},{14,10},{16,20},{18,... | collective-permute-start | bytes 9437192 | tf_op jit(solution)/shard_map/ppermute | solution.py:615
  384.8 45.7 %collective-permute-start.16 = (bf16[384,2048]{1,0:T(8,128)(2,1)}, bf16[384,2048]{1,0:T(8,128)(2,1)}, u32[]{:S(2)}, u32[]{:S(2)}) collective-permute-start(bf16[384,2048]{1,0:T(8,128)(2,1)} %add_convert_fusion.4), channel_id=1, source_target_pairs={{0,8},{2,10},{4,12},{6,14},{8,0},{10,2},{12,4},{14,6},{16,24},{18,... | collective-permute-start | bytes 4718600 | tf_op jit(solution)/shard_map/ppermute | solution.py:615
  456.4 40.7 %collective-permute-start.18 = (bf16[2048,1536]{1,0:T(8,128)(2,1)}, bf16[2048,1536]{1,0:T(8,128)(2,1)}, u32[]{:S(2)}, u32[]{:S(2)}) collective-permute-start(bf16[2048,1536]{1,0:T(8,128)(2,1)} %get-tuple-element.204), channel_id=1, source_target_pairs={{0,2},{2,0},{4,6},{6,4},{8,10},{10,8},{12,14},{14,12},{16,18},{18,... | collective-permute-start | bytes 18874376 | tf_op jit(solution)/shard_map/ppermute | solution.py:615
  456.5 37.0 %collective-permute-start.19 = (bf16[192,4096]{1,0:T(8,128)(2,1)S(1)}, bf16[192,4096]{1,0:T(8,128)(2,1)S(1)}, u32[]{:S(2)}, u32[]{:S(2)}) collective-permute-start(bf16[192,4096]{1,0:T(8,128)(2,1)S(1)} %add_convert_fusion.3), channel_id=1, source_target_pairs={{0,8},{2,10},{4,12},{6,14},{8,0},{10,2},{12,4},{14,6},{16,24},{18,... | collective-permute-start | bytes 4718600 | tf_op jit(solution)/shard_map/ppermute | solution.py:615
  459.2 109.3 %collective-permute-start.15 = (bf16[1024,1536]{1,0:T(8,128)(2,1)}, bf16[1024,1536]{1,0:T(8,128)(2,1)}, u32[]{:S(2)}, u32[]{:S(2)}) collective-permute-start(bf16[1024,1536]{1,0:T(8,128)(2,1)} %product.16), channel_id=1, source_target_pairs={{0,1},{1,0},{2,3},{3,2},{4,5},{5,4},{6,7},{7,6},{8,9},{9,8},{10,11... | collective-permute-start | bytes 9437192 | tf_op jit(solution)/shard_map/ppermute | solution.py:648
  501.6 90.6 %collective-permute-start.27 = (bf16[1024,1536]{1,0:T(8,128)(2,1)}, bf16[1024,1536]{1,0:T(8,128)(2,1)}, u32[]{:S(2)}, u32[]{:S(2)}) collective-permute-start(bf16[1024,1536]{1,0:T(8,128)(2,1)} %add_convert_fusion), channel_id=1, source_target_pairs={{0,4},{2,6},{4,0},{6,2},{8,12},{10,14},{12,8},{14,10},{16,20},{18,... | collective-permute-start | bytes 9437192 | tf_op jit(solution)/shard_map/ppermute | solution.py:615
  512.2 56.2 %collective-permute-start.23 = (bf16[96,4096]{1,0:T(8,128)(2,1)}, bf16[96,4096]{1,0:T(8,128)(2,1)}, u32[]{:S(2)}, u32[]{:S(2)}) collective-permute-start(bf16[96,4096]{1,0:T(8,128)(2,1)} %add_convert_fusion.9), channel_id=1, source_target_pairs={{0,16},{2,18},{4,20},{6,22},{8,24},{10,26},{12,28},{14,30},{16,0},... | collective-permute-start | bytes 2359304 | tf_op jit(solution)/shard_map/ppermute | solution.py:615
  514.5 53.9 %collective-permute-start.22 = (bf16[96,2048]{1,0:T(8,128)(2,1)}, bf16[96,2048]{1,0:T(8,128)(2,1)S(1)}, u32[]{:S(2)}, u32[]{:S(2)}) collective-permute-start(bf16[96,2048]{1,0:T(8,128)(2,1)} %add_convert_fusion.14), channel_id=1, source_target_pairs={{0,16},{2,18},{4,20},{6,22},{8,24},{10,26},{12,28},{14,30},{16,0},... | collective-permute-start | bytes 1179656 | tf_op jit(solution)/shard_map/ppermute | solution.py:615
  590.9 44.8 %collective-permute-start.29 = (bf16[640,1536]{1,0:T(8,128)(2,1)}, bf16[640,1536]{1,0:T(8,128)(2,1)}, u32[]{:S(2)}, u32[]{:S(2)}) collective-permute-start(bf16[640,1536]{1,0:T(8,128)(2,1)} %get-tuple-element.237), channel_id=1, source_target_pairs={{0,1},{1,0},{2,3},{3,2},{4,5},{5,4},{6,7},{7,6},{8,9},{9,8},{10,11... | collective-permute-start | bytes 5898248 | tf_op jit(solution)/shard_map/ppermute | solution.py:648
  598.6 52.5 %collective-permute-start.33 = (bf16[384,1152]{1,0:T(8,128)(2,1)}, bf16[384,1152]{1,0:T(8,128)(2,1)}, u32[]{:S(2)}, u32[]{:S(2)}) collective-permute-start(bf16[384,1152]{1,0:T(8,128)(2,1)} %add_convert_fusion.7), channel_id=1, source_target_pairs={{0,4},{2,6},{4,0},{6,2},{8,12},{10,14},{12,8},{14,10},{16,20},{18,... | collective-permute-start | bytes 2654216 | tf_op jit(solution)/shard_map/ppermute | solution.py:615
  610.5 41.9 %collective-permute-start.32 = (bf16[384,1152]{1,0:T(8,128)(2,1)}, bf16[384,1152]{1,0:T(8,128)(2,1)}, u32[]{:S(2)}, u32[]{:S(2)}) collective-permute-start(bf16[384,1152]{1,0:T(8,128)(2,1)} %add_convert_fusion.6), channel_id=1, source_target_pairs={{0,4},{2,6},{4,0},{6,2},{8,12},{10,14},{12,8},{14,10},{16,20},{18,... | collective-permute-start | bytes 2654216 | tf_op jit(solution)/shard_map/ppermute | solution.py:615
  611.5 43.3 %collective-permute-start.31 = (bf16[512,1536]{1,0:T(8,128)(2,1)}, bf16[512,1536]{1,0:T(8,128)(2,1)}, u32[]{:S(2)}, u32[]{:S(2)}) collective-permute-start(bf16[512,1536]{1,0:T(8,128)(2,1)} %add_convert_fusion.2), channel_id=1, source_target_pairs={{0,8},{2,10},{4,12},{6,14},{8,0},{10,2},{12,4},{14,6},{16,24},{18,... | collective-permute-start | bytes 4718600 | tf_op jit(solution)/shard_map/ppermute | solution.py:615
  612.9 48.2 %collective-permute-start.35 = (bf16[192,768]{1,0:T(8,128)(2,1)}, bf16[192,768]{1,0:T(8,128)(2,1)}, u32[]{:S(2)}, u32[]{:S(2)}) collective-permute-start(bf16[192,768]{1,0:T(8,128)(2,1)} %add_convert_fusion.15), channel_id=1, source_target_pairs={{0,8},{2,10},{4,12},{6,14},{8,0},{10,2},{12,4},{14,6},{16,24},{18,... | collective-permute-start | bytes 884744 | tf_op jit(solution)/shard_map/ppermute | solution.py:615
  648.4 51.1 %collective-permute-start.36 = (bf16[384,1536]{1,0:T(8,128)(2,1)}, bf16[384,1536]{1,0:T(8,128)(2,1)S(1)}, u32[]{:S(2)}, u32[]{:S(2)}) collective-permute-start(bf16[384,1536]{1,0:T(8,128)(2,1)} %get-tuple-element.253), channel_id=1, source_target_pairs={{0,1},{1,0},{2,3},{3,2},{4,5},{5,4},{6,7},{7,6},{8,9},{9,8},{10,11... | collective-permute-start | bytes 3538952 | tf_op jit(solution)/shard_map/ppermute | solution.py:648
  658.7 55.4 %collective-permute-start.44 = (bf16[256,1536]{1,0:T(8,128)(2,1)S(1)}, bf16[256,1536]{1,0:T(8,128)(2,1)}, u32[]{:S(2)}, u32[]{:S(2)}) collective-permute-start(bf16[256,1536]{1,0:T(8,128)(2,1)S(1)} %add_convert_fusion.8), channel_id=1, source_target_pairs={{0,16},{2,18},{4,20},{6,22},{8,24},{10,26},{12,28},{14,30},{16,0},... | collective-permute-start | bytes 2359304 | tf_op jit(solution)/shard_map/ppermute | solution.py:615
  666.0 52.3 %collective-permute-start.43 = (bf16[96,768]{1,0:T(8,128)(2,1)}, bf16[96,768]{1,0:T(8,128)(2,1)}, u32[]{:S(2)}, u32[]{:S(2)}) collective-permute-start(bf16[96,768]{1,0:T(8,128)(2,1)} %add_convert_fusion.18), channel_id=1, source_target_pairs={{0,16},{2,18},{4,20},{6,22},{8,24},{10,26},{12,28},{14,30},{16,0},... | collective-permute-start | bytes 442376 | tf_op jit(solution)/shard_map/ppermute | solution.py:615
  689.1 37.6 %collective-permute-start.42 = (bf16[96,1152]{1,0:T(8,128)(2,1)}, bf16[96,1152]{1,0:T(8,128)(2,1)}, u32[]{:S(2)}, u32[]{:S(2)}) collective-permute-start(bf16[96,1152]{1,0:T(8,128)(2,1)} %add_convert_fusion.17), channel_id=1, source_target_pairs={{0,16},{2,18},{4,20},{6,22},{8,24},{10,26},{12,28},{14,30},{16,0},... | collective-permute-start | bytes 663560 | tf_op jit(solution)/shard_map/ppermute | solution.py:615
  (136 other events, 1872.2 us)
Sparse Core Ops, SparseCore 0:
  14.7 117.4 all-gather.3
  133.8 99.0 all-gather.5
  235.1 61.8 all-gather.7
